TPU v7x, 128 devices: a whole 4x4x4 slice. The times are simulated.
128 devices in a mesh: dp: 4 (over z), shard: 32 (over y, x, core).
Axes of the slice: x: 4, y: 4, z: 4, core: 2. Of those that a mesh axis runs over, the one named last changes fastest.
Arguments:
- gradients: bfloat16 [4, 8, 512, 16, 512], P('dp', None, 'shard'), may hold values from -6 to 6
- owner_list: int32 [128], replicated, may hold values from 0 to 127, as said below
- row_offset: int32 [128], replicated, may hold values from 0 to 3584, as said below
- col_offset: int32 [128], replicated, may hold values from 0 to 7680, as said below
- left_factor: float32 [256, 512, 512], P(('dp', 'shard')), may hold values from -32 to 32, as said below
- right_factor: float32 [256, 512, 512], P(('dp', 'shard')), may hold values from -32 to 32, as said below
- left_root: float32 [256, 512, 512], P(('dp', 'shard')), may hold values from -2 to 2, as said below
- right_root: float32 [256, 512, 512], P(('dp', 'shard')), may hold values from -2 to 2, as said below
Outputs:
- update: bfloat16 [8, 512, 16, 512], P(None, 'shard', None, 'dp')
- new_left_factor: float32 [256, 512, 512], P(('dp', 'shard'))
- new_right_factor: float32 [256, 512, 512], P(('dp', 'shard'))
- new_left_root: float32 [256, 512, 512], P(('dp', 'shard'))
- new_right_root: float32 [256, 512, 512], P(('dp', 'shard'))
Inputs may be any that keep to these rules, and one draw needn't show every extreme that they name: `owner_list`: no owner is named by more than 2 entries, and some owner by exactly 2. `row_offset`: multiples of 512; with col_offset, every block of the 8 x 16 grid is named exactly once. `col_offset`: multiples of 512; with row_offset, every block of the grid is named exactly once. `left_factor`: each slot symmetric positive definite. `right_factor`: each slot symmetric positive definite. `left_root`: each slot symmetric. `right_root`: each slot symmetric.
All inputs are finite; a program needn't handle non-finite values.
Results may differ from a plain program's by a relative error of at most 0.012.
Values may be sent and summed in bfloat16 or wider, within the bound.
No kernel may reach another device: no remote copies, remote signals or barrier semaphores. Data moves between devices by JAX's collectives and lax.ppermute only.
A program may use at most 128 MiB of HBM per device.

v0:
```python
import functools

import jax
import jax.numpy as jnp
from jax import lax
from jax.experimental import pallas as pl
from jax.experimental.pallas import tpu as pltpu
from jax.sharding import PartitionSpec as P

decay_rate = 0.9
f32 = jnp.float32
bf16 = jnp.bfloat16
MIB = 1 << 20


def params(mib):
    return pltpu.CompilerParams(vmem_limit_bytes=mib * MIB)


def halves(x):
    high = x.astype(bf16)
    return high, (x - high.astype(f32)).astype(bf16)


def mul(a, b):
    return jnp.dot(a, b, preferred_element_type=f32)


def mul_t(a, b):
    return lax.dot_general(a, b, (((1,), (1,)), ((), ())), preferred_element_type=f32)


def t_mul(a, b):
    return lax.dot_general(a, b, (((0,), (0,)), ((), ())), preferred_element_type=f32)


def mul3(a, b):
    return mul(a[0], b[0]) + (mul(a[0], b[1]) + mul(a[1], b[0]))


def vmem(x):
    return pltpu.with_memory_space_constraint(x, pltpu.VMEM)


def hbm(x):
    return pltpu.with_memory_space_constraint(x, pltpu.HBM)


def stored(*shape, dtype=f32):
    return pltpu.HBM(shape, dtype)


whole = pl.BlockSpec(memory_space=pltpu.VMEM)
scalars = pl.BlockSpec(memory_space=pltpu.SMEM)
in_place = pl.BlockSpec(memory_space=pl.ANY)


def window_kernel(at, mine, *refs):
    outs, sem = refs[:-1], refs[-1]
    copies = []
    for k, out in enumerate(outs):
        height, rows, cols, width = out.shape
        column = pl.multiple_of(at[2 * k + 1] * width, width)
        copy = pltpu.make_async_copy(
            mine.at[pl.ds(at[2 * k], height), :, :, pl.ds(column, width)],
            out,
            sem.at[k],
        )
        copy.start()
        copies.append(copy)
    for copy in copies:
        copy.wait()


def windows(mine, width, pairs, name):
    row_blocks, rows, cols, _ = mine.shape
    at = jnp.stack([jnp.asarray(v, jnp.int32) for pair in pairs for v in pair])
    return pl.pallas_call(
        window_kernel,
        out_shape=(stored(row_blocks // 2, rows, cols, width, dtype=bf16),) * len(pairs),
        in_specs=[scalars, in_place],
        out_specs=(in_place,) * len(pairs),
        scratch_shapes=[pltpu.SemaphoreType.DMA((len(pairs),))],
        compiler_params=params(2),
        name=name,
    )(at, hbm(mine))


def merge_kernel(at, mine, low_in, high_in, low_out, high_out):
    half, rows, cols, width = low_in.shape
    for k, (came, out) in enumerate(((low_in, low_out), (high_in, high_out))):
        column = pl.ds(pl.multiple_of(at[k] * width, width), width)
        for b in range(half):
            own = mine[k * half + b, :, :, column].astype(f32)
            out[b] = (own + came[b].astype(f32)).astype(bf16)


def merged(mine, at, low_in, high_in):
    return pl.pallas_call(
        merge_kernel,
        out_shape=(jax.ShapeDtypeStruct(low_in.shape, bf16),) * 2,
        in_specs=[scalars] + [whole] * 3,
        out_specs=(whole, whole),
        compiler_params=params(4),
        name="merge_far_part",
    )(at, mine, vmem(low_in), vmem(high_in))


def gather_kernel(table, me, mine, ups, downs, ups_more, downs_more, out, held):
    row_blocks, rows, cols, _ = mine.shape
    width = ups.shape[-1]
    half = row_blocks // 2
    column = pl.ds(pl.multiple_of(me[0] * width, width), width)
    out[...] = jnp.zeros_like(out)
    for b in range(row_blocks):
        near, far = (downs, ups_more) if b < half else (ups, downs_more)
        total = mine[b, :, :, column].astype(f32) + near[b % half].astype(f32)
        total = total + far[b % half].astype(f32)
        held[b] = total.reshape(rows * cols, width)
        for c in range(cols):
            piece = held[b, pl.ds(c, rows, stride=cols), :]
            out[table[b * cols + c]] = piece.astype(out.dtype)


def gather_pieces(table, me, mine, arrived, slots):
    half, rows, cols, width = arrived[0].shape
    return pl.pallas_call(
        gather_kernel,
        out_shape=jax.ShapeDtypeStruct((slots, rows, width), bf16),
        in_specs=[scalars, scalars] + [whole] * 5,
        out_specs=whole,
        scratch_shapes=[pltpu.VMEM((2 * half, rows * cols, width), f32)],
        compiler_params=params(6),
        name="sum_and_gather",
    )(table, me, mine, *[vmem(a) for a in arrived])


def place_kernel(per_step, rows, cols, table, arrived, out, held):
    step = pl.program_id(0)
    for b in range(per_step):
        for c in range(cols):
            slot = table[(step * per_step + b) * cols + c]
            held[b, pl.ds(c, rows, stride=cols), :] = arrived[slot].astype(f32)
        out[b] = held[b].reshape(rows, cols, held.shape[-1]).astype(out.dtype)


def place_pieces(table, arrived, row_blocks, cols):
    slots, rows, width = arrived.shape
    per_step = 4
    return pl.pallas_call(
        functools.partial(place_kernel, per_step, rows, cols),
        out_shape=jax.ShapeDtypeStruct((row_blocks, rows, cols, width), bf16),
        grid=(row_blocks // per_step,),
        in_specs=[scalars, whole],
        out_specs=pl.BlockSpec((per_step, rows, cols, width), lambda i: (i, 0, 0, 0)),
        scratch_shapes=[pltpu.VMEM((per_step, rows * cols, width), f32)],
        compiler_params=params(4),
        name="place_pieces",
    )(table, vmem(arrived))


def early_kernel(t, sides, count, *refs):
    ins, outs = refs[: 2 * sides], refs[2 * sides : 6 * sides]
    roots, factors, highs, lows, products, in_sem, out_sem = refs[6 * sides :]

    @pl.when(t < count[0])
    def _():
        coming, going = [], []
        for k in range(sides):
            for i, held in enumerate((roots, factors)):
                copy = pltpu.make_async_copy(
                    ins[2 * k + i].at[t], held.at[k], in_sem.at[2 * k + i]
                )
                copy.start()
                coming.append(copy)
        for k in range(sides):
            coming[2 * k].wait()
            x = halves(roots[k])
            square = halves(mul3(x, x))
            fourth = halves(mul3(square, square))
            fifth = halves(mul3(x, fourth))
            highs[k], lows[k] = fifth
            coming[2 * k + 1].wait()
            n = roots.shape[1]
            total = jnp.zeros((128, 128), f32)
            on = lax.broadcasted_iota(jnp.int32, (128, 128), 0)
            on = on == lax.broadcasted_iota(jnp.int32, (128, 128), 1)
            for d in range(0, n, 128):
                total += factors[k, d : d + 128, d : d + 128]
            outs[4 * k + 3][0] = jnp.sum(jnp.where(on, total, 0.0))
            products[k] = decay_rate * mul3(fifth, halves(factors[k]))
            for i, held in enumerate((highs, lows, products)):
                copy = pltpu.make_async_copy(
                    held.at[k], outs[4 * k + i], out_sem.at[3 * k + i]
                )
                copy.start()
                going.append(copy)
        for copy in going:
            copy.wait()

    @pl.when(t >= count[0])
    def _():
        for k in range(sides):
            outs[4 * k + 3][0] = jnp.float32(0.0)


def early(t, count, *pairs):
    n = pairs[0].shape[1]
    sides = len(pairs) // 2
    made = pl.pallas_call(
        functools.partial(early_kernel, t, sides),
        out_shape=(
            stored(n, n, dtype=bf16),
            stored(n, n, dtype=bf16),
            stored(n, n),
            jax.ShapeDtypeStruct((1,), f32),
        )
        * sides,
        in_specs=[scalars] + [in_place] * len(pairs),
        out_specs=(in_place, in_place, in_place, scalars) * sides,
        scratch_shapes=[
            pltpu.VMEM((sides, n, n), f32),
            pltpu.VMEM((sides, n, n), f32),
            pltpu.VMEM((sides, n, n), bf16),
            pltpu.VMEM((sides, n, n), bf16),
            pltpu.VMEM((sides, n, n), f32),
            pltpu.SemaphoreType.DMA((2 * sides,)),
            pltpu.SemaphoreType.DMA((3 * sides,)),
        ],
        compiler_params=params(24),
        cost_estimate=pl.CostEstimate(
            flops=sides * 12 * 2 * n**3,
            bytes_accessed=sides * 16 * n * n,
            transcendentals=0,
        ),
        name="early_products",
    )(count, *[hbm(x) for x in pairs])
    return [made[4 * k : 4 * k + 4] for k in range(sides)]


def assembled(pieces, t, block):
    parts, shards, _, rows, width = pieces.shape
    for z in range(parts):
        block[:, z * width : (z + 1) * width] = pieces[z, :, t].reshape(
            shards * rows, width
        )
    return block[...]


def scale_of(trace, square, gain, n):
    return n / (decay_rate * trace + gain * square)


def update_kernel(gain, slots, count, pieces, xl, xr, *refs):
    ready, refs = refs[: 6 * slots], refs[6 * slots :]
    out, block, fives, singles, made, in_sem, out_sem = refs
    parts, shards, rows, width = made.shape[1:]
    n = xl.shape[1]

    def arrivals(t):
        fl, pl_, _, fr, pr, _ = ready[6 * t : 6 * t + 6]
        sources = (
            (fl, fives.at[t, 0]),
            (xl.at[t], singles.at[t, 0]),
            (pl_, singles.at[t, 1]),
            (fr, fives.at[t, 1]),
            (xr.at[t], singles.at[t, 2]),
            (pr, singles.at[t, 3]),
        )
        return [
            pltpu.make_async_copy(a, b, in_sem.at[t, k]) for k, (a, b) in enumerate(sources)
        ]

    def departure(t):
        return pltpu.make_async_copy(made.at[t], out.at[:, :, t], out_sem.at[t])

    for t in range(slots):

        @pl.when(t < count[0])
        def _():
            for copy in arrivals(t):
                copy.start()

    for t in range(slots):

        @pl.when(t < count[0])
        def _():
            copies = arrivals(t)
            g = assembled(pieces, t, block)
            wide = g.astype(f32)
            square = jnp.sum(wide * wide)
            left_scale = scale_of(ready[6 * t + 2][0], square, gain, n)
            right_scale = scale_of(ready[6 * t + 5][0], square, gain, n)
            copies[0].wait()
            m = mul_t(mul(fives[t, 0], g).astype(bf16), g)
            copies[1].wait()
            copies[2].wait()
            left = 1.25 * singles[t, 0] - (0.25 * left_scale) * (singles[t, 1] + gain * m)
            part = mul(left.astype(bf16), g).astype(bf16)
            copies[3].wait()
            m = mul(mul_t(fives[t, 1], g).astype(bf16), g)
            copies[4].wait()
            copies[5].wait()
            right = 1.25 * singles[t, 2] - (0.25 * right_scale) * (singles[t, 3] + gain * m)
            done = mul(part, right.astype(bf16)).astype(bf16)
            for z in range(parts):
                made[t, z] = done[:, z * width : (z + 1) * width].reshape(
                    shards, rows, width
                )

        @pl.when(t >= count[0])
        def _():
            made[t] = jnp.zeros_like(made[t])

        departure(t).start()
    for t in range(slots):
        departure(t).wait()


def update_pieces(gain, count, pieces, xl, xr, ready):
    parts, shards, slots, rows, width = pieces.shape
    n = xl.shape[1]
    inputs, specs = [], []
    for left, right in ready:
        for high, _, product, trace in (left, right):
            inputs += [hbm(high), hbm(product), trace]
            specs += [in_place, in_place, scalars]
    return pl.pallas_call(
        functools.partial(update_kernel, gain, slots),
        out_shape=stored(*pieces.shape, dtype=bf16),
        in_specs=[scalars, whole, in_place, in_place] + specs,
        out_specs=in_place,
        scratch_shapes=[
            pltpu.VMEM((n, n), bf16),
            pltpu.VMEM((slots, 2, n, n), bf16),
            pltpu.VMEM((slots, 4, n, n), f32),
            pltpu.VMEM((slots, parts, shards, rows, width), bf16),
            pltpu.SemaphoreType.DMA((slots, 6)),
            pltpu.SemaphoreType.DMA((slots,)),
        ],
        compiler_params=params(28),
        name="update_pieces",
    )(count, vmem(pieces), hbm(xl), hbm(xr), *inputs)


def state_kernel(gain, slots, count, pieces, left, right, xl, xr, *refs):
    ready, refs = refs[: 8 * slots], refs[8 * slots :]
    outs, refs = refs[:4], refs[4:]
    block, fives, singles, made, in_sem, out_sem = refs
    n = xl.shape[1]
    olds = (left, right, xl, xr)

    def arrivals(t):
        flh, fll, pl_, _, frh, frl, pr, _ = ready[8 * t : 8 * t + 8]
        sources = [(a, fives.at[t, k]) for k, a in enumerate((flh, fll, frh, frl))]
        sources += [(a.at[t], singles.at[t, k]) for k, a in enumerate(olds)]
        sources += [(a, singles.at[t, 4 + k]) for k, a in enumerate((pl_, pr))]
        return [
            pltpu.make_async_copy(a, b, in_sem.at[t, k]) for k, (a, b) in enumerate(sources)
        ]

    def departures(t):
        return [
            pltpu.make_async_copy(made.at[t, k], out.at[t], out_sem.at[t, k])
            for k, out in enumerate(outs)
        ]

    def carried(t):
        return [
            pltpu.make_async_copy(old.at[t], out.at[t], out_sem.at[t, k])
            for k, (old, out) in enumerate(zip(olds, outs))
        ]

    for t in range(slots):

        @pl.when(t < count[0])
        def _():
            for copy in arrivals(t):
                copy.start()

        @pl.when(t >= count[0])
        def _():
            for copy in carried(t):
                copy.start()

    for t in range(slots):

        @pl.when(t < count[0])
        def _():
            copies, leaving = arrivals(t), departures(t)
            g = assembled(pieces, t, block)
            wide = g.astype(f32)
            square = jnp.sum(wide * wide)
            left_scale = scale_of(ready[8 * t + 3][0], square, gain, n)
            right_scale = scale_of(ready[8 * t + 7][0], square, gain, n)
            for copy in copies:
                copy.wait()
            made[t, 0] = decay_rate * singles[t, 0] + gain * mul_t(g, g)
            leaving[0].start()
            made[t, 1] = decay_rate * singles[t, 1] + gain * t_mul(g, g)
            leaving[1].start()
            high, low = halves(mul(fives[t, 0], g) + mul(fives[t, 1], g))
            m = mul_t(high, g) + mul_t(low, g)
            made[t, 2] = 1.25 * singles[t, 2] - (0.25 * left_scale) * (singles[t, 4] + gain * m)
            leaving[2].start()
            high, low = halves(mul_t(fives[t, 2], g) + mul_t(fives[t, 3], g))
            m = mul(high, g) + mul(low, g)
            made[t, 3] = 1.25 * singles[t, 3] - (0.25 * right_scale) * (singles[t, 5] + gain * m)
            leaving[3].start()

    for t in range(slots):

        @pl.when(t < count[0])
        def _():
            for copy in departures(t):
                copy.wait()

        @pl.when(t >= count[0])
        def _():
            for copy in carried(t):
                copy.wait()


def new_state(gain, count, pieces, left, right, xl, xr, ready):
    slots, n, _ = left.shape
    inputs, specs = [], []
    for sides in ready:
        for high, low, product, trace in sides:
            inputs += [hbm(high), hbm(low), hbm(product), trace]
            specs += [in_place, in_place, in_place, scalars]
    return pl.pallas_call(
        functools.partial(state_kernel, gain, slots),
        out_shape=(stored(slots, n, n),) * 4,
        in_specs=[scalars, whole] + [in_place] * 4 + specs,
        out_specs=(in_place,) * 4,
        scratch_shapes=[
            pltpu.VMEM((n, n), bf16),
            pltpu.VMEM((slots, 4, n, n), bf16),
            pltpu.VMEM((slots, 6, n, n), f32),
            pltpu.VMEM((slots, 4, n, n), f32),
            pltpu.SemaphoreType.DMA((slots, 10)),
            pltpu.SemaphoreType.DMA((slots, 4)),
        ],
        compiler_params=params(40),
        cost_estimate=pl.CostEstimate(
            flops=slots * 10 * 2 * n**3,
            bytes_accessed=slots * 48 * n * n,
            transcendentals=0,
        ),
        name="new_state",
    )(count, vmem(pieces), *[hbm(x) for x in (left, right, xl, xr)], *inputs)


def body(
    gradients, owner_list, row_offset, col_offset, left_factor, right_factor, left_root, right_root
):
    replicas = lax.axis_size("dp")
    shards = lax.axis_size("shard")
    slots, n, _ = left_factor.shape
    _, row_blocks, rows, cols, _ = gradients.shape
    width = n // replicas
    gain = (1.0 - decay_rate) / n
    me = lax.axis_index("dp")
    mine = gradients[0]

    def hop(x, step):
        return lax.ppermute(x, "dp", [(i, (i + step) % replicas) for i in range(replicas)])

    def column(step):
        return lax.rem(me + step, replicas).astype(jnp.int32)

    half = row_blocks // 2
    far_low, far_high = windows(mine, width, ((0, column(2)), (half, column(2))), "far_parts")
    far_low, far_high = hop(far_low, 1), hop(far_high, -1)
    near_high, near_low = windows(
        mine, width, ((half, column(1)), (0, column(3))), "near_parts"
    )
    near_high, near_low = hop(near_high, 1), hop(near_low, -1)

    entries = jnp.arange(owner_list.shape[0], dtype=jnp.int32)
    same = owner_list[None, :] == owner_list[:, None]
    earlier = jnp.sum(same & (entries[None, :] < entries[:, None]), axis=1)
    slot_of = owner_list * slots + earlier.astype(jnp.int32)
    block_of = row_offset // n * cols + col_offset // n
    table = jnp.sum(
        jnp.where(block_of[None, :] == entries[:, None], slot_of[None, :], 0), axis=1
    ).astype(jnp.int32)
    owner = lax.axis_index(("dp", "shard"))
    count = jnp.sum((owner_list == owner).astype(jnp.int32)).reshape(1)

    (left_ready,) = early(0, count, left_root, left_factor)
    far_low, far_high, left_ready = lax.optimization_barrier((far_low, far_high, left_ready))
    far_low, far_high = merged(mine, jnp.stack([column(1), column(3)]), far_low, far_high)
    far_low, far_high = hop(far_low, 1), hop(far_high, -1)
    (right_ready,) = early(0, count, right_root, right_factor)
    arrived = (near_high, near_low, far_low, far_high)
    arrived, left_ready, right_ready = lax.optimization_barrier(
        (arrived, left_ready, right_ready)
    )
    ready = [(left_ready, right_ready)]

    all_slots = replicas * shards * slots
    outgoing = gather_pieces(
        table, me.reshape(1).astype(jnp.int32), mine, arrived, all_slots
    )
    incoming = lax.all_to_all(outgoing, ("dp", "shard"), split_axis=0, concat_axis=0, tiled=True)
    for t in range(1, slots):
        ready.append(early(t, count, left_root, left_factor, right_root, right_factor))
    incoming, ready = lax.optimization_barrier((incoming, ready))
    pieces = incoming.reshape(replicas, shards, slots, rows, width)
    outbound = update_pieces(gain, count, pieces, left_root, right_root, ready)
    returned = lax.all_to_all(
        outbound.reshape(all_slots, rows, width),
        ("dp", "shard"), split_axis=0, concat_axis=0, tiled=True,
    )
    new_left, new_right, new_xl, new_xr = new_state(
        gain, count, pieces, left_factor, right_factor, left_root, right_root, ready
    )
    update = place_pieces(table, returned, row_blocks, cols)
    return update, new_left, new_right, new_xl, new_xr


def solution(mesh):
    slots = P(("dp", "shard"), None, None)
    in_specs = (P("dp", None, "shard", None, None), P(), P(), P(), slots, slots, slots, slots)
    out_specs = (P(None, "shard", None, "dp"), slots, slots, slots, slots)
    return jax.shard_map(body, mesh=mesh, in_specs=in_specs, out_specs=out_specs, check_vma=False)
```

profile of v0, /device:TPU:9, one launch (start us, length us, event | category | flops | bytes accessed | tf_op | source)
XLA Modules:
  0.0 366.3 jit_solution(426249276836415175)
XLA Ops:
  0.6 0.1 pad_add_fusion
  0.7 0.0 copy-start.1
  0.7 0.0 copy-start.2
  0.7 0.0 copy-start.3
  0.7 17.5 %far_parts.1 = (bf16[4,16,16,128]{3,2,1,0:T(8,128)(2,1)}, bf16[4,16,16,128]{3,2,1,0:T(8,128)(2,1)}) custom-call(s32[4]{0:T(128)S(1)} %get-tuple-element.130.at, bf16[8,16,16,512]{3,2,1,0:T(8,128)(2,1)} %bitcast.8), custom_call_target="tpu_custom_call" | custom-call | tf_op jit(solution)/shard_map/far_parts/pallas_call | solution.py:78
  18.3 1.7 collective-permute-start.2
  20.0 2.2 collective-permute-start.3
  22.2 17.5 %near_parts.1 = (bf16[4,16,16,128]{3,2,1,0:T(8,128)(2,1)}, bf16[4,16,16,128]{3,2,1,0:T(8,128)(2,1)}) custom-call(s32[4]{0:T(128)S(1)} %get-tuple-element.129.at, bf16[8,16,16,512]{3,2,1,0:T(8,128)(2,1)} %bitcast.9), custom_call_target="tpu_custom_call" | custom-call | tf_op jit(solution)/shard_map/near_parts/pallas_call | solution.py:78
  39.7 0.1 collective-permute-start
  39.8 2.7 collective-permute-start.1
  42.5 0.1 pad_add_fusion.1.at
  42.6 0.0 copy-done.1
  42.6 0.2 convert_reduce_fusion
  42.7 0.6 fusion.1
  43.4 0.0 copy-done.2
  43.4 0.0 copy-done.3
  43.4 0.1 select_reduce_fusion.table
  43.5 0.0 copy-start
  43.5 1.3 early_products.3
  44.9 0.0 collective-permute-done.2.low_in
  44.9 0.0 collective-permute-done.3.high_in
  44.9 0.2 copy-done
  45.1 0.7 merge_far_part.1
  45.8 4.7 %collective-permute-start.4 = (bf16[4,16,16,128]{3,2,1,0:T(8,128)(2,1)S(1)}, bf16[4,16,16,128]{3,2,1,0:T(8,128)(2,1)S(1)}, u32[]{:S(2)}, u32[]{:S(2)}) collective-permute-start(bf16[4,16,16,128]{3,2,1,0:T(8,128)(2,1)S(1)} %get-tuple-element.76), channel_id=1, source_target_pairs={{0,32},{32,64},{64,96},{96,0},{1,33},{33,65},{65,97},{97,1},{2,34}... | collective-permute-start | bytes 786440 | tf_op jit(solution)/shard_map/ppermute | solution.py:467
  50.5 0.0 collective-permute-start.5
  50.5 1.2 early_products.4
  51.7 0.0 collective-permute-done.ups
  51.7 0.0 collective-permute-done.1.downs
  51.7 2.1 collective-permute-done.4.ups_more
  53.8 3.3 collective-permute-done.5.downs_more
  57.1 2.1 sum_and_gather.1
  59.3 13.4 %all-to-all-start = ((bf16[256,16,128]{2,1,0:T(8,128)(2,1)}), bf16[256,16,128]{2,1,0:T(8,128)(2,1)S(1)}, u32[]{:S(2)}, u32[]{:S(2)}) async-start(bf16[256,16,128]{2,1,0:T(8,128)(2,1)} %sum_and_gather.1), calls=%async_computation | async-start | bytes 2097152 | tf_op jit(solution)/shard_map/all_to_all | solution.py:506
  72.7 1.4 early_products.5
  74.1 15.7 %all-to-all-done = bf16[256,16,128]{2,1,0:T(8,128)(2,1)S(1)} async-done(((bf16[256,16,128]{2,1,0:T(8,128)(2,1)}), bf16[256,16,128]{2,1,0:T(8,128)(2,1)S(1)}, u32[]{:S(2)}, u32[]{:S(2)}) %all-to-all-start) | async-done | bytes 1048608 | tf_op jit(solution)/shard_map/all_to_all | solution.py:506
  89.9 4.3 %update_pieces.1 = bf16[4,32,2,16,128]{4,3,2,1,0:T(8,128)(2,1)} custom-call(s32[1]{0:T(128)} %bitcast.count, bf16[4,32,2,16,128]{4,3,2,1,0:T(8,128)(2,1)S(1)} %bitcast.12, f32[2,512,512]{2,1,0:T(8,128)} %xl.3, f32[2,512,512]{2,1,0:T(8,128)} %xr.3, bf16[512,512]{1,0:T(8,128)(2,1)} %get-tuple-element.107.refs_0_, ...), custom_call_target="tpu_custom_call" | custom-call | tf_op jit(solution)/shard_map/update_pieces/pallas_call | solution.py:328
  94.1 11.9 %all-to-all-start.1 = ((bf16[256,16,128]{2,1,0:T(8,128)(2,1)}), bf16[256,16,128]{2,1,0:T(8,128)(2,1)S(1)}, u32[]{:S(2)}, u32[]{:S(2)}) async-start(bf16[256,16,128]{2,1,0:T(8,128)(2,1)} %bitcast.14), calls=%async_computation.1 | async-start | bytes 2097152 | tf_op jit(solution)/shard_map/all_to_all | solution.py:512
  106.0 258.5 %new_state.1 = (f32[2,512,512]{2,1,0:T(8,128)}, f32[2,512,512]{2,1,0:T(8,128)}, f32[2,512,512]{2,1,0:T(8,128)}, f32[2,512,512]{2,1,0:T(8,128)}) custom-call(s32[1]{0:T(128)} %bitcast.count, bf16[4,32,2,16,128]{4,3,2,1,0:T(8,128)(2,1)S(1)} %bitcast.13, f32[2,512,512]{2,1,0:T(8,128)} %left.1, f32[2,512,512]{2,1,0:T(8,128)} %right.1, f32[2,512,512]{2,1,0:T(8,128)} %xl.3, ...), custom_call_target="tpu_custom_call" | custom-call | flops 5368709120 | bytes 25165824 | tf_op jit(solution)/shard_map/new_state/pallas_call | solution.py:431
  364.6 0.0 all-to-all-done.1.arrived
  364.6 1.7 place_pieces.1
  (1 shorter events, 0.0 us)
Async XLA Ops:
  0.7 41.9 %copy-start.1 = (s32[128]{0:T(128)S(1)}, s32[128]{0:T(128)}, u32[]{:S(2)}) copy-start(s32[128]{0:T(128)} %param.9) | copy-start | bytes 1540
  0.7 42.7 %copy-start.2 = (s32[128]{0:T(128)S(1)}, s32[128]{0:T(128)}, u32[]{:S(2)}) copy-start(s32[128]{0:T(128)} %param.11) | copy-start | bytes 1540
  0.7 42.7 %copy-start.3 = (s32[128]{0:T(128)S(1)}, s32[128]{0:T(128)}, u32[]{:S(2)}) copy-start(s32[128]{0:T(128)} %param.10) | copy-start | bytes 1540
  18.3 26.6 %collective-permute-start.2 = (bf16[4,16,16,128]{3,2,1,0:T(8,128)(2,1)}, bf16[4,16,16,128]{3,2,1,0:T(8,128)(2,1)S(1)}, u32[]{:S(2)}, u32[]{:S(2)}) collective-permute-start(bf16[4,16,16,128]{3,2,1,0:T(8,128)(2,1)} %get-tuple-element.68), channel_id=1, source_target_pairs={{0,32},{32,64},{64,96},{96,0},{1,33},{33,65},{65,97},{97,1},{2,34}... | collective-permute-start | bytes 786440 | tf_op jit(solution)/shard_map/ppermute | solution.py:467
  20.0 24.9 %collective-permute-start.3 = (bf16[4,16,16,128]{3,2,1,0:T(8,128)(2,1)}, bf16[4,16,16,128]{3,2,1,0:T(8,128)(2,1)S(1)}, u32[]{:S(2)}, u32[]{:S(2)}) collective-permute-start(bf16[4,16,16,128]{3,2,1,0:T(8,128)(2,1)} %get-tuple-element.69), channel_id=1, source_target_pairs={{0,96},{32,0},{64,32},{96,64},{1,97},{33,1},{65,33},{97,65},{2,98}... | collective-permute-start | bytes 786440 | tf_op jit(solution)/shard_map/ppermute | solution.py:467
  39.7 12.0 %collective-permute-start = (bf16[4,16,16,128]{3,2,1,0:T(8,128)(2,1)}, bf16[4,16,16,128]{3,2,1,0:T(8,128)(2,1)S(1)}, u32[]{:S(2)}, u32[]{:S(2)}) collective-permute-start(bf16[4,16,16,128]{3,2,1,0:T(8,128)(2,1)} %get-tuple-element.66), channel_id=1, source_target_pairs={{0,32},{32,64},{64,96},{96,0},{1,33},{33,65},{65,97},{97,1},{2,34}... | collective-permute-start | bytes 786440 | tf_op jit(solution)/shard_map/ppermute | solution.py:467
  39.8 11.9 %collective-permute-start.1 = (bf16[4,16,16,128]{3,2,1,0:T(8,128)(2,1)}, bf16[4,16,16,128]{3,2,1,0:T(8,128)(2,1)S(1)}, u32[]{:S(2)}, u32[]{:S(2)}) collective-permute-start(bf16[4,16,16,128]{3,2,1,0:T(8,128)(2,1)} %get-tuple-element.67), channel_id=1, source_target_pairs={{0,96},{32,0},{64,32},{96,64},{1,97},{33,1},{65,33},{97,65},{2,98}... | collective-permute-start | bytes 786440 | tf_op jit(solution)/shard_map/ppermute | solution.py:467
  43.5 1.6 copy-start
  45.8 8.0 %collective-permute-start.4 = (bf16[4,16,16,128]{3,2,1,0:T(8,128)(2,1)S(1)}, bf16[4,16,16,128]{3,2,1,0:T(8,128)(2,1)S(1)}, u32[]{:S(2)}, u32[]{:S(2)}) collective-permute-start(bf16[4,16,16,128]{3,2,1,0:T(8,128)(2,1)S(1)} %get-tuple-element.76), channel_id=1, source_target_pairs={{0,32},{32,64},{64,96},{96,0},{1,33},{33,65},{65,97},{97,1},{2,34}... | collective-permute-start | bytes 786440 | tf_op jit(solution)/shard_map/ppermute | solution.py:467
  50.5 6.6 %collective-permute-start.5 = (bf16[4,16,16,128]{3,2,1,0:T(8,128)(2,1)S(1)}, bf16[4,16,16,128]{3,2,1,0:T(8,128)(2,1)S(1)}, u32[]{:S(2)}, u32[]{:S(2)}) collective-permute-start(bf16[4,16,16,128]{3,2,1,0:T(8,128)(2,1)S(1)} %get-tuple-element.77), channel_id=1, source_target_pairs={{0,96},{32,0},{64,32},{96,64},{1,97},{33,1},{65,33},{97,65},{2,98}... | collective-permute-start | bytes 786440 | tf_op jit(solution)/shard_map/ppermute | solution.py:467
  59.3 30.6 %all-to-all-start = ((bf16[256,16,128]{2,1,0:T(8,128)(2,1)}), bf16[256,16,128]{2,1,0:T(8,128)(2,1)S(1)}, u32[]{:S(2)}, u32[]{:S(2)}) async-start(bf16[256,16,128]{2,1,0:T(8,128)(2,1)} %sum_and_gather.1), calls=%async_computation | async-start | bytes 2097152 | tf_op jit(solution)/shard_map/all_to_all | solution.py:506
  94.1 270.5 %all-to-all-start.1 = ((bf16[256,16,128]{2,1,0:T(8,128)(2,1)}), bf16[256,16,128]{2,1,0:T(8,128)(2,1)S(1)}, u32[]{:S(2)}, u32[]{:S(2)}) async-start(bf16[256,16,128]{2,1,0:T(8,128)(2,1)} %bitcast.14), calls=%async_computation.1 | async-start | bytes 2097152 | tf_op jit(solution)/shard_map/all_to_all | solution.py:512
where the time goes:
time: 367 us; the launch traced here: 366 us
  Pallas kernels  306 us (83%)
  starting transfers between devices  36.7 us (10%)
  waiting for transfers between devices  21.2 us (6%)
    pallas_call x1, Pallas kernels, new_state(): pl.pallas_call(functools.partial(state_kernel, gain, slots), out_shape=(s...  259 us
    pallas_call x2, Pallas kernels, windows(): pl.pallas_call(window_kernel, out_shape=(stored(row_blocks // 2, rows, co...  35.1 us
    all_to_all x1, waiting for transfers between devices, body(): lax.all_to_all(outgoing, ('dp', 'shard'), split_axis=0, concat_axis=0, ti...  15.7 us
    all_to_all x1, starting transfers between devices, body(): lax.all_to_all(outgoing, ('dp', 'shard'), split_axis=0, concat_axis=0, ti...  13.4 us
    all_to_all x1, starting transfers between devices, body(): lax.all_to_all(outbound.reshape(all_slots, rows, width), ('dp', 'shard'),...  11.9 us
    ppermute x6, starting transfers between devices, hop(): lax.ppermute(x, 'dp', [(i, (i + step) % replicas) for i in range(replicas)])  11.3 us
  transfers between devices with their start and end apart: 8, of which 3 were waited for; matrix products, arithmetic and copies ran while one was open for 0% of the time, Pallas kernels for 77%

commit v1 on v0

--- a/solution.py
+++ b/solution.py
@@ -55,35 +55,26 @@
 in_place = pl.BlockSpec(memory_space=pl.ANY)
 
 
-def window_kernel(at, mine, *refs):
-    outs, sem = refs[:-1], refs[-1]
-    copies = []
+def window_kernel(at, mine, *outs):
     for k, out in enumerate(outs):
-        height, rows, cols, width = out.shape
-        column = pl.multiple_of(at[2 * k + 1] * width, width)
-        copy = pltpu.make_async_copy(
-            mine.at[pl.ds(at[2 * k], height), :, :, pl.ds(column, width)],
-            out,
-            sem.at[k],
-        )
-        copy.start()
-        copies.append(copy)
-    for copy in copies:
-        copy.wait()
-
-
-def windows(mine, width, pairs, name):
+        half, width = out.shape[0], out.shape[-1]
+        column = pl.ds(pl.multiple_of(at[2 * k + 1] * width, width), width)
+        for b in range(half):
+            out[b] = mine[at[2 * k] + b, :, :, column]
+
+
+def windows(mine, width, pairs):
     row_blocks, rows, cols, _ = mine.shape
     at = jnp.stack([jnp.asarray(v, jnp.int32) for pair in pairs for v in pair])
     return pl.pallas_call(
         window_kernel,
-        out_shape=(stored(row_blocks // 2, rows, cols, width, dtype=bf16),) * len(pairs),
-        in_specs=[scalars, in_place],
-        out_specs=(in_place,) * len(pairs),
-        scratch_shapes=[pltpu.SemaphoreType.DMA((len(pairs),))],
-        compiler_params=params(2),
-        name=name,
-    )(at, hbm(mine))
+        out_shape=(jax.ShapeDtypeStruct((row_blocks // 2, rows, cols, width), bf16),)
+        * len(pairs),
+        in_specs=[scalars, whole],
+        out_specs=(whole,) * len(pairs),
+        compiler_params=params(6),
+        name="windows",
+    )(at, vmem(mine))
 
 
 def merge_kernel(at, mine, low_in, high_in, low_out, high_out):
@@ -103,7 +94,7 @@
         out_specs=(whole, whole),
         compiler_params=params(4),
         name="merge_far_part",
-    )(at, mine, vmem(low_in), vmem(high_in))
+    )(at, vmem(mine), vmem(low_in), vmem(high_in))
 
 
 def gather_kernel(table, me, mine, ups, downs, ups_more, downs_more, out, held):
@@ -132,7 +123,7 @@
         scratch_shapes=[pltpu.VMEM((2 * half, rows * cols, width), f32)],
         compiler_params=params(6),
         name="sum_and_gather",
-    )(table, me, mine, *[vmem(a) for a in arrived])
+    )(table, me, vmem(mine), *[vmem(a) for a in arrived])
 
 
 def place_kernel(per_step, rows, cols, table, arrived, out, held):
@@ -159,29 +150,47 @@
     )(table, vmem(arrived))
 
 
-def early_kernel(t, sides, count, *refs):
-    ins, outs = refs[: 2 * sides], refs[2 * sides : 6 * sides]
-    roots, factors, highs, lows, products, in_sem, out_sem = refs[6 * sides :]
-
-    @pl.when(t < count[0])
-    def _():
-        coming, going = [], []
-        for k in range(sides):
-            for i, held in enumerate((roots, factors)):
-                copy = pltpu.make_async_copy(
-                    ins[2 * k + i].at[t], held.at[k], in_sem.at[2 * k + i]
-                )
+def early_kernel(slots, count, *refs):
+    items = len(slots)
+    ins, outs = refs[: 2 * items], refs[2 * items : 6 * items]
+    roots, factors, highs, lows, products, in_sem, out_sem = refs[6 * items :]
+    n = roots.shape[1]
+
+    def arrivals(k):
+        return [
+            pltpu.make_async_copy(
+                ins[2 * k + i].at[slots[k]], held.at[k], in_sem.at[k, i]
+            )
+            for i, held in enumerate((roots, factors))
+        ]
+
+    def departures(k):
+        return [
+            pltpu.make_async_copy(held.at[k], outs[4 * k + i], out_sem.at[k, i])
+            for i, held in enumerate((highs, lows, products))
+        ]
+
+    for k in range(items):
+
+        @pl.when(slots[k] < count[0])
+        def _():
+            for copy in arrivals(k):
                 copy.start()
-                coming.append(copy)
-        for k in range(sides):
-            coming[2 * k].wait()
+
+    for k in range(items):
+
+        @pl.when(slots[k] < count[0])
+        def _():
+            coming, going = arrivals(k), departures(k)
+            coming[0].wait()
             x = halves(roots[k])
             square = halves(mul3(x, x))
             fourth = halves(mul3(square, square))
             fifth = halves(mul3(x, fourth))
             highs[k], lows[k] = fifth
-            coming[2 * k + 1].wait()
-            n = roots.shape[1]
+            going[0].start()
+            going[1].start()
+            coming[1].wait()
             total = jnp.zeros((128, 128), f32)
             on = lax.broadcasted_iota(jnp.int32, (128, 128), 0)
             on = on == lax.broadcasted_iota(jnp.int32, (128, 128), 1)
@@ -189,53 +198,52 @@
                 total += factors[k, d : d + 128, d : d + 128]
             outs[4 * k + 3][0] = jnp.sum(jnp.where(on, total, 0.0))
             products[k] = decay_rate * mul3(fifth, halves(factors[k]))
-            for i, held in enumerate((highs, lows, products)):
-                copy = pltpu.make_async_copy(
-                    held.at[k], outs[4 * k + i], out_sem.at[3 * k + i]
-                )
-                copy.start()
-                going.append(copy)
-        for copy in going:
-            copy.wait()
-
-    @pl.when(t >= count[0])
-    def _():
-        for k in range(sides):
+            going[2].start()
+
+        @pl.when(slots[k] >= count[0])
+        def _():
             outs[4 * k + 3][0] = jnp.float32(0.0)
 
-
-def early(t, count, *pairs):
-    n = pairs[0].shape[1]
-    sides = len(pairs) // 2
+    for k in range(items):
+
+        @pl.when(slots[k] < count[0])
+        def _():
+            for copy in departures(k):
+                copy.wait()
+
+
+def early(count, *items):
+    n = items[0][1].shape[1]
+    many = len(items)
     made = pl.pallas_call(
-        functools.partial(early_kernel, t, sides),
+        functools.partial(early_kernel, [t for t, _, _ in items]),
         out_shape=(
             stored(n, n, dtype=bf16),
             stored(n, n, dtype=bf16),
             stored(n, n),
             jax.ShapeDtypeStruct((1,), f32),
         )
-        * sides,
-        in_specs=[scalars] + [in_place] * len(pairs),
-        out_specs=(in_place, in_place, in_place, scalars) * sides,
+        * many,
+        in_specs=[scalars] + [in_place] * (2 * many),
+        out_specs=(in_place, in_place, in_place, scalars) * many,
         scratch_shapes=[
-            pltpu.VMEM((sides, n, n), f32),
-            pltpu.VMEM((sides, n, n), f32),
-            pltpu.VMEM((sides, n, n), bf16),
-            pltpu.VMEM((sides, n, n), bf16),
-            pltpu.VMEM((sides, n, n), f32),
-            pltpu.SemaphoreType.DMA((2 * sides,)),
-            pltpu.SemaphoreType.DMA((3 * sides,)),
+            pltpu.VMEM((many, n, n), f32),
+            pltpu.VMEM((many, n, n), f32),
+            pltpu.VMEM((many, n, n), bf16),
+            pltpu.VMEM((many, n, n), bf16),
+            pltpu.VMEM((many, n, n), f32),
+            pltpu.SemaphoreType.DMA((many, 2)),
+            pltpu.SemaphoreType.DMA((many, 3)),
         ],
-        compiler_params=params(24),
+        compiler_params=params(28),
         cost_estimate=pl.CostEstimate(
-            flops=sides * 12 * 2 * n**3,
-            bytes_accessed=sides * 16 * n * n,
+            flops=many * 12 * 2 * n**3,
+            bytes_accessed=many * 16 * n * n,
             transcendentals=0,
         ),
         name="early_products",
-    )(count, *[hbm(x) for x in pairs])
-    return [made[4 * k : 4 * k + 4] for k in range(sides)]
+    )(count, *[hbm(x) for _, *pair in items for x in pair])
+    return [made[4 * k : 4 * k + 4] for k in range(many)]
 
 
 def assembled(pieces, t, block):
@@ -253,8 +261,8 @@
 
 def update_kernel(gain, slots, count, pieces, xl, xr, *refs):
     ready, refs = refs[: 6 * slots], refs[6 * slots :]
-    out, block, fives, singles, made, in_sem, out_sem = refs
-    parts, shards, rows, width = made.shape[1:]
+    out, block, fives, singles, in_sem = refs
+    parts, shards, _, rows, width = out.shape
     n = xl.shape[1]
 
     def arrivals(t):
@@ -270,9 +278,6 @@
         return [
             pltpu.make_async_copy(a, b, in_sem.at[t, k]) for k, (a, b) in enumerate(sources)
         ]
-
-    def departure(t):
-        return pltpu.make_async_copy(made.at[t], out.at[:, :, t], out_sem.at[t])
 
     for t in range(slots):
 
@@ -304,21 +309,17 @@
             right = 1.25 * singles[t, 2] - (0.25 * right_scale) * (singles[t, 3] + gain * m)
             done = mul(part, right.astype(bf16)).astype(bf16)
             for z in range(parts):
-                made[t, z] = done[:, z * width : (z + 1) * width].reshape(
+                out[z, :, t] = done[:, z * width : (z + 1) * width].reshape(
                     shards, rows, width
                 )
 
         @pl.when(t >= count[0])
         def _():
-            made[t] = jnp.zeros_like(made[t])
-
-        departure(t).start()
-    for t in range(slots):
-        departure(t).wait()
+            out[:, :, t] = jnp.zeros_like(out[:, :, t])
 
 
 def update_pieces(gain, count, pieces, xl, xr, ready):
-    parts, shards, slots, rows, width = pieces.shape
+    slots = pieces.shape[2]
     n = xl.shape[1]
     inputs, specs = [], []
     for left, right in ready:
@@ -327,16 +328,14 @@
             specs += [in_place, in_place, scalars]
     return pl.pallas_call(
         functools.partial(update_kernel, gain, slots),
-        out_shape=stored(*pieces.shape, dtype=bf16),
+        out_shape=jax.ShapeDtypeStruct(pieces.shape, bf16),
         in_specs=[scalars, whole, in_place, in_place] + specs,
-        out_specs=in_place,
+        out_specs=whole,
         scratch_shapes=[
             pltpu.VMEM((n, n), bf16),
             pltpu.VMEM((slots, 2, n, n), bf16),
             pltpu.VMEM((slots, 4, n, n), f32),
-            pltpu.VMEM((slots, parts, shards, rows, width), bf16),
             pltpu.SemaphoreType.DMA((slots, 6)),
-            pltpu.SemaphoreType.DMA((slots,)),
         ],
         compiler_params=params(28),
         name="update_pieces",
@@ -367,8 +366,8 @@
 
     def carried(t):
         return [
-            pltpu.make_async_copy(old.at[t], out.at[t], out_sem.at[t, k])
-            for k, (old, out) in enumerate(zip(olds, outs))
+            pltpu.make_async_copy(old.at[t], made.at[t, k], in_sem.at[t, k])
+            for k, old in enumerate(olds)
         ]
 
     for t in range(slots):
@@ -408,17 +407,15 @@
             made[t, 3] = 1.25 * singles[t, 3] - (0.25 * right_scale) * (singles[t, 5] + gain * m)
             leaving[3].start()
 
+        @pl.when(t >= count[0])
+        def _():
+            for came, leaves in zip(carried(t), departures(t)):
+                came.wait()
+                leaves.start()
+
     for t in range(slots):
-
-        @pl.when(t < count[0])
-        def _():
-            for copy in departures(t):
-                copy.wait()
-
-        @pl.when(t >= count[0])
-        def _():
-            for copy in carried(t):
-                copy.wait()
+        for copy in departures(t):
+            copy.wait()
 
 
 def new_state(gain, count, pieces, left, right, xl, xr, ready):
@@ -470,11 +467,12 @@
         return lax.rem(me + step, replicas).astype(jnp.int32)
 
     half = row_blocks // 2
-    far_low, far_high = windows(mine, width, ((0, column(2)), (half, column(2))), "far_parts")
+    far_low, far_high, near_high, near_low = windows(
+        mine,
+        width,
+        ((0, column(2)), (half, column(2)), (half, column(1)), (0, column(3))),
+    )
     far_low, far_high = hop(far_low, 1), hop(far_high, -1)
-    near_high, near_low = windows(
-        mine, width, ((half, column(1)), (0, column(3))), "near_parts"
-    )
     near_high, near_low = hop(near_high, 1), hop(near_low, -1)
 
     entries = jnp.arange(owner_list.shape[0], dtype=jnp.int32)
@@ -488,25 +486,22 @@
     owner = lax.axis_index(("dp", "shard"))
     count = jnp.sum((owner_list == owner).astype(jnp.int32)).reshape(1)
 
-    (left_ready,) = early(0, count, left_root, left_factor)
-    far_low, far_high, left_ready = lax.optimization_barrier((far_low, far_high, left_ready))
     far_low, far_high = merged(mine, jnp.stack([column(1), column(3)]), far_low, far_high)
     far_low, far_high = hop(far_low, 1), hop(far_high, -1)
-    (right_ready,) = early(0, count, right_root, right_factor)
+    (first,) = early(count, (0, left_root, left_factor))
     arrived = (near_high, near_low, far_low, far_high)
-    arrived, left_ready, right_ready = lax.optimization_barrier(
-        (arrived, left_ready, right_ready)
-    )
-    ready = [(left_ready, right_ready)]
+    arrived, first = lax.optimization_barrier((arrived, first))
 
     all_slots = replicas * shards * slots
     outgoing = gather_pieces(
         table, me.reshape(1).astype(jnp.int32), mine, arrived, all_slots
     )
     incoming = lax.all_to_all(outgoing, ("dp", "shard"), split_axis=0, concat_axis=0, tiled=True)
-    for t in range(1, slots):
-        ready.append(early(t, count, left_root, left_factor, right_root, right_factor))
+    sides = ((left_root, left_factor), (right_root, right_factor))
+    rest = [(t, *side) for t in range(slots) for side in sides][1:]
+    ready = [first, *early(count, *rest)]
     incoming, ready = lax.optimization_barrier((incoming, ready))
+    ready = [ready[2 * t : 2 * t + 2] for t in range(slots)]
     pieces = incoming.reshape(replicas, shards, slots, rows, width)
     outbound = update_pieces(gain, count, pieces, left_root, right_root, ready)
     returned = lax.all_to_all(

time: 367 us -> 94.7 us (0.26)
  the two profiles are of different devices: /device:TPU:9 before, /device:TPU:1 now
where the time goes in v1:
time: 94.7 us; the launch traced here: 94.4 us
  Pallas kernels  39.9 us (42%)
  starting transfers between devices  28.4 us (30%)
  waiting for transfers between devices  22.6 us (24%)
  local copies, waits for them, and re-layouts  1.7 us (2%)
  other arithmetic  1.03 us (1%)
    pallas_call x2, Pallas kernels, early(): pl.pallas_call(functools.partial(early_kernel, [t for t, _, _ in items]),...  14.4 us
    all_to_all x1, waiting for transfers between devices, body(): lax.all_to_all(outgoing, ('dp', 'shard'), split_axis=0, concat_axis=0, ti...  12.1 us
    pallas_call x1, Pallas kernels, new_state(): pl.pallas_call(functools.partial(state_kernel, gain, slots), out_shape=(s...  11.9 us
    all_to_all x1, starting transfers between devices, body(): lax.all_to_all(outgoing, ('dp', 'shard'), split_axis=0, concat_axis=0, ti...  10.3 us
    ppermute x6, starting transfers between devices, hop(): lax.ppermute(x, 'dp', [(i, (i + step) % replicas) for i in range(replicas)])  10 us
    all_to_all x1, starting transfers between devices, body(): lax.all_to_all(outbound.reshape(all_slots, rows, width), ('dp', 'shard'),...  8.02 us
    pallas_call x1, Pallas kernels, update_pieces(): pl.pallas_call(functools.partial(update_kernel, gain, slots), out_shape=j...  7.56 us
    all_to_all x1, waiting for transfers between devices, body(): lax.all_to_all(outbound.reshape(all_slots, rows, width), ('dp', 'shard'),...  7.4 us
  transfers between devices with their start and end apart: 8, of which 4 were waited for; matrix products, arithmetic and copies ran while one was open for 1% of the time, Pallas kernels for 29%

profile of v1, /device:TPU:1, one launch (start us, length us, event | category | flops | bytes accessed | tf_op | source)
XLA Modules:
  0.0 94.4 jit_solution(12986321347804694884)
XLA Ops:
  0.6 0.0 copy-start.2
  0.6 0.0 copy-start.4
  0.7 0.0 copy-start.3
  0.7 0.1 stack.21.at
  0.8 0.0 copy-start
  0.8 1.6 %copy-done = bf16[1,8,16,16,512]{4,3,2,1,0:T(8,128)(2,1)S(1)} copy-done((bf16[1,8,16,16,512]{4,3,2,1,0:T(8,128)(2,1)S(1)}, bf16[1,8,16,16,512]{4,3,2,1,0:T(8,128)(2,1)}, u32[]{:S(2)}) %copy-start) | copy-done | bytes 2097176
  2.4 0.0 copy-start.1
  2.4 1.6 %windows.1 = (bf16[4,16,16,128]{3,2,1,0:T(8,128)(2,1)}, bf16[4,16,16,128]{3,2,1,0:T(8,128)(2,1)}, bf16[4,16,16,128]{3,2,1,0:T(8,128)(2,1)}, bf16[4,16,16,128]{3,2,1,0:T(8,128)(2,1)S(1)}) custom-call(s32[8]{0:T(128)S(1)} %stack.21.at, bf16[8,16,16,512]{3,2,1,0:T(8,128)(2,1)S(1)} %bitcast.8), custom_call_target="tpu_custom_call" | custom-call | tf_op jit(solution)/shard_map/windows/pallas_call | solution.py:69
  3.9 2.5 %collective-permute-start.2 = (bf16[4,16,16,128]{3,2,1,0:T(8,128)(2,1)}, bf16[4,16,16,128]{3,2,1,0:T(8,128)(2,1)S(1)}, u32[]{:S(2)}, u32[]{:S(2)}) collective-permute-start(bf16[4,16,16,128]{3,2,1,0:T(8,128)(2,1)} %get-tuple-element.58), channel_id=1, source_target_pairs={{0,32},{32,64},{64,96},{96,0},{1,33},{33,65},{65,97},{97,1},{2,34}... | collective-permute-start | bytes 786440 | tf_op jit(solution)/shard_map/ppermute | solution.py:464
  6.4 2.1 %collective-permute-start.3 = (bf16[4,16,16,128]{3,2,1,0:T(8,128)(2,1)}, bf16[4,16,16,128]{3,2,1,0:T(8,128)(2,1)S(1)}, u32[]{:S(2)}, u32[]{:S(2)}) collective-permute-start(bf16[4,16,16,128]{3,2,1,0:T(8,128)(2,1)} %get-tuple-element.59), channel_id=1, source_target_pairs={{0,96},{32,0},{64,32},{96,64},{1,97},{33,1},{65,33},{97,65},{2,98}... | collective-permute-start | bytes 786440 | tf_op jit(solution)/shard_map/ppermute | solution.py:464
  8.5 0.0 collective-permute-start
  8.5 2.7 %collective-permute-start.1 = (bf16[4,16,16,128]{3,2,1,0:T(8,128)(2,1)S(1)}, bf16[4,16,16,128]{3,2,1,0:T(8,128)(2,1)S(1)}, u32[]{:S(2)}, u32[]{:S(2)}) collective-permute-start(bf16[4,16,16,128]{3,2,1,0:T(8,128)(2,1)S(1)} %get-tuple-element.57), channel_id=1, source_target_pairs={{0,96},{32,0},{64,32},{96,64},{1,97},{33,1},{65,33},{97,65},{2,98}... | collective-permute-start | bytes 786440 | tf_op jit(solution)/shard_map/ppermute | solution.py:464
  11.2 0.0 copy-done.2
  11.2 0.2 convert_reduce_fusion
  11.4 0.7 fusion.1
  12.0 0.0 copy-done.4
  12.0 0.0 copy-done.3
  12.1 0.1 pad_add_fusion.at
  12.1 0.1 select_reduce_fusion.table
  12.2 2.5 %collective-permute-done.2.low_in = bf16[4,16,16,128]{3,2,1,0:T(8,128)(2,1)S(1)} collective-permute-done((bf16[4,16,16,128]{3,2,1,0:T(8,128)(2,1)}, bf16[4,16,16,128]{3,2,1,0:T(8,128)(2,1)S(1)}, u32[]{:S(2)}, u32[]{:S(2)}) %collective-permute-start.2) | collective-permute-done | bytes 262176 | tf_op jit(solution)/shard_map/ppermute | solution.py:464
  14.7 0.0 collective-permute-done.3.high_in
  14.7 0.0 copy-done.1
  14.7 0.7 merge_far_part.1
  15.4 0.4 collective-permute-start.4
  15.8 2.3 %collective-permute-start.5 = (bf16[4,16,16,128]{3,2,1,0:T(8,128)(2,1)S(1)}, bf16[4,16,16,128]{3,2,1,0:T(8,128)(2,1)S(1)}, u32[]{:S(2)}, u32[]{:S(2)}) collective-permute-start(bf16[4,16,16,128]{3,2,1,0:T(8,128)(2,1)S(1)} %get-tuple-element.61), channel_id=1, source_target_pairs={{0,96},{32,0},{64,32},{96,64},{1,97},{33,1},{65,33},{97,65},{2,98}... | collective-permute-start | bytes 786440 | tf_op jit(solution)/shard_map/ppermute | solution.py:464
  18.2 7.1 %early_products.2 = (bf16[512,512]{1,0:T(8,128)(2,1)}, bf16[512,512]{1,0:T(8,128)(2,1)}, f32[512,512]{1,0:T(8,128)}, f32[1]{0:T(128)}) custom-call(s32[1]{0:T(128)} %bitcast.count, f32[2,512,512]{2,1,0:T(8,128)} %xl.3, f32[2,512,512]{2,1,0:T(8,128)} %left.1), custom_call_target="tpu_custom_call" | custom-call | flops 3221225472 | bytes 4194304 | tf_op jit(solution)/shard_map/early_products/pallas_call | solution.py:218
  25.3 0.0 collective-permute-done.ups
  25.3 0.0 collective-permute-done.1.downs
  25.3 0.6 collective-permute-done.4.ups_more
  26.0 0.0 collective-permute-done.5.downs_more
  26.0 2.1 %sum_and_gather.1 = bf16[256,16,128]{2,1,0:T(8,128)(2,1)} custom-call(s32[128]{0:T(128)S(1)} %select_reduce_fusion.table, s32[1]{0:T(128)} %bitcast.1.me, bf16[8,16,16,512]{3,2,1,0:T(8,128)(2,1)S(1)} %bitcast.10, bf16[4,16,16,128]{3,2,1,0:T(8,128)(2,1)S(1)} %collective-permute-done.ups, bf16[4,16,16,128]{3,2,1,0:T(8,128)(2,1)S(1)} %collective-permute-done.1.downs, ...), custom_call_target="tpu_custom_call" | custom-call | tf_op jit(solution)/shard_map/sum_and_gather/pallas_call | solution.py:118
  28.1 10.3 %all-to-all-start = ((bf16[256,16,128]{2,1,0:T(8,128)(2,1)}), bf16[256,16,128]{2,1,0:T(8,128)(2,1)S(1)}, u32[]{:S(2)}, u32[]{:S(2)}) async-start(bf16[256,16,128]{2,1,0:T(8,128)(2,1)} %sum_and_gather.1), calls=%async_computation | async-start | bytes 2097152 | tf_op jit(solution)/shard_map/all_to_all | solution.py:499
  38.4 7.3 %early_products.3 = (bf16[512,512]{1,0:T(8,128)(2,1)}, bf16[512,512]{1,0:T(8,128)(2,1)}, f32[512,512]{1,0:T(8,128)}, f32[1]{0:T(128)}, bf16[512,512]{1,0:T(8,128...) custom-call(s32[1]{0:T(128)} %bitcast.count, ...), custom_call_target="tpu_custom_call" | custom-call | flops 9663676416 | bytes 12582912 | tf_op jit(solution)/shard_map/early_products/pallas_call | solution.py:218
  45.7 12.1 %all-to-all-done = bf16[256,16,128]{2,1,0:T(8,128)(2,1)S(1)} async-done(((bf16[256,16,128]{2,1,0:T(8,128)(2,1)}), bf16[256,16,128]{2,1,0:T(8,128)(2,1)S(1)}, u32[]{:S(2)}, u32[]{:S(2)}) %all-to-all-start) | async-done | bytes 1048608 | tf_op jit(solution)/shard_map/all_to_all | solution.py:499
  57.7 7.6 %update_pieces.1 = bf16[4,32,2,16,128]{4,3,2,1,0:T(8,128)(2,1)} custom-call(s32[1]{0:T(128)} %bitcast.count, bf16[4,32,2,16,128]{4,3,2,1,0:T(8,128)(2,1)S(1)} %bitcast.11, f32[2,512,512]{2,1,0:T(8,128)} %xl.3, f32[2,512,512]{2,1,0:T(8,128)} %xr.3, bf16[512,512]{1,0:T(8,128)(2,1)} %get-tuple-element.87.refs_0_, f32[512,512]{1,0:T(8,128)} %get-tuple-element.88.refs_1_.refs_2_, ...), custom_call_target="tpu_custom_call" | custom-call | tf_op jit(solution)/shard_map/update_pieces/pallas_call | solution.py:329
  65.3 8.0 %all-to-all-start.1 = ((bf16[256,16,128]{2,1,0:T(8,128)(2,1)}), bf16[256,16,128]{2,1,0:T(8,128)(2,1)S(1)}, u32[]{:S(2)}, u32[]{:S(2)}) async-start(bf16[256,16,128]{2,1,0:T(8,128)(2,1)} %bitcast.7), calls=%async_computation.1 | async-start | bytes 2097152 | tf_op jit(solution)/shard_map/all_to_all | solution.py:507
  73.3 11.9 %new_state.1 = (f32[2,512,512]{2,1,0:T(8,128)}, f32[2,512,512]{2,1,0:T(8,128)}, f32[2,512,512]{2,1,0:T(8,128)}, f32[2,512,512]{2,1,0:T(8,128)}) custom-call(s32[1]{0:T(128)} %bitcast.count, bf16[4,32,2,16,128]{4,3,2,1,0:T(8,128)(2,1)S(1)} %bitcast.12, f32[2,512,512]{2,1,0:T(8,128)} %left.1, f32[2,512,512]{2,1,0:T(8,128)} %right.1, f32[2,512,512]{2,1,0:T(8,128)} %xl.3, ...), custom_call_target="tpu_custom_call" | custom-call | flops 5368709120 | bytes 25165824 | tf_op jit(solution)/shard_map/new_state/pallas_call | solution.py:428
  85.3 7.4 %all-to-all-done.1.arrived = bf16[256,16,128]{2,1,0:T(8,128)(2,1)S(1)} async-done(((bf16[256,16,128]{2,1,0:T(8,128)(2,1)}), bf16[256,16,128]{2,1,0:T(8,128)(2,1)S(1)}, u32[]{:S(2)}, u32[]{:S(2)}) %all-to-all-start.1) | async-done | bytes 1048608 | tf_op jit(solution)/shard_map/all_to_all | solution.py:507
  92.7 1.7 %place_pieces.1 = bf16[8,16,16,128]{3,2,1,0:T(8,128)(2,1)} custom-call(s32[128]{0:T(128)S(1)} %select_reduce_fusion.table, bf16[256,16,128]{2,1,0:T(8,128)(2,1)S(1)} %all-to-all-done.1.arrived), custom_call_target="tpu_custom_call" | custom-call | tf_op jit(solution)/shard_map/place_pieces/pallas_call | solution.py:141
  (1 shorter events, 0.0 us)
Async XLA Ops:
  0.6 10.6 %copy-start.2 = (s32[128]{0:T(128)S(1)}, s32[128]{0:T(128)}, u32[]{:S(2)}) copy-start(s32[128]{0:T(128)} %param.9) | copy-start | bytes 1540
  0.6 11.4 %copy-start.4 = (s32[128]{0:T(128)S(1)}, s32[128]{0:T(128)}, u32[]{:S(2)}) copy-start(s32[128]{0:T(128)} %param.10) | copy-start | bytes 1540
  0.7 11.4 %copy-start.3 = (s32[128]{0:T(128)S(1)}, s32[128]{0:T(128)}, u32[]{:S(2)}) copy-start(s32[128]{0:T(128)} %param.11) | copy-start | bytes 1540
  0.8 1.6 %copy-start = (bf16[1,8,16,16,512]{4,3,2,1,0:T(8,128)(2,1)S(1)}, bf16[1,8,16,16,512]{4,3,2,1,0:T(8,128)(2,1)}, u32[]{:S(2)}) copy-start(bf16[1,8,16,16,512]{4,3,2,1,0:T(8,128)(2,1)} %param.8) | copy-start | bytes 6291460
  2.4 12.4 %copy-start.1 = (bf16[1,8,16,16,512]{4,3,2,1,0:T(8,128)(2,1)S(1)}, bf16[1,8,16,16,512]{4,3,2,1,0:T(8,128)(2,1)}, u32[]{:S(2)}) copy-start(bf16[1,8,16,16,512]{4,3,2,1,0:T(8,128)(2,1)} %param.8) | copy-start | bytes 6291460
  3.9 10.8 %collective-permute-start.2 = (bf16[4,16,16,128]{3,2,1,0:T(8,128)(2,1)}, bf16[4,16,16,128]{3,2,1,0:T(8,128)(2,1)S(1)}, u32[]{:S(2)}, u32[]{:S(2)}) collective-permute-start(bf16[4,16,16,128]{3,2,1,0:T(8,128)(2,1)} %get-tuple-element.58), channel_id=1, source_target_pairs={{0,32},{32,64},{64,96},{96,0},{1,33},{33,65},{65,97},{97,1},{2,34}... | collective-permute-start | bytes 786440 | tf_op jit(solution)/shard_map/ppermute | solution.py:464
  6.4 8.4 %collective-permute-start.3 = (bf16[4,16,16,128]{3,2,1,0:T(8,128)(2,1)}, bf16[4,16,16,128]{3,2,1,0:T(8,128)(2,1)S(1)}, u32[]{:S(2)}, u32[]{:S(2)}) collective-permute-start(bf16[4,16,16,128]{3,2,1,0:T(8,128)(2,1)} %get-tuple-element.59), channel_id=1, source_target_pairs={{0,96},{32,0},{64,32},{96,64},{1,97},{33,1},{65,33},{97,65},{2,98}... | collective-permute-start | bytes 786440 | tf_op jit(solution)/shard_map/ppermute | solution.py:464
  8.5 16.8 %collective-permute-start = (bf16[4,16,16,128]{3,2,1,0:T(8,128)(2,1)}, bf16[4,16,16,128]{3,2,1,0:T(8,128)(2,1)S(1)}, u32[]{:S(2)}, u32[]{:S(2)}) collective-permute-start(bf16[4,16,16,128]{3,2,1,0:T(8,128)(2,1)} %get-tuple-element.56), channel_id=1, source_target_pairs={{0,32},{32,64},{64,96},{96,0},{1,33},{33,65},{65,97},{97,1},{2,34}... | collective-permute-start | bytes 786440 | tf_op jit(solution)/shard_map/ppermute | solution.py:464
  8.5 16.8 %collective-permute-start.1 = (bf16[4,16,16,128]{3,2,1,0:T(8,128)(2,1)S(1)}, bf16[4,16,16,128]{3,2,1,0:T(8,128)(2,1)S(1)}, u32[]{:S(2)}, u32[]{:S(2)}) collective-permute-start(bf16[4,16,16,128]{3,2,1,0:T(8,128)(2,1)S(1)} %get-tuple-element.57), channel_id=1, source_target_pairs={{0,96},{32,0},{64,32},{96,64},{1,97},{33,1},{65,33},{97,65},{2,98}... | collective-permute-start | bytes 786440 | tf_op jit(solution)/shard_map/ppermute | solution.py:464
  15.4 10.5 %collective-permute-start.4 = (bf16[4,16,16,128]{3,2,1,0:T(8,128)(2,1)S(1)}, bf16[4,16,16,128]{3,2,1,0:T(8,128)(2,1)S(1)}, u32[]{:S(2)}, u32[]{:S(2)}) collective-permute-start(bf16[4,16,16,128]{3,2,1,0:T(8,128)(2,1)S(1)} %get-tuple-element.60), channel_id=1, source_target_pairs={{0,32},{32,64},{64,96},{96,0},{1,33},{33,65},{65,97},{97,1},{2,34}... | collective-permute-start | bytes 786440 | tf_op jit(solution)/shard_map/ppermute | solution.py:464
  15.8 10.1 %collective-permute-start.5 = (bf16[4,16,16,128]{3,2,1,0:T(8,128)(2,1)S(1)}, bf16[4,16,16,128]{3,2,1,0:T(8,128)(2,1)S(1)}, u32[]{:S(2)}, u32[]{:S(2)}) collective-permute-start(bf16[4,16,16,128]{3,2,1,0:T(8,128)(2,1)S(1)} %get-tuple-element.61), channel_id=1, source_target_pairs={{0,96},{32,0},{64,32},{96,64},{1,97},{33,1},{65,33},{97,65},{2,98}... | collective-permute-start | bytes 786440 | tf_op jit(solution)/shard_map/ppermute | solution.py:464
  28.1 29.7 %all-to-all-start = ((bf16[256,16,128]{2,1,0:T(8,128)(2,1)}), bf16[256,16,128]{2,1,0:T(8,128)(2,1)S(1)}, u32[]{:S(2)}, u32[]{:S(2)}) async-start(bf16[256,16,128]{2,1,0:T(8,128)(2,1)} %sum_and_gather.1), calls=%async_computation | async-start | bytes 2097152 | tf_op jit(solution)/shard_map/all_to_all | solution.py:499
  65.3 27.4 %all-to-all-start.1 = ((bf16[256,16,128]{2,1,0:T(8,128)(2,1)}), bf16[256,16,128]{2,1,0:T(8,128)(2,1)S(1)}, u32[]{:S(2)}, u32[]{:S(2)}) async-start(bf16[256,16,128]{2,1,0:T(8,128)(2,1)} %bitcast.7), calls=%async_computation.1 | async-start | bytes 2097152 | tf_op jit(solution)/shard_map/all_to_all | solution.py:507

commit v2 on v1

--- a/solution.py
+++ b/solution.py
@@ -55,53 +55,63 @@
 in_place = pl.BlockSpec(memory_space=pl.ANY)
 
 
-def window_kernel(at, mine, *outs):
-    for k, out in enumerate(outs):
+def column_at(hop, width):
+    replicas = lax.axis_size("dp")
+    z = lax.rem(lax.axis_index("dp").astype(jnp.int32) + hop, replicas)
+    return pl.ds(pl.multiple_of(z * width, width), width)
+
+
+def window_kernel(parts, mine, *refs):
+    outs, sem = refs[:-1], refs[-1]
+    copies = []
+    for k, ((low, hop), out) in enumerate(zip(parts, outs)):
         half, width = out.shape[0], out.shape[-1]
-        column = pl.ds(pl.multiple_of(at[2 * k + 1] * width, width), width)
-        for b in range(half):
-            out[b] = mine[at[2 * k] + b, :, :, column]
-
-
-def windows(mine, width, pairs):
+        source = mine.at[low : low + half, :, :, column_at(hop, width)]
+        copies.append(pltpu.make_async_copy(source, out, sem.at[k]))
+    for copy in copies:
+        copy.start()
+    for copy in copies:
+        copy.wait()
+
+
+def windows(mine, width, parts):
     row_blocks, rows, cols, _ = mine.shape
-    at = jnp.stack([jnp.asarray(v, jnp.int32) for pair in pairs for v in pair])
     return pl.pallas_call(
-        window_kernel,
-        out_shape=(jax.ShapeDtypeStruct((row_blocks // 2, rows, cols, width), bf16),)
-        * len(pairs),
-        in_specs=[scalars, whole],
-        out_specs=(whole,) * len(pairs),
-        compiler_params=params(6),
+        functools.partial(window_kernel, parts),
+        out_shape=(pltpu.VMEM((row_blocks // 2, rows, cols, width), bf16),) * len(parts),
+        in_specs=[in_place],
+        out_specs=(whole,) * len(parts),
+        scratch_shapes=[pltpu.SemaphoreType.DMA((len(parts),))],
+        compiler_params=params(4),
         name="windows",
-    )(at, vmem(mine))
-
-
-def merge_kernel(at, mine, low_in, high_in, low_out, high_out):
-    half, rows, cols, width = low_in.shape
+    )(hbm(mine))
+
+
+def merge_kernel(hops, mine, low_in, high_in, low_out, high_out):
+    half, width = low_in.shape[0], low_in.shape[-1]
     for k, (came, out) in enumerate(((low_in, low_out), (high_in, high_out))):
-        column = pl.ds(pl.multiple_of(at[k] * width, width), width)
+        column = column_at(hops[k], width)
         for b in range(half):
             own = mine[k * half + b, :, :, column].astype(f32)
             out[b] = (own + came[b].astype(f32)).astype(bf16)
 
 
-def merged(mine, at, low_in, high_in):
+def merged(mine, hops, low_in, high_in):
     return pl.pallas_call(
-        merge_kernel,
-        out_shape=(jax.ShapeDtypeStruct(low_in.shape, bf16),) * 2,
-        in_specs=[scalars] + [whole] * 3,
+        functools.partial(merge_kernel, hops),
+        out_shape=(pltpu.VMEM(low_in.shape, bf16),) * 2,
+        in_specs=[whole] * 3,
         out_specs=(whole, whole),
         compiler_params=params(4),
         name="merge_far_part",
-    )(at, vmem(mine), vmem(low_in), vmem(high_in))
-
-
-def gather_kernel(table, me, mine, ups, downs, ups_more, downs_more, out, held):
+    )(vmem(mine), vmem(low_in), vmem(high_in))
+
+
+def gather_kernel(table, mine, ups, downs, ups_more, downs_more, out, held):
     row_blocks, rows, cols, _ = mine.shape
     width = ups.shape[-1]
     half = row_blocks // 2
-    column = pl.ds(pl.multiple_of(me[0] * width, width), width)
+    column = column_at(0, width)
     out[...] = jnp.zeros_like(out)
     for b in range(row_blocks):
         near, far = (downs, ups_more) if b < half else (ups, downs_more)
@@ -113,17 +123,17 @@
             out[table[b * cols + c]] = piece.astype(out.dtype)
 
 
-def gather_pieces(table, me, mine, arrived, slots):
+def gather_pieces(table, mine, arrived, slots):
     half, rows, cols, width = arrived[0].shape
     return pl.pallas_call(
         gather_kernel,
         out_shape=jax.ShapeDtypeStruct((slots, rows, width), bf16),
-        in_specs=[scalars, scalars] + [whole] * 5,
+        in_specs=[scalars] + [whole] * 5,
         out_specs=whole,
         scratch_shapes=[pltpu.VMEM((2 * half, rows * cols, width), f32)],
         compiler_params=params(6),
         name="sum_and_gather",
-    )(table, me, vmem(mine), *[vmem(a) for a in arrived])
+    )(table, vmem(mine), *[vmem(a) for a in arrived])
 
 
 def place_kernel(per_step, rows, cols, table, arrived, out, held):
@@ -153,7 +163,7 @@
 def early_kernel(slots, count, *refs):
     items = len(slots)
     ins, outs = refs[: 2 * items], refs[2 * items : 6 * items]
-    roots, factors, highs, lows, products, in_sem, out_sem = refs[6 * items :]
+    roots, factors, highs, lows, products, traces, in_sem, out_sem = refs[6 * items :]
     n = roots.shape[1]
 
     def arrivals(k):
@@ -167,7 +177,7 @@
     def departures(k):
         return [
             pltpu.make_async_copy(held.at[k], outs[4 * k + i], out_sem.at[k, i])
-            for i, held in enumerate((highs, lows, products))
+            for i, held in enumerate((highs, lows, products, traces))
         ]
 
     for k in range(items):
@@ -196,13 +206,10 @@
             on = on == lax.broadcasted_iota(jnp.int32, (128, 128), 1)
             for d in range(0, n, 128):
                 total += factors[k, d : d + 128, d : d + 128]
-            outs[4 * k + 3][0] = jnp.sum(jnp.where(on, total, 0.0))
+            traces[k] = jnp.full(traces.shape[1:], jnp.sum(jnp.where(on, total, 0.0)))
             products[k] = decay_rate * mul3(fifth, halves(factors[k]))
             going[2].start()
-
-        @pl.when(slots[k] >= count[0])
-        def _():
-            outs[4 * k + 3][0] = jnp.float32(0.0)
+            going[3].start()
 
     for k in range(items):
 
@@ -221,19 +228,20 @@
             stored(n, n, dtype=bf16),
             stored(n, n, dtype=bf16),
             stored(n, n),
-            jax.ShapeDtypeStruct((1,), f32),
+            stored(8, 128),
         )
         * many,
         in_specs=[scalars] + [in_place] * (2 * many),
-        out_specs=(in_place, in_place, in_place, scalars) * many,
+        out_specs=(in_place,) * (4 * many),
         scratch_shapes=[
             pltpu.VMEM((many, n, n), f32),
             pltpu.VMEM((many, n, n), f32),
             pltpu.VMEM((many, n, n), bf16),
             pltpu.VMEM((many, n, n), bf16),
             pltpu.VMEM((many, n, n), f32),
+            pltpu.VMEM((many, 8, 128), f32),
             pltpu.SemaphoreType.DMA((many, 2)),
-            pltpu.SemaphoreType.DMA((many, 3)),
+            pltpu.SemaphoreType.DMA((many, 4)),
         ],
         compiler_params=params(28),
         cost_estimate=pl.CostEstimate(
@@ -255,23 +263,27 @@
     return block[...]
 
 
-def scale_of(trace, square, gain, n):
-    return n / (decay_rate * trace + gain * square)
+def quarter_scale(trace, block, gain):
+    wide = block.astype(f32)
+    square = jnp.sum(wide * wide)
+    total = decay_rate * trace[0:1, 0:1] + gain * square
+    return (0.25 * block.shape[0]) / total
 
 
 def update_kernel(gain, slots, count, pieces, xl, xr, *refs):
     ready, refs = refs[: 6 * slots], refs[6 * slots :]
-    out, block, fives, singles, in_sem = refs
+    out, blocks, fives, singles, traces, in_sem = refs
     parts, shards, _, rows, width = out.shape
-    n = xl.shape[1]
 
     def arrivals(t):
-        fl, pl_, _, fr, pr, _ = ready[6 * t : 6 * t + 6]
+        fl, pl_, tl, fr, pr, tr = ready[6 * t : 6 * t + 6]
         sources = (
             (fl, fives.at[t, 0]),
+            (tl, traces.at[t, 0]),
             (xl.at[t], singles.at[t, 0]),
             (pl_, singles.at[t, 1]),
             (fr, fives.at[t, 1]),
+            (tr, traces.at[t, 1]),
             (xr.at[t], singles.at[t, 2]),
             (pr, singles.at[t, 3]),
         )
@@ -279,65 +291,70 @@
             pltpu.make_async_copy(a, b, in_sem.at[t, k]) for k, (a, b) in enumerate(sources)
         ]
 
-    for t in range(slots):
-
-        @pl.when(t < count[0])
-        def _():
-            for copy in arrivals(t):
+    def work(ts):
+        copies = {t: arrivals(t) for t in ts}
+        for t in ts:
+            for copy in copies[t]:
                 copy.start()
-
-    for t in range(slots):
-
-        @pl.when(t < count[0])
-        def _():
-            copies = arrivals(t)
-            g = assembled(pieces, t, block)
-            wide = g.astype(f32)
-            square = jnp.sum(wide * wide)
-            left_scale = scale_of(ready[6 * t + 2][0], square, gain, n)
-            right_scale = scale_of(ready[6 * t + 5][0], square, gain, n)
-            copies[0].wait()
-            m = mul_t(mul(fives[t, 0], g).astype(bf16), g)
-            copies[1].wait()
-            copies[2].wait()
-            left = 1.25 * singles[t, 0] - (0.25 * left_scale) * (singles[t, 1] + gain * m)
-            part = mul(left.astype(bf16), g).astype(bf16)
-            copies[3].wait()
-            m = mul(mul_t(fives[t, 1], g).astype(bf16), g)
-            copies[4].wait()
-            copies[5].wait()
-            right = 1.25 * singles[t, 2] - (0.25 * right_scale) * (singles[t, 3] + gain * m)
-            done = mul(part, right.astype(bf16)).astype(bf16)
+        g, side, part = {}, {}, {}
+        for t in ts:
+            g[t] = assembled(pieces, t, blocks.at[t])
+        for t in ts:
+            copies[t][0].wait()
+        for t in ts:
+            side[t] = mul_t(mul(fives[t, 0], g[t]).astype(bf16), g[t])
+        for t in ts:
+            for copy in copies[t][1:4]:
+                copy.wait()
+        for t in ts:
+            scale = quarter_scale(traces[t, 0], g[t], gain)
+            side[t] = 1.25 * singles[t, 0] - scale * (singles[t, 1] + gain * side[t])
+            part[t] = mul(side[t].astype(bf16), g[t]).astype(bf16)
+        for t in ts:
+            copies[t][4].wait()
+        for t in ts:
+            side[t] = mul(mul_t(fives[t, 1], g[t]).astype(bf16), g[t])
+        for t in ts:
+            for copy in copies[t][5:]:
+                copy.wait()
+        for t in ts:
+            scale = quarter_scale(traces[t, 1], g[t], gain)
+            side[t] = 1.25 * singles[t, 2] - scale * (singles[t, 3] + gain * side[t])
+            done = mul(part[t], side[t].astype(bf16)).astype(bf16)
             for z in range(parts):
                 out[z, :, t] = done[:, z * width : (z + 1) * width].reshape(
                     shards, rows, width
                 )
 
-        @pl.when(t >= count[0])
-        def _():
-            out[:, :, t] = jnp.zeros_like(out[:, :, t])
+    for live in range(slots + 1):
+
+        @pl.when(count[0] == live)
+        def _():
+            work(range(live))
+            for t in range(live, slots):
+                out[:, :, t] = jnp.zeros_like(out[:, :, t])
 
 
 def update_pieces(gain, count, pieces, xl, xr, ready):
     slots = pieces.shape[2]
     n = xl.shape[1]
-    inputs, specs = [], []
-    for left, right in ready:
-        for high, _, product, trace in (left, right):
-            inputs += [hbm(high), hbm(product), trace]
-            specs += [in_place, in_place, scalars]
+    inputs = []
+    for sides in ready:
+        for high, _, product, trace in sides:
+            inputs += [hbm(high), hbm(product), hbm(trace)]
     return pl.pallas_call(
         functools.partial(update_kernel, gain, slots),
         out_shape=jax.ShapeDtypeStruct(pieces.shape, bf16),
-        in_specs=[scalars, whole, in_place, in_place] + specs,
+        in_specs=[scalars, whole] + [in_place] * (2 + len(inputs)),
         out_specs=whole,
         scratch_shapes=[
-            pltpu.VMEM((n, n), bf16),
+            pltpu.VMEM((slots, n, n), bf16),
             pltpu.VMEM((slots, 2, n, n), bf16),
             pltpu.VMEM((slots, 4, n, n), f32),
-            pltpu.SemaphoreType.DMA((slots, 6)),
+            pltpu.VMEM((slots, 2, 8, 128), f32),
+            pltpu.SemaphoreType.DMA((slots, 8)),
         ],
-        compiler_params=params(28),
+        compiler_params=params(32),
         name="update_pieces",
     )(count, vmem(pieces), hbm(xl), hbm(xr), *inputs)
 
@@ -345,15 +362,16 @@
 def state_kernel(gain, slots, count, pieces, left, right, xl, xr, *refs):
     ready, refs = refs[: 8 * slots], refs[8 * slots :]
     outs, refs = refs[:4], refs[4:]
-    block, fives, singles, made, in_sem, out_sem = refs
+    block, fives, singles, traces, made, in_sem, out_sem = refs
     n = xl.shape[1]
     olds = (left, right, xl, xr)
 
     def arrivals(t):
-        flh, fll, pl_, _, frh, frl, pr, _ = ready[8 * t : 8 * t + 8]
+        flh, fll, pl_, tl, frh, frl, pr, tr = ready[8 * t : 8 * t + 8]
         sources = [(a, fives.at[t, k]) for k, a in enumerate((flh, fll, frh, frl))]
         sources += [(a.at[t], singles.at[t, k]) for k, a in enumerate(olds)]
         sources += [(a, singles.at[t, 4 + k]) for k, a in enumerate((pl_, pr))]
+        sources += [(a, traces.at[t, k]) for k, a in enumerate((tl, tr))]
         return [
             pltpu.make_async_copy(a, b, in_sem.at[t, k]) for k, (a, b) in enumerate(sources)
         ]
@@ -388,23 +406,21 @@
         def _():
             copies, leaving = arrivals(t), departures(t)
             g = assembled(pieces, t, block)
-            wide = g.astype(f32)
-            square = jnp.sum(wide * wide)
-            left_scale = scale_of(ready[8 * t + 3][0], square, gain, n)
-            right_scale = scale_of(ready[8 * t + 7][0], square, gain, n)
             for copy in copies:
                 copy.wait()
+            left_scale = quarter_scale(traces[t, 0], g, gain)
+            right_scale = quarter_scale(traces[t, 1], g, gain)
             made[t, 0] = decay_rate * singles[t, 0] + gain * mul_t(g, g)
             leaving[0].start()
             made[t, 1] = decay_rate * singles[t, 1] + gain * t_mul(g, g)
             leaving[1].start()
             high, low = halves(mul(fives[t, 0], g) + mul(fives[t, 1], g))
             m = mul_t(high, g) + mul_t(low, g)
-            made[t, 2] = 1.25 * singles[t, 2] - (0.25 * left_scale) * (singles[t, 4] + gain * m)
+            made[t, 2] = 1.25 * singles[t, 2] - left_scale * (singles[t, 4] + gain * m)
             leaving[2].start()
             high, low = halves(mul_t(fives[t, 2], g) + mul_t(fives[t, 3], g))
             m = mul(high, g) + mul(low, g)
-            made[t, 3] = 1.25 * singles[t, 3] - (0.25 * right_scale) * (singles[t, 5] + gain * m)
+            made[t, 3] = 1.25 * singles[t, 3] - right_scale * (singles[t, 5] + gain * m)
             leaving[3].start()
 
         @pl.when(t >= count[0])
@@ -420,22 +436,19 @@
 
 def new_state(gain, count, pieces, left, right, xl, xr, ready):
     slots, n, _ = left.shape
-    inputs, specs = [], []
-    for sides in ready:
-        for high, low, product, trace in sides:
-            inputs += [hbm(high), hbm(low), hbm(product), trace]
-            specs += [in_place, in_place, in_place, scalars]
+    inputs = [hbm(x) for sides in ready for made in sides for x in made]
     return pl.pallas_call(
         functools.partial(state_kernel, gain, slots),
         out_shape=(stored(slots, n, n),) * 4,
-        in_specs=[scalars, whole] + [in_place] * 4 + specs,
+        in_specs=[scalars, whole] + [in_place] * (4 + len(inputs)),
         out_specs=(in_place,) * 4,
         scratch_shapes=[
             pltpu.VMEM((n, n), bf16),
             pltpu.VMEM((slots, 4, n, n), bf16),
             pltpu.VMEM((slots, 6, n, n), f32),
+            pltpu.VMEM((slots, 2, 8, 128), f32),
             pltpu.VMEM((slots, 4, n, n), f32),
-            pltpu.SemaphoreType.DMA((slots, 10)),
+            pltpu.SemaphoreType.DMA((slots, 12)),
             pltpu.SemaphoreType.DMA((slots, 4)),
         ],
         compiler_params=params(40),
@@ -457,20 +470,14 @@
     _, row_blocks, rows, cols, _ = gradients.shape
     width = n // replicas
     gain = (1.0 - decay_rate) / n
-    me = lax.axis_index("dp")
     mine = gradients[0]
 
     def hop(x, step):
         return lax.ppermute(x, "dp", [(i, (i + step) % replicas) for i in range(replicas)])
 
-    def column(step):
-        return lax.rem(me + step, replicas).astype(jnp.int32)
-
     half = row_blocks // 2
     far_low, far_high, near_high, near_low = windows(
-        mine,
-        width,
-        ((0, column(2)), (half, column(2)), (half, column(1)), (0, column(3))),
+        mine, width, ((0, 2), (half, 2), (half, 1), (0, 3))
     )
     far_low, far_high = hop(far_low, 1), hop(far_high, -1)
     near_high, near_low = hop(near_high, 1), hop(near_low, -1)
@@ -486,16 +493,14 @@
     owner = lax.axis_index(("dp", "shard"))
     count = jnp.sum((owner_list == owner).astype(jnp.int32)).reshape(1)
 
-    far_low, far_high = merged(mine, jnp.stack([column(1), column(3)]), far_low, far_high)
+    far_low, far_high = merged(mine, (1, 3), far_low, far_high)
     far_low, far_high = hop(far_low, 1), hop(far_high, -1)
     (first,) = early(count, (0, left_root, left_factor))
     arrived = (near_high, near_low, far_low, far_high)
     arrived, first = lax.optimization_barrier((arrived, first))
 
     all_slots = replicas * shards * slots
-    outgoing = gather_pieces(
-        table, me.reshape(1).astype(jnp.int32), mine, arrived, all_slots
-    )
+    outgoing = gather_pieces(table, mine, arrived, all_slots)
     incoming = lax.all_to_all(outgoing, ("dp", "shard"), split_axis=0, concat_axis=0, tiled=True)
     sides = ((left_root, left_factor), (right_root, right_factor))
     rest = [(t, *side) for t in range(slots) for side in sides][1:]

time: 94.7 us -> 91.4 us (0.965)
  Pallas kernels: 39.9 us -> 48.1 us
  waiting for transfers between devices: 22.6 us -> 16.7 us
  starting transfers between devices: 28.4 us -> 24 us
  local copies, waits for them, and re-layouts: 1.7 us -> 0.02 us
    all_to_all x1, waiting for transfers between devices: 12.1 us -> 4.88 us  [body(): lax.all_to_all(outgoing, ('dp', 'shard'), split_axis=0, concat_axis=0, ti...]
    pallas_call x2, Pallas kernels: 14.4 us -> 21 us  [early(): pl.pallas_call(functools.partial(early_kernel, [t for t, _, _ in items]),...]
    all_to_all x1, starting transfers between devices: 8.02 us -> 3.59 us  [body(): lax.all_to_all(outbound.reshape(all_slots, rows, width), ('dp', 'shard'),...]
    unnamed x10 -> x8, local copies, waits for them, and re-layouts: 1.61 us -> 0.02 us
    pallas_call x1, Pallas kernels: 7.56 us -> 9.06 us  [update_pieces(): pl.pallas_call(functools.partial(update_kernel, gain, slots), out_shape=j...]
    ppermute x6, waiting for transfers between devices: 3.15 us -> 4.27 us  [hop(): lax.ppermute(x, 'dp', [(i, (i + step) % replicas) for i in range(replicas)])]
  transfers between devices with their start and end apart: 8 -> 8, of which waited for: 4 -> 4; matrix products, arithmetic and copies ran while one was open for 1% -> 1% of each run, Pallas kernels for 29% -> 36%
where the time goes in v2:
time: 91.4 us; the launch traced here: 90.5 us
  Pallas kernels  48.1 us (53%)
  starting transfers between devices  24 us (26%)
  waiting for transfers between devices  16.7 us (18%)
  other arithmetic  0.92 us (1%)
    pallas_call x2, Pallas kernels, early(): pl.pallas_call(functools.partial(early_kernel, [t for t, _, _ in items]),...  21 us
    pallas_call x1, Pallas kernels, new_state(): pl.pallas_call(functools.partial(state_kernel, gain, slots), out_shape=(s...  11.8 us
    all_to_all x1, starting transfers between devices, body(): lax.all_to_all(outgoing, ('dp', 'shard'), split_axis=0, concat_axis=0, ti...  10.2 us
    ppermute x6, starting transfers between devices, hop(): lax.ppermute(x, 'dp', [(i, (i + step) % replicas) for i in range(replicas)])  10.2 us
    pallas_call x1, Pallas kernels, update_pieces(): pl.pallas_call(functools.partial(update_kernel, gain, slots), out_shape=j...  9.06 us
    all_to_all x1, waiting for transfers between devices, body(): lax.all_to_all(outbound.reshape(all_slots, rows, width), ('dp', 'shard'),...  7.55 us
    all_to_all x1, waiting for transfers between devices, body(): lax.all_to_all(outgoing, ('dp', 'shard'), split_axis=0, concat_axis=0, ti...  4.88 us
    ppermute x6, waiting for transfers between devices, hop(): lax.ppermute(x, 'dp', [(i, (i + step) % replicas) for i in range(replicas)])  4.27 us
  transfers between devices with their start and end apart: 8, of which 4 were waited for; matrix products, arithmetic and copies ran while one was open for 1% of the time, Pallas kernels for 36%

profile of v2, /device:TPU:1, one launch (start us, length us, event | category | flops | bytes accessed | tf_op | source)
XLA Modules:
  0.0 90.5 jit_solution(10071623895622940238)
XLA Ops:
  0.6 0.0 copy-start
  0.6 0.0 copy-start.1
  0.7 0.0 copy-start.3
  0.7 0.0 copy-start.2
  0.7 2.3 %windows.1 = (bf16[4,16,16,128]{3,2,1,0:T(8,128)(2,1)}, bf16[4,16,16,128]{3,2,1,0:T(8,128)(2,1)}, bf16[4,16,16,128]{3,2,1,0:T(8,128)(2,1)}, bf16[4,16,16,128]{3,2,1,0:T(8,128)(2,1)S(1)}) custom-call(bf16[8,16,16,512]{3,2,1,0:T(8,128)(2,1)} %bitcast.4), custom_call_target="tpu_custom_call" | custom-call | tf_op jit(solution)/shard_map/windows/pallas_call | solution.py:79
  3.0 2.5 %collective-permute-start.2 = (bf16[4,16,16,128]{3,2,1,0:T(8,128)(2,1)}, bf16[4,16,16,128]{3,2,1,0:T(8,128)(2,1)S(1)}, u32[]{:S(2)}, u32[]{:S(2)}) collective-permute-start(bf16[4,16,16,128]{3,2,1,0:T(8,128)(2,1)} %get-tuple-element.58), channel_id=1, source_target_pairs={{0,32},{32,64},{64,96},{96,0},{1,33},{33,65},{65,97},{97,1},{2,34}... | collective-permute-start | bytes 786440 | tf_op jit(solution)/shard_map/ppermute | solution.py:476
  5.5 2.2 %collective-permute-start.3 = (bf16[4,16,16,128]{3,2,1,0:T(8,128)(2,1)}, bf16[4,16,16,128]{3,2,1,0:T(8,128)(2,1)S(1)}, u32[]{:S(2)}, u32[]{:S(2)}) collective-permute-start(bf16[4,16,16,128]{3,2,1,0:T(8,128)(2,1)} %get-tuple-element.59), channel_id=1, source_target_pairs={{0,96},{32,0},{64,32},{96,64},{1,97},{33,1},{65,33},{97,65},{2,98}... | collective-permute-start | bytes 786440 | tf_op jit(solution)/shard_map/ppermute | solution.py:476
  7.7 0.0 collective-permute-start
  7.7 2.7 %collective-permute-start.1 = (bf16[4,16,16,128]{3,2,1,0:T(8,128)(2,1)S(1)}, bf16[4,16,16,128]{3,2,1,0:T(8,128)(2,1)S(1)}, u32[]{:S(2)}, u32[]{:S(2)}) collective-permute-start(bf16[4,16,16,128]{3,2,1,0:T(8,128)(2,1)S(1)} %get-tuple-element.57), channel_id=1, source_target_pairs={{0,96},{32,0},{64,32},{96,64},{1,97},{33,1},{65,33},{97,65},{2,98}... | collective-permute-start | bytes 786440 | tf_op jit(solution)/shard_map/ppermute | solution.py:476
  10.4 0.0 copy-done.1
  10.4 0.2 convert_reduce_fusion
  10.6 0.6 fusion.1
  11.2 0.0 copy-done.3
  11.2 0.0 copy-done.2
  11.2 0.1 select_reduce_fusion.table
  11.3 2.5 %collective-permute-done.2.low_in = bf16[4,16,16,128]{3,2,1,0:T(8,128)(2,1)S(1)} collective-permute-done((bf16[4,16,16,128]{3,2,1,0:T(8,128)(2,1)}, bf16[4,16,16,128]{3,2,1,0:T(8,128)(2,1)S(1)}, u32[]{:S(2)}, u32[]{:S(2)}) %collective-permute-start.2) | collective-permute-done | bytes 262176 | tf_op jit(solution)/shard_map/ppermute | solution.py:476
  13.9 0.0 collective-permute-done.3.high_in
  13.9 0.0 copy-done
  13.9 0.1 merge_far_part.1
  14.0 0.4 collective-permute-start.4
  14.4 2.3 %collective-permute-start.5 = (bf16[4,16,16,128]{3,2,1,0:T(8,128)(2,1)S(1)}, bf16[4,16,16,128]{3,2,1,0:T(8,128)(2,1)S(1)}, u32[]{:S(2)}, u32[]{:S(2)}) collective-permute-start(bf16[4,16,16,128]{3,2,1,0:T(8,128)(2,1)S(1)} %get-tuple-element.61), channel_id=1, source_target_pairs={{0,96},{32,0},{64,32},{96,64},{1,97},{33,1},{65,33},{97,65},{2,98}... | collective-permute-start | bytes 786440 | tf_op jit(solution)/shard_map/ppermute | solution.py:476
  16.8 6.6 %early_products.2 = (bf16[512,512]{1,0:T(8,128)(2,1)}, bf16[512,512]{1,0:T(8,128)(2,1)}, f32[512,512]{1,0:T(8,128)}, f32[8,128]{1,0:T(8,128)}) custom-call(s32[1]{0:T(128)} %bitcast.count, f32[2,512,512]{2,1,0:T(8,128)} %xl.3, f32[2,512,512]{2,1,0:T(8,128)} %left.1), custom_call_target="tpu_custom_call" | custom-call | flops 3221225472 | bytes 4194304 | tf_op jit(solution)/shard_map/early_products/pallas_call | solution.py:225
  23.3 0.0 collective-permute-done.ups
  23.4 0.0 collective-permute-done.1.downs
  23.4 1.7 %collective-permute-done.4.ups_more = bf16[4,16,16,128]{3,2,1,0:T(8,128)(2,1)S(1)} collective-permute-done((bf16[4,16,16,128]{3,2,1,0:T(8,128)(2,1)S(1)}, bf16[4,16,16,128]{3,2,1,0:T(8,128)(2,1)S(1)}, u32[]{:S(2)}, u32[]{:S(2)}) %collective-permute-start.4) | collective-permute-done | bytes 262176 | tf_op jit(solution)/shard_map/ppermute | solution.py:476
  25.1 0.0 collective-permute-done.5.downs_more
  25.1 2.1 %sum_and_gather.1 = bf16[256,16,128]{2,1,0:T(8,128)(2,1)} custom-call(s32[128]{0:T(128)S(1)} %select_reduce_fusion.table, bf16[8,16,16,512]{3,2,1,0:T(8,128)(2,1)S(1)} %bitcast.6, bf16[4,16,16,128]{3,2,1,0:T(8,128)(2,1)S(1)} %collective-permute-done.ups, bf16[4,16,16,128]{3,2,1,0:T(8,128)(2,1)S(1)} %collective-permute-done.1.downs, ...), custom_call_target="tpu_custom_call" | custom-call | tf_op jit(solution)/shard_map/sum_and_gather/pallas_call | solution.py:128
  27.2 10.2 %all-to-all-start = ((bf16[256,16,128]{2,1,0:T(8,128)(2,1)}), bf16[256,16,128]{2,1,0:T(8,128)(2,1)S(1)}, u32[]{:S(2)}, u32[]{:S(2)}) async-start(bf16[256,16,128]{2,1,0:T(8,128)(2,1)} %sum_and_gather.1), calls=%async_computation | async-start | bytes 2097152 | tf_op jit(solution)/shard_map/all_to_all | solution.py:504
  37.4 14.5 %early_products.3 = (bf16[512,512]{1,0:T(8,128)(2,1)}, bf16[512,512]{1,0:T(8,128)(2,1)}, f32[512,512]{1,0:T(8,128)}, f32[8,128]{1,0:T(8,128)}, bf16[512,512]{1,0...) custom-call(s32[1]{0:T(128)} %bitcast.count, ...), custom_call_target="tpu_custom_call" | custom-call | flops 9663676416 | bytes 12582912 | tf_op jit(solution)/shard_map/early_products/pallas_call | solution.py:225
  51.9 4.9 %all-to-all-done = bf16[256,16,128]{2,1,0:T(8,128)(2,1)S(1)} async-done(((bf16[256,16,128]{2,1,0:T(8,128)(2,1)}), bf16[256,16,128]{2,1,0:T(8,128)(2,1)S(1)}, u32[]{:S(2)}, u32[]{:S(2)}) %all-to-all-start) | async-done | bytes 1048608 | tf_op jit(solution)/shard_map/all_to_all | solution.py:504
  56.8 9.1 %update_pieces.1 = bf16[4,32,2,16,128]{4,3,2,1,0:T(8,128)(2,1)} custom-call(s32[1]{0:T(128)} %bitcast.count, bf16[4,32,2,16,128]{4,3,2,1,0:T(8,128)(2,1)S(1)} %bitcast.7, f32[2,512,512]{2,1,0:T(8,128)} %xl.3, f32[2,512,512]{2,1,0:T(8,128)} %xr.3, bf16[512,512]{1,0:T(8,128)(2,1)} %get-tuple-element.87.refs_0_, f32[512,512]{1,0:T(8,128)} %get-tuple-element.88.refs_1_.refs_2_, ...), custom_call_target="tpu_custom_call" | custom-call | tf_op jit(solution)/shard_map/update_pieces/pallas_call | solution.py:345
  65.9 3.6 %all-to-all-start.1 = ((bf16[256,16,128]{2,1,0:T(8,128)(2,1)}), bf16[256,16,128]{2,1,0:T(8,128)(2,1)S(1)}, u32[]{:S(2)}, u32[]{:S(2)}) async-start(bf16[256,16,128]{2,1,0:T(8,128)(2,1)} %bitcast.3), calls=%async_computation.1 | async-start | bytes 2097152 | tf_op jit(solution)/shard_map/all_to_all | solution.py:512
  69.4 11.8 %new_state.1 = (f32[2,512,512]{2,1,0:T(8,128)}, f32[2,512,512]{2,1,0:T(8,128)}, f32[2,512,512]{2,1,0:T(8,128)}, f32[2,512,512]{2,1,0:T(8,128)}) custom-call(s32[1]{0:T(128)} %bitcast.count, bf16[4,32,2,16,128]{4,3,2,1,0:T(8,128)(2,1)S(1)} %bitcast.8, f32[2,512,512]{2,1,0:T(8,128)} %left.1, f32[2,512,512]{2,1,0:T(8,128)} %right.1, f32[2,512,512]{2,1,0:T(8,128)} %xl.3, ...), custom_call_target="tpu_custom_call" | custom-call | flops 5368709120 | bytes 25165824 | tf_op jit(solution)/shard_map/new_state/pallas_call | solution.py:440
  81.2 7.5 %all-to-all-done.1.arrived = bf16[256,16,128]{2,1,0:T(8,128)(2,1)S(1)} async-done(((bf16[256,16,128]{2,1,0:T(8,128)(2,1)}), bf16[256,16,128]{2,1,0:T(8,128)(2,1)S(1)}, u32[]{:S(2)}, u32[]{:S(2)}) %all-to-all-start.1) | async-done | bytes 1048608 | tf_op jit(solution)/shard_map/all_to_all | solution.py:512
  88.8 1.7 %place_pieces.1 = bf16[8,16,16,128]{3,2,1,0:T(8,128)(2,1)} custom-call(s32[128]{0:T(128)S(1)} %select_reduce_fusion.table, bf16[256,16,128]{2,1,0:T(8,128)(2,1)S(1)} %all-to-all-done.1.arrived), custom_call_target="tpu_custom_call" | custom-call | tf_op jit(solution)/shard_map/place_pieces/pallas_call | solution.py:151
  (1 shorter events, 0.0 us)
Async XLA Ops:
  0.6 13.2 %copy-start = (bf16[1,8,16,16,512]{4,3,2,1,0:T(8,128)(2,1)S(1)}, bf16[1,8,16,16,512]{4,3,2,1,0:T(8,128)(2,1)}, u32[]{:S(2)}) copy-start(bf16[1,8,16,16,512]{4,3,2,1,0:T(8,128)(2,1)} %param.8) | copy-start | bytes 6291460
  0.6 9.7 %copy-start.1 = (s32[128]{0:T(128)S(1)}, s32[128]{0:T(128)}, u32[]{:S(2)}) copy-start(s32[128]{0:T(128)} %param.9) | copy-start | bytes 1540
  0.7 10.5 %copy-start.3 = (s32[128]{0:T(128)S(1)}, s32[128]{0:T(128)}, u32[]{:S(2)}) copy-start(s32[128]{0:T(128)} %param.10) | copy-start | bytes 1540
  0.7 10.5 %copy-start.2 = (s32[128]{0:T(128)S(1)}, s32[128]{0:T(128)}, u32[]{:S(2)}) copy-start(s32[128]{0:T(128)} %param.11) | copy-start | bytes 1540
  3.0 10.9 %collective-permute-start.2 = (bf16[4,16,16,128]{3,2,1,0:T(8,128)(2,1)}, bf16[4,16,16,128]{3,2,1,0:T(8,128)(2,1)S(1)}, u32[]{:S(2)}, u32[]{:S(2)}) collective-permute-start(bf16[4,16,16,128]{3,2,1,0:T(8,128)(2,1)} %get-tuple-element.58), channel_id=1, source_target_pairs={{0,32},{32,64},{64,96},{96,0},{1,33},{33,65},{65,97},{97,1},{2,34}... | collective-permute-start | bytes 786440 | tf_op jit(solution)/shard_map/ppermute | solution.py:476
  5.5 8.4 %collective-permute-start.3 = (bf16[4,16,16,128]{3,2,1,0:T(8,128)(2,1)}, bf16[4,16,16,128]{3,2,1,0:T(8,128)(2,1)S(1)}, u32[]{:S(2)}, u32[]{:S(2)}) collective-permute-start(bf16[4,16,16,128]{3,2,1,0:T(8,128)(2,1)} %get-tuple-element.59), channel_id=1, source_target_pairs={{0,96},{32,0},{64,32},{96,64},{1,97},{33,1},{65,33},{97,65},{2,98}... | collective-permute-start | bytes 786440 | tf_op jit(solution)/shard_map/ppermute | solution.py:476
  7.7 15.7 %collective-permute-start = (bf16[4,16,16,128]{3,2,1,0:T(8,128)(2,1)}, bf16[4,16,16,128]{3,2,1,0:T(8,128)(2,1)S(1)}, u32[]{:S(2)}, u32[]{:S(2)}) collective-permute-start(bf16[4,16,16,128]{3,2,1,0:T(8,128)(2,1)} %get-tuple-element.56), channel_id=1, source_target_pairs={{0,32},{32,64},{64,96},{96,0},{1,33},{33,65},{65,97},{97,1},{2,34}... | collective-permute-start | bytes 786440 | tf_op jit(solution)/shard_map/ppermute | solution.py:476
  7.7 15.7 %collective-permute-start.1 = (bf16[4,16,16,128]{3,2,1,0:T(8,128)(2,1)S(1)}, bf16[4,16,16,128]{3,2,1,0:T(8,128)(2,1)S(1)}, u32[]{:S(2)}, u32[]{:S(2)}) collective-permute-start(bf16[4,16,16,128]{3,2,1,0:T(8,128)(2,1)S(1)} %get-tuple-element.57), channel_id=1, source_target_pairs={{0,96},{32,0},{64,32},{96,64},{1,97},{33,1},{65,33},{97,65},{2,98}... | collective-permute-start | bytes 786440 | tf_op jit(solution)/shard_map/ppermute | solution.py:476
  14.0 11.1 %collective-permute-start.4 = (bf16[4,16,16,128]{3,2,1,0:T(8,128)(2,1)S(1)}, bf16[4,16,16,128]{3,2,1,0:T(8,128)(2,1)S(1)}, u32[]{:S(2)}, u32[]{:S(2)}) collective-permute-start(bf16[4,16,16,128]{3,2,1,0:T(8,128)(2,1)S(1)} %get-tuple-element.60), channel_id=1, source_target_pairs={{0,32},{32,64},{64,96},{96,0},{1,33},{33,65},{65,97},{97,1},{2,34}... | collective-permute-start | bytes 786440 | tf_op jit(solution)/shard_map/ppermute | solution.py:476
  14.4 10.7 %collective-permute-start.5 = (bf16[4,16,16,128]{3,2,1,0:T(8,128)(2,1)S(1)}, bf16[4,16,16,128]{3,2,1,0:T(8,128)(2,1)S(1)}, u32[]{:S(2)}, u32[]{:S(2)}) collective-permute-start(bf16[4,16,16,128]{3,2,1,0:T(8,128)(2,1)S(1)} %get-tuple-element.61), channel_id=1, source_target_pairs={{0,96},{32,0},{64,32},{96,64},{1,97},{33,1},{65,33},{97,65},{2,98}... | collective-permute-start | bytes 786440 | tf_op jit(solution)/shard_map/ppermute | solution.py:476
  27.2 29.6 %all-to-all-start = ((bf16[256,16,128]{2,1,0:T(8,128)(2,1)}), bf16[256,16,128]{2,1,0:T(8,128)(2,1)S(1)}, u32[]{:S(2)}, u32[]{:S(2)}) async-start(bf16[256,16,128]{2,1,0:T(8,128)(2,1)} %sum_and_gather.1), calls=%async_computation | async-start | bytes 2097152 | tf_op jit(solution)/shard_map/all_to_all | solution.py:504
  65.9 22.9 %all-to-all-start.1 = ((bf16[256,16,128]{2,1,0:T(8,128)(2,1)}), bf16[256,16,128]{2,1,0:T(8,128)(2,1)S(1)}, u32[]{:S(2)}, u32[]{:S(2)}) async-start(bf16[256,16,128]{2,1,0:T(8,128)(2,1)} %bitcast.3), calls=%async_computation.1 | async-start | bytes 2097152 | tf_op jit(solution)/shard_map/all_to_all | solution.py:512

commit v3 on v2

--- a/solution.py
+++ b/solution.py
@@ -163,7 +163,7 @@
 def early_kernel(slots, count, *refs):
     items = len(slots)
     ins, outs = refs[: 2 * items], refs[2 * items : 6 * items]
-    roots, factors, highs, lows, products, traces, in_sem, out_sem = refs[6 * items :]
+    roots, factors, lows, products, traces, in_sem, out_sem = refs[6 * items :]
     n = roots.shape[1]
 
     def arrivals(k):
@@ -176,16 +176,13 @@
 
     def departures(k):
         return [
-            pltpu.make_async_copy(held.at[k], outs[4 * k + i], out_sem.at[k, i])
-            for i, held in enumerate((highs, lows, products, traces))
+            pltpu.make_async_copy(held.at[k], outs[4 * k + 1 + i], out_sem.at[k, i])
+            for i, held in enumerate((lows, products, traces))
         ]
 
-    for k in range(items):
-
-        @pl.when(slots[k] < count[0])
-        def _():
-            for copy in arrivals(k):
-                copy.start()
+    @pl.when(slots[0] < count[0])
+    def _():
+        arrivals(0)[0].start()
 
     for k in range(items):
 
@@ -193,13 +190,19 @@
         def _():
             coming, going = arrivals(k), departures(k)
             coming[0].wait()
+            coming[1].start()
+            if k + 1 < items:
+
+                @pl.when(slots[k + 1] < count[0])
+                def _():
+                    arrivals(k + 1)[0].start()
+
             x = halves(roots[k])
             square = halves(mul3(x, x))
             fourth = halves(mul3(square, square))
             fifth = halves(mul3(x, fourth))
-            highs[k], lows[k] = fifth
+            outs[4 * k][...], lows[k] = fifth
             going[0].start()
-            going[1].start()
             coming[1].wait()
             total = jnp.zeros((128, 128), f32)
             on = lax.broadcasted_iota(jnp.int32, (128, 128), 0)
@@ -208,8 +211,8 @@
                 total += factors[k, d : d + 128, d : d + 128]
             traces[k] = jnp.full(traces.shape[1:], jnp.sum(jnp.where(on, total, 0.0)))
             products[k] = decay_rate * mul3(fifth, halves(factors[k]))
+            going[1].start()
             going[2].start()
-            going[3].start()
 
     for k in range(items):
 
@@ -225,23 +228,22 @@
     made = pl.pallas_call(
         functools.partial(early_kernel, [t for t, _, _ in items]),
         out_shape=(
-            stored(n, n, dtype=bf16),
+            pltpu.VMEM((n, n), bf16),
             stored(n, n, dtype=bf16),
             stored(n, n),
             stored(8, 128),
         )
         * many,
         in_specs=[scalars] + [in_place] * (2 * many),
-        out_specs=(in_place,) * (4 * many),
+        out_specs=(whole, in_place, in_place, in_place) * many,
         scratch_shapes=[
             pltpu.VMEM((many, n, n), f32),
             pltpu.VMEM((many, n, n), f32),
             pltpu.VMEM((many, n, n), bf16),
-            pltpu.VMEM((many, n, n), bf16),
             pltpu.VMEM((many, n, n), f32),
             pltpu.VMEM((many, 8, 128), f32),
             pltpu.SemaphoreType.DMA((many, 2)),
-            pltpu.SemaphoreType.DMA((many, 4)),
+            pltpu.SemaphoreType.DMA((many, 3)),
         ],
         compiler_params=params(28),
         cost_estimate=pl.CostEstimate(
@@ -263,26 +265,27 @@
     return block[...]
 
 
-def quarter_scale(trace, block, gain):
+def square_sum(block):
     wide = block.astype(f32)
-    square = jnp.sum(wide * wide)
-    total = decay_rate * trace[0:1, 0:1] + gain * square
-    return (0.25 * block.shape[0]) / total
+    return jnp.sum(wide * wide)
+
+
+def quarter_scale(trace, square, gain, n):
+    return (0.25 * n) / (decay_rate * trace[0:1, 0:1] + gain * square)
 
 
 def update_kernel(gain, slots, count, pieces, xl, xr, *refs):
     ready, refs = refs[: 6 * slots], refs[6 * slots :]
-    out, blocks, fives, singles, traces, in_sem = refs
-    parts, shards, _, rows, width = out.shape
+    out, blocks, singles, traces, made, in_sem, out_sem = refs
+    parts, shards, _, rows, width = made.shape
+    n = parts * width
 
     def arrivals(t):
-        fl, pl_, tl, fr, pr, tr = ready[6 * t : 6 * t + 6]
+        _, pl_, tl, _, pr, tr = ready[6 * t : 6 * t + 6]
         sources = (
-            (fl, fives.at[t, 0]),
             (tl, traces.at[t, 0]),
             (xl.at[t], singles.at[t, 0]),
             (pl_, singles.at[t, 1]),
-            (fr, fives.at[t, 1]),
             (tr, traces.at[t, 1]),
             (xr.at[t], singles.at[t, 2]),
             (pr, singles.at[t, 3]),
@@ -291,48 +294,58 @@
             pltpu.make_async_copy(a, b, in_sem.at[t, k]) for k, (a, b) in enumerate(sources)
         ]
 
+    def departure(h):
+        span = pl.ds(h * parts // 2, parts // 2)
+        return pltpu.make_async_copy(made.at[span], out.at[span], out_sem.at[h])
+
     def work(ts):
         copies = {t: arrivals(t) for t in ts}
         for t in ts:
             for copy in copies[t]:
                 copy.start()
-        g, side, part = {}, {}, {}
+        g, left, right, part, square = {}, {}, {}, {}, {}
         for t in ts:
             g[t] = assembled(pieces, t, blocks.at[t])
+            square[t] = square_sum(g[t])
         for t in ts:
-            copies[t][0].wait()
+            left[t] = mul_t(mul(ready[6 * t][...], g[t]).astype(bf16), g[t])
         for t in ts:
-            side[t] = mul_t(mul(fives[t, 0], g[t]).astype(bf16), g[t])
+            right[t] = mul(mul_t(ready[6 * t + 3][...], g[t]).astype(bf16), g[t])
         for t in ts:
-            for copy in copies[t][1:4]:
+            for copy in copies[t][:3]:
                 copy.wait()
+            scale = quarter_scale(traces[t, 0], square[t], gain, n)
+            left[t] = 1.25 * singles[t, 0] - scale * (singles[t, 1] + gain * left[t])
+            part[t] = mul(left[t].astype(bf16), g[t]).astype(bf16)
         for t in ts:
-            scale = quarter_scale(traces[t, 0], g[t], gain)
-            side[t] = 1.25 * singles[t, 0] - scale * (singles[t, 1] + gain * side[t])
-            part[t] = mul(side[t].astype(bf16), g[t]).astype(bf16)
-        for t in ts:
-            copies[t][4].wait()
-        for t in ts:
-            side[t] = mul(mul_t(fives[t, 1], g[t]).astype(bf16), g[t])
-        for t in ts:
-            for copy in copies[t][5:]:
+            for copy in copies[t][3:]:
                 copy.wait()
-        for t in ts:
-            scale = quarter_scale(traces[t, 1], g[t], gain)
-            side[t] = 1.25 * singles[t, 2] - scale * (singles[t, 3] + gain * side[t])
-            done = mul(part[t], side[t].astype(bf16)).astype(bf16)
-            for z in range(parts):
-                out[z, :, t] = done[:, z * width : (z + 1) * width].reshape(
-                    shards, rows, width
-                )
+            scale = quarter_scale(traces[t, 1], square[t], gain, n)
+            right[t] = 1.25 * singles[t, 2] - scale * (singles[t, 3] + gain * right[t])
+            right[t] = right[t].astype(bf16)
+        for h in range(2):
+            for t in ts:
+                done = mul(part[t], right[t][:, h * n // 2 : (h + 1) * n // 2]).astype(bf16)
+                for k in range(parts // 2):
+                    made[h * parts // 2 + k, :, t] = done[
+                        :, k * width : (k + 1) * width
+                    ].reshape(shards, rows, width)
+            departure(h).start()
 
     for live in range(slots + 1):
 
         @pl.when(count[0] == live)
         def _():
-            work(range(live))
             for t in range(live, slots):
-                out[:, :, t] = jnp.zeros_like(out[:, :, t])
+                made[:, :, t] = jnp.zeros_like(made[:, :, t])
+            if live:
+                work(range(live))
+            else:
+                departure(0).start()
+                departure(1).start()
+
+    departure(0).wait()
+    departure(1).wait()
 
 
 def update_pieces(gain, count, pieces, xl, xr, ready):
@@ -341,18 +354,20 @@
     inputs = []
     for sides in ready:
         for high, _, product, trace in sides:
-            inputs += [hbm(high), hbm(product), hbm(trace)]
+            inputs += [vmem(high), hbm(product), hbm(trace)]
     return pl.pallas_call(
         functools.partial(update_kernel, gain, slots),
-        out_shape=jax.ShapeDtypeStruct(pieces.shape, bf16),
-        in_specs=[scalars, whole] + [in_place] * (2 + len(inputs)),
-        out_specs=whole,
+        out_shape=stored(*pieces.shape, dtype=bf16),
+        in_specs=[scalars, whole] + [in_place] * 2
+        + [whole, in_place, in_place] * (len(inputs) // 3),
+        out_specs=in_place,
         scratch_shapes=[
             pltpu.VMEM((slots, n, n), bf16),
-            pltpu.VMEM((slots, 2, n, n), bf16),
             pltpu.VMEM((slots, 4, n, n), f32),
             pltpu.VMEM((slots, 2, 8, 128), f32),
-            pltpu.SemaphoreType.DMA((slots, 8)),
+            pltpu.VMEM(pieces.shape, bf16),
+            pltpu.SemaphoreType.DMA((slots, 6)),
+            pltpu.SemaphoreType.DMA((2,)),
         ],
         compiler_params=params(32),
         name="update_pieces",
@@ -408,8 +423,9 @@
             g = assembled(pieces, t, block)
             for copy in copies:
                 copy.wait()
-            left_scale = quarter_scale(traces[t, 0], g, gain)
-            right_scale = quarter_scale(traces[t, 1], g, gain)
+            square = square_sum(g)
+            left_scale = quarter_scale(traces[t, 0], square, gain, n)
+            right_scale = quarter_scale(traces[t, 1], square, gain, n)
             made[t, 0] = decay_rate * singles[t, 0] + gain * mul_t(g, g)
             leaving[0].start()
             made[t, 1] = decay_rate * singles[t, 1] + gain * t_mul(g, g)
@@ -476,10 +492,9 @@
         return lax.ppermute(x, "dp", [(i, (i + step) % replicas) for i in range(replicas)])
 
     half = row_blocks // 2
-    far_low, far_high, near_high, near_low = windows(
-        mine, width, ((0, 2), (half, 2), (half, 1), (0, 3))
-    )
+    far_low, far_high = windows(mine, width, ((0, 2), (half, 2)))
     far_low, far_high = hop(far_low, 1), hop(far_high, -1)
+    near_high, near_low = windows(mine, width, ((half, 1), (0, 3)))
     near_high, near_low = hop(near_high, 1), hop(near_low, -1)
 
     entries = jnp.arange(owner_list.shape[0], dtype=jnp.int32)

time: 91.4 us -> 90.8 us (level)
  Pallas kernels: 48.1 us -> 18.5 us
  waiting for transfers between devices: 16.7 us -> 38.8 us
  starting transfers between devices: 24 us -> 31.4 us
    pallas_call x2, Pallas kernels: 21 us -> 1.67 us  [early(): pl.pallas_call(functools.partial(early_kernel, [t for t, _, _ in items]),...]
    all_to_all x1, waiting for transfers between devices: 4.88 us -> 18.3 us  [body(): lax.all_to_all(outgoing, ('dp', 'shard'), split_axis=0, concat_axis=0, ti...]
    all_to_all x1, starting transfers between devices: 3.59 us -> 10.9 us  [body(): lax.all_to_all(outbound.reshape(all_slots, rows, width), ('dp', 'shard'),...]
    pallas_call x1, Pallas kernels: 9.06 us -> 1.87 us  [update_pieces(): pl.pallas_call(functools.partial(update_kernel, gain, slots), out_shape=s...]
    all_to_all x1, waiting for transfers between devices: 7.55 us -> 12.1 us  [body(): lax.all_to_all(outbound.reshape(all_slots, rows, width), ('dp', 'shard'),...]
    pallas_call x1, Pallas kernels: 11.8 us -> 7.21 us  [new_state(): pl.pallas_call(functools.partial(state_kernel, gain, slots), out_shape=(s...]
    ppermute x6, waiting for transfers between devices: 4.27 us -> 8.33 us  [hop(): lax.ppermute(x, 'dp', [(i, (i + step) % replicas) for i in range(replicas)])]
    pallas_call x1 -> x2, Pallas kernels: 2.27 us -> 3.76 us  [windows(): pl.pallas_call(functools.partial(window_kernel, parts), out_shape=(pltpu....]
  transfers between devices with their start and end apart: 8 -> 8, of which waited for: 4 -> 5; matrix products, arithmetic and copies ran while one was open for 1% -> 1% of each run, Pallas kernels for 36% -> 12%
where the time goes in v3:
time: 90.8 us; the launch traced here: 90.4 us
  waiting for transfers between devices  38.8 us (43%)
  starting transfers between devices  31.4 us (35%)
  Pallas kernels  18.5 us (20%)
  other arithmetic  0.93 us (1%)
    all_to_all x1, waiting for transfers between devices, body(): lax.all_to_all(outgoing, ('dp', 'shard'), split_axis=0, concat_axis=0, ti...  18.3 us
    all_to_all x1, waiting for transfers between devices, body(): lax.all_to_all(outbound.reshape(all_slots, rows, width), ('dp', 'shard'),...  12.1 us
    all_to_all x1, starting transfers between devices, body(): lax.all_to_all(outbound.reshape(all_slots, rows, width), ('dp', 'shard'),...  10.9 us
    ppermute x6, starting transfers between devices, hop(): lax.ppermute(x, 'dp', [(i, (i + step) % replicas) for i in range(replicas)])  10.2 us
    all_to_all x1, starting transfers between devices, body(): lax.all_to_all(outgoing, ('dp', 'shard'), split_axis=0, concat_axis=0, ti...  10.2 us
    ppermute x6, waiting for transfers between devices, hop(): lax.ppermute(x, 'dp', [(i, (i + step) % replicas) for i in range(replicas)])  8.33 us
    pallas_call x1, Pallas kernels, new_state(): pl.pallas_call(functools.partial(state_kernel, gain, slots), out_shape=(s...  7.21 us
    pallas_call x2, Pallas kernels, windows(): pl.pallas_call(functools.partial(window_kernel, parts), out_shape=(pltpu....  3.76 us
  transfers between devices with their start and end apart: 8, of which 5 were waited for; matrix products, arithmetic and copies ran while one was open for 1% of the time, Pallas kernels for 12%

profile of v3, /device:TPU:1, one launch (start us, length us, event | category | flops | bytes accessed | tf_op | source)
XLA Modules:
  0.0 90.4 jit_solution(10591530813278597625)
XLA Ops:
  0.6 0.0 copy-start.5
  0.6 0.0 copy-start.6
  0.7 0.0 copy-start.7
  0.7 0.0 copy-start
  0.7 2.0 %windows.3 = (bf16[4,16,16,128]{3,2,1,0:T(8,128)(2,1)}, bf16[4,16,16,128]{3,2,1,0:T(8,128)(2,1)}) custom-call(bf16[8,16,16,512]{3,2,1,0:T(8,128)(2,1)} %bitcast.4), custom_call_target="tpu_custom_call" | custom-call | tf_op jit(solution)/shard_map/windows/pallas_call | solution.py:79
  2.7 2.5 %collective-permute-start.2 = (bf16[4,16,16,128]{3,2,1,0:T(8,128)(2,1)}, bf16[4,16,16,128]{3,2,1,0:T(8,128)(2,1)S(1)}, u32[]{:S(2)}, u32[]{:S(2)}) collective-permute-start(bf16[4,16,16,128]{3,2,1,0:T(8,128)(2,1)} %get-tuple-element.58), channel_id=1, source_target_pairs={{0,32},{32,64},{64,96},{96,0},{1,33},{33,65},{65,97},{97,1},{2,34}... | collective-permute-start | bytes 786440 | tf_op jit(solution)/shard_map/ppermute | solution.py:492
  5.2 2.2 %collective-permute-start.3 = (bf16[4,16,16,128]{3,2,1,0:T(8,128)(2,1)}, bf16[4,16,16,128]{3,2,1,0:T(8,128)(2,1)S(1)}, u32[]{:S(2)}, u32[]{:S(2)}) collective-permute-start(bf16[4,16,16,128]{3,2,1,0:T(8,128)(2,1)} %get-tuple-element.59), channel_id=1, source_target_pairs={{0,96},{32,0},{64,32},{96,64},{1,97},{33,1},{65,33},{97,65},{2,98}... | collective-permute-start | bytes 786440 | tf_op jit(solution)/shard_map/ppermute | solution.py:492
  7.4 1.8 %windows.2 = (bf16[4,16,16,128]{3,2,1,0:T(8,128)(2,1)}, bf16[4,16,16,128]{3,2,1,0:T(8,128)(2,1)S(1)}) custom-call(bf16[8,16,16,512]{3,2,1,0:T(8,128)(2,1)} %bitcast.5), custom_call_target="tpu_custom_call" | custom-call | tf_op jit(solution)/shard_map/windows/pallas_call | solution.py:79
  9.2 0.1 collective-permute-start
  9.3 2.7 %collective-permute-start.1 = (bf16[4,16,16,128]{3,2,1,0:T(8,128)(2,1)S(1)}, bf16[4,16,16,128]{3,2,1,0:T(8,128)(2,1)S(1)}, u32[]{:S(2)}, u32[]{:S(2)}) collective-permute-start(bf16[4,16,16,128]{3,2,1,0:T(8,128)(2,1)S(1)} %get-tuple-element.57), channel_id=1, source_target_pairs={{0,96},{32,0},{64,32},{96,64},{1,97},{33,1},{65,33},{97,65},{2,98}... | collective-permute-start | bytes 786440 | tf_op jit(solution)/shard_map/ppermute | solution.py:492
  11.9 0.0 copy-done.5
  11.9 0.2 convert_reduce_fusion
  12.1 0.6 fusion.1
  12.8 0.0 copy-done.6
  12.8 0.0 copy-done.7
  12.8 0.1 select_reduce_fusion.table
  12.9 0.7 collective-permute-done.2.low_in
  13.6 0.0 collective-permute-done.3.high_in
  13.6 0.0 copy-done
  13.6 0.1 merge_far_part.1
  13.7 0.4 collective-permute-start.4
  14.1 2.3 %collective-permute-start.5 = (bf16[4,16,16,128]{3,2,1,0:T(8,128)(2,1)S(1)}, bf16[4,16,16,128]{3,2,1,0:T(8,128)(2,1)S(1)}, u32[]{:S(2)}, u32[]{:S(2)}) collective-permute-start(bf16[4,16,16,128]{3,2,1,0:T(8,128)(2,1)S(1)} %get-tuple-element.61), channel_id=1, source_target_pairs={{0,96},{32,0},{64,32},{96,64},{1,97},{33,1},{65,33},{97,65},{2,98}... | collective-permute-start | bytes 786440 | tf_op jit(solution)/shard_map/ppermute | solution.py:492
  16.5 0.7 early_products.2
  17.2 0.0 copy-start.1
  17.2 2.0 %collective-permute-done.ups = bf16[4,16,16,128]{3,2,1,0:T(8,128)(2,1)S(1)} collective-permute-done((bf16[4,16,16,128]{3,2,1,0:T(8,128)(2,1)}, bf16[4,16,16,128]{3,2,1,0:T(8,128)(2,1)S(1)}, u32[]{:S(2)}, u32[]{:S(2)}) %collective-permute-start) | collective-permute-done | bytes 262176 | tf_op jit(solution)/shard_map/ppermute | solution.py:492
  19.2 0.0 collective-permute-done.1.downs
  19.2 5.6 %collective-permute-done.4.ups_more = bf16[4,16,16,128]{3,2,1,0:T(8,128)(2,1)S(1)} collective-permute-done((bf16[4,16,16,128]{3,2,1,0:T(8,128)(2,1)S(1)}, bf16[4,16,16,128]{3,2,1,0:T(8,128)(2,1)S(1)}, u32[]{:S(2)}, u32[]{:S(2)}) %collective-permute-start.4) | collective-permute-done | bytes 262176 | tf_op jit(solution)/shard_map/ppermute | solution.py:492
  24.8 0.0 collective-permute-done.5.downs_more
  24.8 2.1 %sum_and_gather.1 = bf16[256,16,128]{2,1,0:T(8,128)(2,1)} custom-call(s32[128]{0:T(128)S(1)} %select_reduce_fusion.table, bf16[8,16,16,512]{3,2,1,0:T(8,128)(2,1)S(1)} %bitcast.7, bf16[4,16,16,128]{3,2,1,0:T(8,128)(2,1)S(1)} %collective-permute-done.ups, bf16[4,16,16,128]{3,2,1,0:T(8,128)(2,1)S(1)} %collective-permute-done.1.downs, ...), custom_call_target="tpu_custom_call" | custom-call | tf_op jit(solution)/shard_map/sum_and_gather/pallas_call | solution.py:128
  26.9 10.2 %all-to-all-start = ((bf16[256,16,128]{2,1,0:T(8,128)(2,1)}), bf16[256,16,128]{2,1,0:T(8,128)(2,1)S(1)}, u32[]{:S(2)}, u32[]{:S(2)}) async-start(bf16[256,16,128]{2,1,0:T(8,128)(2,1)} %sum_and_gather.1), calls=%async_computation | async-start | bytes 2097152 | tf_op jit(solution)/shard_map/all_to_all | solution.py:519
  37.2 1.0 %early_products.3 = (bf16[512,512]{1,0:T(8,128)(2,1)S(1)}, bf16[512,512]{1,0:T(8,128)(2,1)}, f32[512,512]{1,0:T(8,128)}, f32[8,128]{1,0:T(8,128)}, bf16[512,512]...) custom-call(s32[1]{0:T(128)} %bitcast.count, ...), custom_call_target="tpu_custom_call" | custom-call | flops 9663676416 | bytes 12582912 | tf_op jit(solution)/shard_map/early_products/pallas_call | solution.py:228
  38.2 0.0 copy-start.2
  38.2 0.0 copy-start.3
  38.2 0.0 copy-start.4
  38.2 18.3 %all-to-all-done = bf16[256,16,128]{2,1,0:T(8,128)(2,1)S(1)} async-done(((bf16[256,16,128]{2,1,0:T(8,128)(2,1)}), bf16[256,16,128]{2,1,0:T(8,128)(2,1)S(1)}, u32[]{:S(2)}, u32[]{:S(2)}) %all-to-all-start) | async-done | bytes 1048608 | tf_op jit(solution)/shard_map/all_to_all | solution.py:519
  56.5 0.0 copy-done.1
  56.5 1.9 %update_pieces.1 = bf16[4,32,2,16,128]{4,3,2,1,0:T(8,128)(2,1)} custom-call(s32[1]{0:T(128)} %bitcast.count, bf16[4,32,2,16,128]{4,3,2,1,0:T(8,128)(2,1)S(1)} %bitcast.8, f32[2,512,512]{2,1,0:T(8,128)} %xl.3, f32[2,512,512]{2,1,0:T(8,128)} %xr.3, bf16[512,512]{1,0:T(8,128)(2,1)S(1)} %get-tuple-element.87.refs_0_, ...), custom_call_target="tpu_custom_call" | custom-call | tf_op jit(solution)/shard_map/update_pieces/pallas_call | solution.py:358
  58.4 0.0 copy-done.2
  58.4 0.0 copy-done.3
  58.4 0.0 copy-done.4
  58.4 10.9 %all-to-all-start.1 = ((bf16[256,16,128]{2,1,0:T(8,128)(2,1)}), bf16[256,16,128]{2,1,0:T(8,128)(2,1)S(1)}, u32[]{:S(2)}, u32[]{:S(2)}) async-start(bf16[256,16,128]{2,1,0:T(8,128)(2,1)} %bitcast.10), calls=%async_computation.1 | async-start | bytes 2097152 | tf_op jit(solution)/shard_map/all_to_all | solution.py:527
  69.4 7.2 %new_state.1 = (f32[2,512,512]{2,1,0:T(8,128)}, f32[2,512,512]{2,1,0:T(8,128)}, f32[2,512,512]{2,1,0:T(8,128)}, f32[2,512,512]{2,1,0:T(8,128)}) custom-call(s32[1]{0:T(128)} %bitcast.count, bf16[4,32,2,16,128]{4,3,2,1,0:T(8,128)(2,1)S(1)} %bitcast.9, f32[2,512,512]{2,1,0:T(8,128)} %left.1, f32[2,512,512]{2,1,0:T(8,128)} %right.1, f32[2,512,512]{2,1,0:T(8,128)} %xl.3, ...), custom_call_target="tpu_custom_call" | custom-call | flops 5368709120 | bytes 25165824 | tf_op jit(solution)/shard_map/new_state/pallas_call | solution.py:456
  76.6 12.1 %all-to-all-done.1.arrived = bf16[256,16,128]{2,1,0:T(8,128)(2,1)S(1)} async-done(((bf16[256,16,128]{2,1,0:T(8,128)(2,1)}), bf16[256,16,128]{2,1,0:T(8,128)(2,1)S(1)}, u32[]{:S(2)}, u32[]{:S(2)}) %all-to-all-start.1) | async-done | bytes 1048608 | tf_op jit(solution)/shard_map/all_to_all | solution.py:527
  88.7 1.7 %place_pieces.1 = bf16[8,16,16,128]{3,2,1,0:T(8,128)(2,1)} custom-call(s32[128]{0:T(128)S(1)} %select_reduce_fusion.table, bf16[256,16,128]{2,1,0:T(8,128)(2,1)S(1)} %all-to-all-done.1.arrived), custom_call_target="tpu_custom_call" | custom-call | tf_op jit(solution)/shard_map/place_pieces/pallas_call | solution.py:151
  (1 shorter events, 0.0 us)
Async XLA Ops:
  0.6 11.3 %copy-start.5 = (s32[128]{0:T(128)S(1)}, s32[128]{0:T(128)}, u32[]{:S(2)}) copy-start(s32[128]{0:T(128)} %param.9) | copy-start | bytes 1540
  0.6 12.1 %copy-start.6 = (s32[128]{0:T(128)S(1)}, s32[128]{0:T(128)}, u32[]{:S(2)}) copy-start(s32[128]{0:T(128)} %param.11) | copy-start | bytes 1540
  0.7 12.1 %copy-start.7 = (s32[128]{0:T(128)S(1)}, s32[128]{0:T(128)}, u32[]{:S(2)}) copy-start(s32[128]{0:T(128)} %param.10) | copy-start | bytes 1540
  0.7 12.9 %copy-start = (bf16[1,8,16,16,512]{4,3,2,1,0:T(8,128)(2,1)S(1)}, bf16[1,8,16,16,512]{4,3,2,1,0:T(8,128)(2,1)}, u32[]{:S(2)}) copy-start(bf16[1,8,16,16,512]{4,3,2,1,0:T(8,128)(2,1)} %param.8) | copy-start | bytes 6291460
  2.7 10.9 %collective-permute-start.2 = (bf16[4,16,16,128]{3,2,1,0:T(8,128)(2,1)}, bf16[4,16,16,128]{3,2,1,0:T(8,128)(2,1)S(1)}, u32[]{:S(2)}, u32[]{:S(2)}) collective-permute-start(bf16[4,16,16,128]{3,2,1,0:T(8,128)(2,1)} %get-tuple-element.58), channel_id=1, source_target_pairs={{0,32},{32,64},{64,96},{96,0},{1,33},{33,65},{65,97},{97,1},{2,34}... | collective-permute-start | bytes 786440 | tf_op jit(solution)/shard_map/ppermute | solution.py:492
  5.2 8.4 %collective-permute-start.3 = (bf16[4,16,16,128]{3,2,1,0:T(8,128)(2,1)}, bf16[4,16,16,128]{3,2,1,0:T(8,128)(2,1)S(1)}, u32[]{:S(2)}, u32[]{:S(2)}) collective-permute-start(bf16[4,16,16,128]{3,2,1,0:T(8,128)(2,1)} %get-tuple-element.59), channel_id=1, source_target_pairs={{0,96},{32,0},{64,32},{96,64},{1,97},{33,1},{65,33},{97,65},{2,98}... | collective-permute-start | bytes 786440 | tf_op jit(solution)/shard_map/ppermute | solution.py:492
  9.2 10.0 %collective-permute-start = (bf16[4,16,16,128]{3,2,1,0:T(8,128)(2,1)}, bf16[4,16,16,128]{3,2,1,0:T(8,128)(2,1)S(1)}, u32[]{:S(2)}, u32[]{:S(2)}) collective-permute-start(bf16[4,16,16,128]{3,2,1,0:T(8,128)(2,1)} %get-tuple-element.56), channel_id=1, source_target_pairs={{0,32},{32,64},{64,96},{96,0},{1,33},{33,65},{65,97},{97,1},{2,34}... | collective-permute-start | bytes 786440 | tf_op jit(solution)/shard_map/ppermute | solution.py:492
  9.3 9.9 %collective-permute-start.1 = (bf16[4,16,16,128]{3,2,1,0:T(8,128)(2,1)S(1)}, bf16[4,16,16,128]{3,2,1,0:T(8,128)(2,1)S(1)}, u32[]{:S(2)}, u32[]{:S(2)}) collective-permute-start(bf16[4,16,16,128]{3,2,1,0:T(8,128)(2,1)S(1)} %get-tuple-element.57), channel_id=1, source_target_pairs={{0,96},{32,0},{64,32},{96,64},{1,97},{33,1},{65,33},{97,65},{2,98}... | collective-permute-start | bytes 786440 | tf_op jit(solution)/shard_map/ppermute | solution.py:492
  13.7 11.1 %collective-permute-start.4 = (bf16[4,16,16,128]{3,2,1,0:T(8,128)(2,1)S(1)}, bf16[4,16,16,128]{3,2,1,0:T(8,128)(2,1)S(1)}, u32[]{:S(2)}, u32[]{:S(2)}) collective-permute-start(bf16[4,16,16,128]{3,2,1,0:T(8,128)(2,1)S(1)} %get-tuple-element.60), channel_id=1, source_target_pairs={{0,32},{32,64},{64,96},{96,0},{1,33},{33,65},{65,97},{97,1},{2,34}... | collective-permute-start | bytes 786440 | tf_op jit(solution)/shard_map/ppermute | solution.py:492
  14.1 10.7 %collective-permute-start.5 = (bf16[4,16,16,128]{3,2,1,0:T(8,128)(2,1)S(1)}, bf16[4,16,16,128]{3,2,1,0:T(8,128)(2,1)S(1)}, u32[]{:S(2)}, u32[]{:S(2)}) collective-permute-start(bf16[4,16,16,128]{3,2,1,0:T(8,128)(2,1)S(1)} %get-tuple-element.61), channel_id=1, source_target_pairs={{0,96},{32,0},{64,32},{96,64},{1,97},{33,1},{65,33},{97,65},{2,98}... | collective-permute-start | bytes 786440 | tf_op jit(solution)/shard_map/ppermute | solution.py:492
  17.2 39.3 %copy-start.1 = (bf16[512,512]{1,0:T(8,128)(2,1)}, bf16[512,512]{1,0:T(8,128)(2,1)S(1)}, u32[]{:S(2)}) copy-start(bf16[512,512]{1,0:T(8,128)(2,1)S(1)} %get-tuple-element.87.refs_0_) | copy-start | bytes 1572868
  26.9 29.6 %all-to-all-start = ((bf16[256,16,128]{2,1,0:T(8,128)(2,1)}), bf16[256,16,128]{2,1,0:T(8,128)(2,1)S(1)}, u32[]{:S(2)}, u32[]{:S(2)}) async-start(bf16[256,16,128]{2,1,0:T(8,128)(2,1)} %sum_and_gather.1), calls=%async_computation | async-start | bytes 2097152 | tf_op jit(solution)/shard_map/all_to_all | solution.py:519
  38.2 20.2 %copy-start.2 = (bf16[512,512]{1,0:T(8,128)(2,1)}, bf16[512,512]{1,0:T(8,128)(2,1)S(1)}, u32[]{:S(2)}) copy-start(bf16[512,512]{1,0:T(8,128)(2,1)S(1)} %get-tuple-element.90.refs_3_.refs_4_) | copy-start | bytes 1572868
  38.2 20.2 %copy-start.3 = (bf16[512,512]{1,0:T(8,128)(2,1)}, bf16[512,512]{1,0:T(8,128)(2,1)S(1)}, u32[]{:S(2)}) copy-start(bf16[512,512]{1,0:T(8,128)(2,1)S(1)} %get-tuple-element.93.refs_6_.refs_8_) | copy-start | bytes 1572868
  38.2 20.2 %copy-start.4 = (bf16[512,512]{1,0:T(8,128)(2,1)}, bf16[512,512]{1,0:T(8,128)(2,1)S(1)}, u32[]{:S(2)}) copy-start(bf16[512,512]{1,0:T(8,128)(2,1)S(1)} %get-tuple-element.96.refs_9_.refs_12_) | copy-start | bytes 1572868
  58.4 30.3 %all-to-all-start.1 = ((bf16[256,16,128]{2,1,0:T(8,128)(2,1)}), bf16[256,16,128]{2,1,0:T(8,128)(2,1)S(1)}, u32[]{:S(2)}, u32[]{:S(2)}) async-start(bf16[256,16,128]{2,1,0:T(8,128)(2,1)} %bitcast.10), calls=%async_computation.1 | async-start | bytes 2097152 | tf_op jit(solution)/shard_map/all_to_all | solution.py:527

commit v4 on v3

v4 whole, which is shorter than its diff:
```python
import functools

import jax
import jax.numpy as jnp
from jax import lax
from jax.experimental import pallas as pl
from jax.experimental.pallas import tpu as pltpu
from jax.sharding import PartitionSpec as P

decay_rate = 0.9
f32 = jnp.float32
bf16 = jnp.bfloat16
MIB = 1 << 20


def params(mib):
    return pltpu.CompilerParams(vmem_limit_bytes=mib * MIB)


def halves(x):
    high = x.astype(bf16)
    return high, (x - high.astype(f32)).astype(bf16)


def mul(a, b):
    return jnp.dot(a, b, preferred_element_type=f32)


def mul_t(a, b):
    return lax.dot_general(a, b, (((1,), (1,)), ((), ())), preferred_element_type=f32)


def t_mul(a, b):
    return lax.dot_general(a, b, (((0,), (0,)), ((), ())), preferred_element_type=f32)


def mul3(a, b):
    return mul(a[0], b[0]) + (mul(a[0], b[1]) + mul(a[1], b[0]))


def vmem(x):
    return pltpu.with_memory_space_constraint(x, pltpu.VMEM)


def hbm(x):
    return pltpu.with_memory_space_constraint(x, pltpu.HBM)


def stored(*shape, dtype=f32):
    return pltpu.HBM(shape, dtype)


whole = pl.BlockSpec(memory_space=pltpu.VMEM)
scalars = pl.BlockSpec(memory_space=pltpu.SMEM)
in_place = pl.BlockSpec(memory_space=pl.ANY)


def column_at(hop, width):
    replicas = lax.axis_size("dp")
    z = lax.rem(lax.axis_index("dp").astype(jnp.int32) + hop, replicas)
    return pl.ds(pl.multiple_of(z * width, width), width)


def window_kernel(parts, mine, *refs):
    outs, sem = refs[:-1], refs[-1]
    copies = []
    for k, ((low, hop), out) in enumerate(zip(parts, outs)):
        half, width = out.shape[0], out.shape[-1]
        source = mine.at[low : low + half, :, :, column_at(hop, width)]
        copies.append(pltpu.make_async_copy(source, out, sem.at[k]))
    for copy in copies:
        copy.start()
    for copy in copies:
        copy.wait()


def windows(mine, width, parts):
    row_blocks, rows, cols, _ = mine.shape
    return pl.pallas_call(
        functools.partial(window_kernel, parts),
        out_shape=(pltpu.VMEM((row_blocks // 2, rows, cols, width), bf16),) * len(parts),
        in_specs=[in_place],
        out_specs=(whole,) * len(parts),
        scratch_shapes=[pltpu.SemaphoreType.DMA((len(parts),))],
        compiler_params=params(4),
        name="windows",
    )(hbm(mine))


def merge_kernel(hops, mine, low_in, high_in, low_out, high_out):
    half, width = low_in.shape[0], low_in.shape[-1]
    for k, (came, out) in enumerate(((low_in, low_out), (high_in, high_out))):
        column = column_at(hops[k], width)
        for b in range(half):
            own = mine[k * half + b, :, :, column].astype(f32)
            out[b] = (own + came[b].astype(f32)).astype(bf16)


def merged(mine, hops, low_in, high_in):
    return pl.pallas_call(
        functools.partial(merge_kernel, hops),
        out_shape=(pltpu.VMEM(low_in.shape, bf16),) * 2,
        in_specs=[whole] * 3,
        out_specs=(whole, whole),
        compiler_params=params(4),
        name="merge_far_part",
    )(vmem(mine), vmem(low_in), vmem(high_in))


def gather_kernel(table, mine, ups, downs, ups_more, downs_more, out, held):
    row_blocks, rows, cols, _ = mine.shape
    width = ups.shape[-1]
    half = row_blocks // 2
    column = column_at(0, width)
    out[...] = jnp.zeros_like(out)
    for b in range(row_blocks):
        near, far = (downs, ups_more) if b < half else (ups, downs_more)
        total = mine[b, :, :, column].astype(f32) + near[b % half].astype(f32)
        total = total + far[b % half].astype(f32)
        held[b] = total.reshape(rows * cols, width)
        for c in range(cols):
            piece = held[b, pl.ds(c, rows, stride=cols), :]
            out[table[b * cols + c]] = piece.astype(out.dtype)


def gather_pieces(table, mine, arrived, slots):
    half, rows, cols, width = arrived[0].shape
    return pl.pallas_call(
        gather_kernel,
        out_shape=jax.ShapeDtypeStruct((slots, rows, width), bf16),
        in_specs=[scalars] + [whole] * 5,
        out_specs=whole,
        scratch_shapes=[pltpu.VMEM((2 * half, rows * cols, width), f32)],
        compiler_params=params(6),
        name="sum_and_gather",
    )(table, vmem(mine), *[vmem(a) for a in arrived])


def place_kernel(per_step, rows, cols, table, arrived, out, held):
    step = pl.program_id(0)
    for b in range(per_step):
        for c in range(cols):
            slot = table[(step * per_step + b) * cols + c]
            held[b, pl.ds(c, rows, stride=cols), :] = arrived[slot].astype(f32)
        out[b] = held[b].reshape(rows, cols, held.shape[-1]).astype(out.dtype)


def place_pieces(table, arrived, row_blocks, cols):
    slots, rows, width = arrived.shape
    per_step = 4
    return pl.pallas_call(
        functools.partial(place_kernel, per_step, rows, cols),
        out_shape=jax.ShapeDtypeStruct((row_blocks, rows, cols, width), bf16),
        grid=(row_blocks // per_step,),
        in_specs=[scalars, whole],
        out_specs=pl.BlockSpec((per_step, rows, cols, width), lambda i: (i, 0, 0, 0)),
        scratch_shapes=[pltpu.VMEM((per_step, rows * cols, width), f32)],
        compiler_params=params(4),
        name="place_pieces",
    )(table, vmem(arrived))


def early_kernel(slots, count, *refs):
    items = len(slots)
    ins, outs = refs[:items], refs[items : 3 * items]
    roots, lows, in_sem, out_sem = refs[3 * items :]

    def arrival(k):
        return pltpu.make_async_copy(ins[k].at[slots[k]], roots.at[k], in_sem.at[k])

    def departure(k):
        return pltpu.make_async_copy(lows.at[k], outs[2 * k + 1], out_sem.at[k])

    for k in range(items):

        @pl.when(slots[k] < count[0])
        def _():
            arrival(k).start()

    for k in range(items):

        @pl.when(slots[k] < count[0])
        def _():
            arrival(k).wait()
            x = halves(roots[k])
            square = halves(mul3(x, x))
            fourth = halves(mul3(square, square))
            outs[2 * k][...], lows[k] = halves(mul3(x, fourth))
            departure(k).start()

    for k in range(items):

        @pl.when(slots[k] < count[0])
        def _():
            departure(k).wait()


def early(count, *items):
    n = items[0][1].shape[1]
    many = len(items)
    made = pl.pallas_call(
        functools.partial(early_kernel, [t for t, _ in items]),
        out_shape=(pltpu.VMEM((n, n), bf16), stored(n, n, dtype=bf16)) * many,
        in_specs=[scalars] + [in_place] * many,
        out_specs=(whole, in_place) * many,
        scratch_shapes=[
            pltpu.VMEM((many, n, n), f32),
            pltpu.VMEM((many, n, n), bf16),
            pltpu.SemaphoreType.DMA((many,)),
            pltpu.SemaphoreType.DMA((many,)),
        ],
        compiler_params=params(20),
        cost_estimate=pl.CostEstimate(
            flops=many * 9 * 2 * n**3,
            bytes_accessed=many * 8 * n * n,
            transcendentals=0,
        ),
        name="early_products",
    )(count, *[hbm(root) for _, root in items])
    return [made[2 * k : 2 * k + 2] for k in range(many)]


def assembled(pieces, t, block):
    parts, shards, _, rows, width = pieces.shape
    for z in range(parts):
        block[:, z * width : (z + 1) * width] = pieces[z, :, t].reshape(
            shards * rows, width
        )
    return block[...]


def quarter_scale(factor):
    n, tile = factor.shape[0], 128
    on = lax.broadcasted_iota(jnp.int32, (tile, tile), 0)
    on = on == lax.broadcasted_iota(jnp.int32, (tile, tile), 1)
    total = factor[:tile, :tile]
    for d in range(tile, n, tile):
        total = total + factor[d : d + tile, d : d + tile]
    return (0.25 * n) / jnp.sum(jnp.where(on, total, 0.0))


def update_kernel(gain, slots, count, pieces, left, right, xl, xr, *refs):
    fives, refs = refs[: 2 * slots], refs[2 * slots :]
    out, blocks, singles, made, in_sem, out_sem = refs
    parts, shards, _, rows, width = made.shape
    n = parts * width
    olds = (left, xl, right, xr)

    def arrivals(t):
        return [
            pltpu.make_async_copy(old.at[t], singles.at[t, k], in_sem.at[t, k])
            for k, old in enumerate(olds)
        ]

    def departure(h):
        span = pl.ds(h * parts // 2, parts // 2)
        return pltpu.make_async_copy(made.at[span], out.at[span], out_sem.at[h])

    def root(t, k, gram, copies):
        copies[2 * k].wait()
        factor = singles[t, 2 * k] + (gain / decay_rate) * gram
        scale = quarter_scale(factor)
        product = mul(fives[2 * t + k][...], factor.astype(bf16))
        copies[2 * k + 1].wait()
        return (1.25 * singles[t, 2 * k + 1] - scale * product).astype(bf16)

    def work(ts):
        copies = {t: arrivals(t) for t in ts}
        for k in range(4):
            for t in ts:
                copies[t][k].start()
        g, part, side = {}, {}, {}
        for t in ts:
            g[t] = assembled(pieces, t, blocks.at[t])
        grams = {t: (mul_t(g[t], g[t]), t_mul(g[t], g[t])) for t in ts}
        for t in ts:
            side[t] = root(t, 0, grams[t][0], copies[t])
            part[t] = mul(side[t], g[t]).astype(bf16)
        for t in ts:
            side[t] = root(t, 1, grams[t][1], copies[t])
        for h in range(2):
            for t in ts:
                done = mul(part[t], side[t][:, h * n // 2 : (h + 1) * n // 2]).astype(bf16)
                for k in range(parts // 2):
                    made[h * parts // 2 + k, :, t] = done[
                        :, k * width : (k + 1) * width
                    ].reshape(shards, rows, width)
            departure(h).start()

    for live in range(slots + 1):

        @pl.when(count[0] == live)
        def _():
            for t in range(live, slots):
                made[:, :, t] = jnp.zeros_like(made[:, :, t])
            if live:
                work(range(live))
            else:
                departure(0).start()
                departure(1).start()

    departure(0).wait()
    departure(1).wait()


def update_pieces(gain, count, pieces, state, ready):
    slots = pieces.shape[2]
    n = state[0].shape[1]
    fives = [vmem(high) for sides in ready for high, _ in sides]
    return pl.pallas_call(
        functools.partial(update_kernel, gain, slots),
        out_shape=stored(*pieces.shape, dtype=bf16),
        in_specs=[scalars, whole] + [in_place] * 4 + [whole] * len(fives),
        out_specs=in_place,
        scratch_shapes=[
            pltpu.VMEM((slots, n, n), bf16),
            pltpu.VMEM((slots, 4, n, n), f32),
            pltpu.VMEM(pieces.shape, bf16),
            pltpu.SemaphoreType.DMA((slots, 4)),
            pltpu.SemaphoreType.DMA((2,)),
        ],
        compiler_params=params(36),
        name="update_pieces",
    )(count, vmem(pieces), *[hbm(x) for x in state], *fives)


def state_kernel(gain, slots, count, pieces, left, right, xl, xr, *refs):
    ready, refs = refs[: 4 * slots], refs[4 * slots :]
    outs, refs = refs[:4], refs[4:]
    block, fives, made, in_sem, out_sem = refs
    olds = (left, right, xl, xr)

    def arrivals(t):
        sources = [(a.at[t], made.at[t, k]) for k, a in enumerate(olds)]
        sources += [(a, fives.at[t, k]) for k, a in enumerate(ready[4 * t : 4 * t + 4])]
        return [
            pltpu.make_async_copy(a, b, in_sem.at[t, k]) for k, (a, b) in enumerate(sources)
        ]

    def departures(t):
        return [
            pltpu.make_async_copy(made.at[t, k], out.at[t], out_sem.at[t, k])
            for k, out in enumerate(outs)
        ]

    for t in range(slots):
        for copy in arrivals(t)[:4]:
            copy.start()

        @pl.when(t < count[0])
        def _():
            for copy in arrivals(t)[4:]:
                copy.start()

    for t in range(slots):
        for copy in arrivals(t)[:4]:
            copy.wait()

        @pl.when(t < count[0])
        def _():
            g = assembled(pieces, t, block)
            for copy in arrivals(t)[4:]:
                copy.wait()
            for k in range(2):
                gram = t_mul(g, g) if k else mul_t(g, g)
                made[t, k] = decay_rate * made[t, k] + gain * gram
                departures(t)[k].start()
                factor = made[t, k]
                product = mul3((fives[t, 2 * k], fives[t, 2 * k + 1]), halves(factor))
                made[t, 2 + k] = 1.25 * made[t, 2 + k] - quarter_scale(factor) * product
                departures(t)[2 + k].start()

        @pl.when(t >= count[0])
        def _():
            for copy in departures(t):
                copy.start()

    for t in range(slots):
        for copy in departures(t):
            copy.wait()


def new_state(gain, count, pieces, state, ready):
    slots, n, _ = state[0].shape
    inputs = [hbm(x) for sides in ready for made in sides for x in made]
    return pl.pallas_call(
        functools.partial(state_kernel, gain, slots),
        out_shape=(stored(slots, n, n),) * 4,
        in_specs=[scalars, whole] + [in_place] * (4 + len(inputs)),
        out_specs=(in_place,) * 4,
        scratch_shapes=[
            pltpu.VMEM((n, n), bf16),
            pltpu.VMEM((slots, 4, n, n), bf16),
            pltpu.VMEM((slots, 4, n, n), f32),
            pltpu.SemaphoreType.DMA((slots, 8)),
            pltpu.SemaphoreType.DMA((slots, 4)),
        ],
        compiler_params=params(36),
        cost_estimate=pl.CostEstimate(
            flops=slots * 8 * 2 * n**3,
            bytes_accessed=slots * 36 * n * n,
            transcendentals=0,
        ),
        name="new_state",
    )(count, vmem(pieces), *[hbm(x) for x in state], *inputs)


def body(
    gradients, owner_list, row_offset, col_offset, left_factor, right_factor, left_root, right_root
):
    replicas = lax.axis_size("dp")
    shards = lax.axis_size("shard")
    slots, n, _ = left_factor.shape
    _, row_blocks, rows, cols, _ = gradients.shape
    width = n // replicas
    gain = (1.0 - decay_rate) / n
    mine = gradients[0]

    def hop(x, step):
        return lax.ppermute(x, "dp", [(i, (i + step) % replicas) for i in range(replicas)])

    half = row_blocks // 2
    far = lax.rem(lax.axis_index("dp") + 2, replicas) * width
    far = lax.dynamic_slice_in_dim(mine, far, width, axis=3)
    far_low, far_high = far[:half], far[half:]
    far_low, far_high = hop(far_low, 1), hop(far_high, -1)
    near_high, near_low = windows(mine, width, ((half, 1), (0, 3)))
    near_high, near_low = hop(near_high, 1), hop(near_low, -1)

    entries = jnp.arange(owner_list.shape[0], dtype=jnp.int32)
    same = owner_list[None, :] == owner_list[:, None]
    earlier = jnp.sum(same & (entries[None, :] < entries[:, None]), axis=1)
    slot_of = owner_list * slots + earlier.astype(jnp.int32)
    block_of = row_offset // n * cols + col_offset // n
    table = jnp.sum(
        jnp.where(block_of[None, :] == entries[:, None], slot_of[None, :], 0), axis=1
    ).astype(jnp.int32)
    owner = lax.axis_index(("dp", "shard"))
    count = jnp.sum((owner_list == owner).astype(jnp.int32)).reshape(1)

    far_low, far_high = merged(mine, (1, 3), far_low, far_high)
    far_low, far_high = hop(far_low, 1), hop(far_high, -1)
    (first,) = early(count, (0, left_root))
    arrived = (near_high, near_low, far_low, far_high)
    arrived, first = lax.optimization_barrier((arrived, first))

    all_slots = replicas * shards * slots
    outgoing = gather_pieces(table, mine, arrived, all_slots)
    incoming = lax.all_to_all(outgoing, ("dp", "shard"), split_axis=0, concat_axis=0, tiled=True)
    rest = [(t, side) for t in range(slots) for side in (left_root, right_root)][1:]
    ready = [first, *early(count, *rest)]
    incoming, ready = lax.optimization_barrier((incoming, ready))
    ready = [ready[2 * t : 2 * t + 2] for t in range(slots)]
    pieces = incoming.reshape(replicas, shards, slots, rows, width)
    state = (left_factor, right_factor, left_root, right_root)
    outbound = update_pieces(gain, count, pieces, state, ready)
    returned = lax.all_to_all(
        outbound.reshape(all_slots, rows, width),
        ("dp", "shard"), split_axis=0, concat_axis=0, tiled=True,
    )
    new_left, new_right, new_xl, new_xr = new_state(gain, count, pieces, state, ready)
    update = place_pieces(table, returned, row_blocks, cols)
    return update, new_left, new_right, new_xl, new_xr


def solution(mesh):
    slots = P(("dp", "shard"), None, None)
    in_specs = (P("dp", None, "shard", None, None), P(), P(), P(), slots, slots, slots, slots)
    out_specs = (P(None, "shard", None, "dp"), slots, slots, slots, slots)
    return jax.shard_map(body, mesh=mesh, in_specs=in_specs, out_specs=out_specs, check_vma=False)
```

time: 90.8 us -> 89.8 us (0.989)
  Pallas kernels: 18.5 us -> 15.8 us
  local copies, waits for them, and re-layouts: 0.04 us -> 2.05 us
  starting transfers between devices: 31.4 us -> 30.4 us
    slice x0 -> x1, local copies, waits for them, and re-layouts: none -> 2.01 us  [body(): far_low, far_high = (far[:half], far[half:])]
    pallas_call x2 -> x1, Pallas kernels: 3.76 us -> 1.75 us  [windows(): pl.pallas_call(functools.partial(window_kernel, parts), out_shape=(pltpu....]
  transfers between devices with their start and end apart: 8 -> 8, of which waited for: 5 -> 5; matrix products, arithmetic and copies ran while one was open for 1% -> 1% of each run, Pallas kernels for 12% -> 11%
where the time goes in v4:
time: 89.8 us; the launch traced here: 89.4 us
  waiting for transfers between devices  39.5 us (44%)
  starting transfers between devices  30.4 us (34%)
  Pallas kernels  15.8 us (18%)
  local copies, waits for them, and re-layouts  2.05 us (2%)
  other arithmetic  0.98 us (1%)
    all_to_all x1, waiting for transfers between devices, body(): lax.all_to_all(outgoing, ('dp', 'shard'), split_axis=0, concat_axis=0, ti...  18.6 us
    all_to_all x1, waiting for transfers between devices, body(): lax.all_to_all(outbound.reshape(all_slots, rows, width), ('dp', 'shard'),...  12.5 us
    all_to_all x1, starting transfers between devices, body(): lax.all_to_all(outgoing, ('dp', 'shard'), split_axis=0, concat_axis=0, ti...  10.1 us
    all_to_all x1, starting transfers between devices, body(): lax.all_to_all(outbound.reshape(all_slots, rows, width), ('dp', 'shard'),...  10.1 us
    ppermute x6, starting transfers between devices, hop(): lax.ppermute(x, 'dp', [(i, (i + step) % replicas) for i in range(replicas)])  10.1 us
    ppermute x6, waiting for transfers between devices, hop(): lax.ppermute(x, 'dp', [(i, (i + step) % replicas) for i in range(replicas)])  8.39 us
    pallas_call x1, Pallas kernels, new_state(): pl.pallas_call(functools.partial(state_kernel, gain, slots), out_shape=(s...  6.87 us
    pallas_call x1, Pallas kernels, gather_pieces(): pl.pallas_call(gather_kernel, out_shape=jax.ShapeDtypeStruct((slots, rows...  2.12 us
  transfers between devices with their start and end apart: 8, of which 5 were waited for; matrix products, arithmetic and copies ran while one was open for 1% of the time, Pallas kernels for 11%

profile of v4, /device:TPU:1, one launch (start us, length us, event | category | flops | bytes accessed | tf_op | source)
XLA Modules:
  0.0 89.4 jit_solution(11660333003940614536)
XLA Ops:
  0.6 0.0 copy-start
  0.6 0.0 copy-start.5
  0.7 0.0 copy-start.7
  0.7 0.0 copy-start.6
  0.7 2.0 %dynamic-slice_bitcast_fusion = (bf16[4,16,16,128]{3,2,1,0:T(8,128)(2,1)}, bf16[4,16,16,128]{3,2,1,0:T(8,128)(2,1)}) fusion(bf16[1,8,16,16,512]{4,3,2,1,0:T(8,128)(2,1)} %param.8, s32[]{:T(128)S(6)} %add.22, s32[]{:T(128)S(6)} %select_n.18), kind=kLoop, calls=%fused_computation | loop fusion | bytes 1048584 | tf_op jit(solution)/shard_map/slice | solution.py:425
  2.7 2.5 %collective-permute-start.2 = (bf16[4,16,16,128]{3,2,1,0:T(8,128)(2,1)}, bf16[4,16,16,128]{3,2,1,0:T(8,128)(2,1)S(1)}, u32[]{:S(2)}, u32[]{:S(2)}) collective-permute-start(bf16[4,16,16,128]{3,2,1,0:T(8,128)(2,1)} %get-tuple-element.68), channel_id=1, source_target_pairs={{0,32},{32,64},{64,96},{96,0},{1,33},{33,65},{65,97},{97,1},{2,34}... | collective-permute-start | bytes 786440 | tf_op jit(solution)/shard_map/ppermute | solution.py:420
  5.2 2.1 %collective-permute-start.3 = (bf16[4,16,16,128]{3,2,1,0:T(8,128)(2,1)}, bf16[4,16,16,128]{3,2,1,0:T(8,128)(2,1)S(1)}, u32[]{:S(2)}, u32[]{:S(2)}) collective-permute-start(bf16[4,16,16,128]{3,2,1,0:T(8,128)(2,1)} %get-tuple-element.67), channel_id=1, source_target_pairs={{0,96},{32,0},{64,32},{96,64},{1,97},{33,1},{65,33},{97,65},{2,98}... | collective-permute-start | bytes 786440 | tf_op jit(solution)/shard_map/ppermute | solution.py:420
  7.3 1.8 %windows.1 = (bf16[4,16,16,128]{3,2,1,0:T(8,128)(2,1)}, bf16[4,16,16,128]{3,2,1,0:T(8,128)(2,1)S(1)}) custom-call(bf16[8,16,16,512]{3,2,1,0:T(8,128)(2,1)} %bitcast.8), custom_call_target="tpu_custom_call" | custom-call | tf_op jit(solution)/shard_map/windows/pallas_call | solution.py:79
  9.0 0.1 collective-permute-start
  9.1 2.7 %collective-permute-start.1 = (bf16[4,16,16,128]{3,2,1,0:T(8,128)(2,1)S(1)}, bf16[4,16,16,128]{3,2,1,0:T(8,128)(2,1)S(1)}, u32[]{:S(2)}, u32[]{:S(2)}) collective-permute-start(bf16[4,16,16,128]{3,2,1,0:T(8,128)(2,1)S(1)} %get-tuple-element.37), channel_id=1, source_target_pairs={{0,96},{32,0},{64,32},{96,64},{1,97},{33,1},{65,33},{97,65},{2,98}... | collective-permute-start | bytes 786440 | tf_op jit(solution)/shard_map/ppermute | solution.py:420
  11.8 0.0 copy-done.5
  11.8 0.2 convert_reduce_fusion
  12.0 0.7 fusion.1
  12.7 0.0 copy-done.7
  12.7 0.0 copy-done.6
  12.7 0.8 collective-permute-done.2.low_in
  13.5 0.0 collective-permute-done.3.high_in
  13.5 0.0 copy-done
  13.5 0.1 merge_far_part.1
  13.7 0.4 collective-permute-start.4
  14.1 2.3 %collective-permute-start.5 = (bf16[4,16,16,128]{3,2,1,0:T(8,128)(2,1)S(1)}, bf16[4,16,16,128]{3,2,1,0:T(8,128)(2,1)S(1)}, u32[]{:S(2)}, u32[]{:S(2)}) collective-permute-start(bf16[4,16,16,128]{3,2,1,0:T(8,128)(2,1)S(1)} %get-tuple-element.39), channel_id=1, source_target_pairs={{0,96},{32,0},{64,32},{96,64},{1,97},{33,1},{65,33},{97,65},{2,98}... | collective-permute-start | bytes 786440 | tf_op jit(solution)/shard_map/ppermute | solution.py:420
  16.4 0.1 select_reduce_fusion.table
  16.5 0.7 early_products.2
  17.2 0.0 copy-start.1
  17.2 1.9 %collective-permute-done.ups = bf16[4,16,16,128]{3,2,1,0:T(8,128)(2,1)S(1)} collective-permute-done((bf16[4,16,16,128]{3,2,1,0:T(8,128)(2,1)}, bf16[4,16,16,128]{3,2,1,0:T(8,128)(2,1)S(1)}, u32[]{:S(2)}, u32[]{:S(2)}) %collective-permute-start) | collective-permute-done | bytes 262176 | tf_op jit(solution)/shard_map/ppermute | solution.py:420
  19.1 0.0 collective-permute-done.1.downs
  19.1 5.6 %collective-permute-done.4.ups_more = bf16[4,16,16,128]{3,2,1,0:T(8,128)(2,1)S(1)} collective-permute-done((bf16[4,16,16,128]{3,2,1,0:T(8,128)(2,1)S(1)}, bf16[4,16,16,128]{3,2,1,0:T(8,128)(2,1)S(1)}, u32[]{:S(2)}, u32[]{:S(2)}) %collective-permute-start.4) | collective-permute-done | bytes 262176 | tf_op jit(solution)/shard_map/ppermute | solution.py:420
  24.8 0.0 collective-permute-done.5.downs_more
  24.8 2.1 %sum_and_gather.1 = bf16[256,16,128]{2,1,0:T(8,128)(2,1)} custom-call(s32[128]{0:T(128)S(1)} %select_reduce_fusion.table, bf16[8,16,16,512]{3,2,1,0:T(8,128)(2,1)S(1)} %bitcast.10, bf16[4,16,16,128]{3,2,1,0:T(8,128)(2,1)S(1)} %collective-permute-done.ups, bf16[4,16,16,128]{3,2,1,0:T(8,128)(2,1)S(1)} %collective-permute-done.1.downs, ...), custom_call_target="tpu_custom_call" | custom-call | tf_op jit(solution)/shard_map/sum_and_gather/pallas_call | solution.py:128
  26.9 10.1 %all-to-all-start = ((bf16[256,16,128]{2,1,0:T(8,128)(2,1)}), bf16[256,16,128]{2,1,0:T(8,128)(2,1)S(1)}, u32[]{:S(2)}, u32[]{:S(2)}) async-start(bf16[256,16,128]{2,1,0:T(8,128)(2,1)} %sum_and_gather.1), calls=%async_computation | async-start | bytes 2097152 | tf_op jit(solution)/shard_map/all_to_all | solution.py:449
  37.0 0.7 early_products.3
  37.8 0.0 copy-start.2
  37.8 0.0 copy-start.3
  37.8 0.0 copy-start.4
  37.8 18.6 %all-to-all-done = bf16[256,16,128]{2,1,0:T(8,128)(2,1)S(1)} async-done(((bf16[256,16,128]{2,1,0:T(8,128)(2,1)}), bf16[256,16,128]{2,1,0:T(8,128)(2,1)S(1)}, u32[]{:S(2)}, u32[]{:S(2)}) %all-to-all-start) | async-done | bytes 1048608 | tf_op jit(solution)/shard_map/all_to_all | solution.py:449
  56.4 0.0 copy-done.1
  56.4 1.8 %update_pieces.1 = bf16[4,32,2,16,128]{4,3,2,1,0:T(8,128)(2,1)} custom-call(s32[1]{0:T(128)} %bitcast.count, bf16[4,32,2,16,128]{4,3,2,1,0:T(8,128)(2,1)S(1)} %bitcast.11, f32[2,512,512]{2,1,0:T(8,128)} %left.3, f32[2,512,512]{2,1,0:T(8,128)} %right.3, f32[2,512,512]{2,1,0:T(8,128)} %xl.3, f32[2,512,512]{2,1,0:T(8,128)} %xr.3, ...), custom_call_target="tpu_custom_call" | custom-call | tf_op jit(solution)/shard_map/update_pieces/pallas_call | solution.py:310
  58.2 0.0 copy-done.2
  58.2 0.0 copy-done.3
  58.2 0.0 copy-done.4
  58.2 10.1 %all-to-all-start.1 = ((bf16[256,16,128]{2,1,0:T(8,128)(2,1)}), bf16[256,16,128]{2,1,0:T(8,128)(2,1)S(1)}, u32[]{:S(2)}, u32[]{:S(2)}) async-start(bf16[256,16,128]{2,1,0:T(8,128)(2,1)} %bitcast.13), calls=%async_computation.1 | async-start | bytes 2097152 | tf_op jit(solution)/shard_map/all_to_all | solution.py:457
  68.4 6.9 %new_state.1 = (f32[2,512,512]{2,1,0:T(8,128)}, f32[2,512,512]{2,1,0:T(8,128)}, f32[2,512,512]{2,1,0:T(8,128)}, f32[2,512,512]{2,1,0:T(8,128)}) custom-call(s32[1]{0:T(128)} %bitcast.count, bf16[4,32,2,16,128]{4,3,2,1,0:T(8,128)(2,1)S(1)} %bitcast.12, f32[2,512,512]{2,1,0:T(8,128)} %left.3, f32[2,512,512]{2,1,0:T(8,128)} %right.3, f32[2,512,512]{2,1,0:T(8,128)} %xl.3, ...), custom_call_target="tpu_custom_call" | custom-call | flops 4294967296 | bytes 18874368 | tf_op jit(solution)/shard_map/new_state/pallas_call | solution.py:386
  75.3 12.5 %all-to-all-done.1.arrived = bf16[256,16,128]{2,1,0:T(8,128)(2,1)S(1)} async-done(((bf16[256,16,128]{2,1,0:T(8,128)(2,1)}), bf16[256,16,128]{2,1,0:T(8,128)(2,1)S(1)}, u32[]{:S(2)}, u32[]{:S(2)}) %all-to-all-start.1) | async-done | bytes 1048608 | tf_op jit(solution)/shard_map/all_to_all | solution.py:457
  87.7 1.7 %place_pieces.1 = bf16[8,16,16,128]{3,2,1,0:T(8,128)(2,1)} custom-call(s32[128]{0:T(128)S(1)} %select_reduce_fusion.table, bf16[256,16,128]{2,1,0:T(8,128)(2,1)S(1)} %all-to-all-done.1.arrived), custom_call_target="tpu_custom_call" | custom-call | tf_op jit(solution)/shard_map/place_pieces/pallas_call | solution.py:151
  (1 shorter events, 0.0 us)
Async XLA Ops:
  0.6 12.9 %copy-start = (bf16[1,8,16,16,512]{4,3,2,1,0:T(8,128)(2,1)S(1)}, bf16[1,8,16,16,512]{4,3,2,1,0:T(8,128)(2,1)}, u32[]{:S(2)}) copy-start(bf16[1,8,16,16,512]{4,3,2,1,0:T(8,128)(2,1)} %param.8) | copy-start | bytes 6291460
  0.6 11.2 %copy-start.5 = (s32[128]{0:T(128)S(1)}, s32[128]{0:T(128)}, u32[]{:S(2)}) copy-start(s32[128]{0:T(128)} %param.9) | copy-start | bytes 1540
  0.7 12.0 %copy-start.7 = (s32[128]{0:T(128)S(1)}, s32[128]{0:T(128)}, u32[]{:S(2)}) copy-start(s32[128]{0:T(128)} %param.10) | copy-start | bytes 1540
  0.7 12.0 %copy-start.6 = (s32[128]{0:T(128)S(1)}, s32[128]{0:T(128)}, u32[]{:S(2)}) copy-start(s32[128]{0:T(128)} %param.11) | copy-start | bytes 1540
  2.7 10.8 %collective-permute-start.2 = (bf16[4,16,16,128]{3,2,1,0:T(8,128)(2,1)}, bf16[4,16,16,128]{3,2,1,0:T(8,128)(2,1)S(1)}, u32[]{:S(2)}, u32[]{:S(2)}) collective-permute-start(bf16[4,16,16,128]{3,2,1,0:T(8,128)(2,1)} %get-tuple-element.68), channel_id=1, source_target_pairs={{0,32},{32,64},{64,96},{96,0},{1,33},{33,65},{65,97},{97,1},{2,34}... | collective-permute-start | bytes 786440 | tf_op jit(solution)/shard_map/ppermute | solution.py:420
  5.2 8.4 %collective-permute-start.3 = (bf16[4,16,16,128]{3,2,1,0:T(8,128)(2,1)}, bf16[4,16,16,128]{3,2,1,0:T(8,128)(2,1)S(1)}, u32[]{:S(2)}, u32[]{:S(2)}) collective-permute-start(bf16[4,16,16,128]{3,2,1,0:T(8,128)(2,1)} %get-tuple-element.67), channel_id=1, source_target_pairs={{0,96},{32,0},{64,32},{96,64},{1,97},{33,1},{65,33},{97,65},{2,98}... | collective-permute-start | bytes 786440 | tf_op jit(solution)/shard_map/ppermute | solution.py:420
  9.0 10.1 %collective-permute-start = (bf16[4,16,16,128]{3,2,1,0:T(8,128)(2,1)}, bf16[4,16,16,128]{3,2,1,0:T(8,128)(2,1)S(1)}, u32[]{:S(2)}, u32[]{:S(2)}) collective-permute-start(bf16[4,16,16,128]{3,2,1,0:T(8,128)(2,1)} %get-tuple-element.36), channel_id=1, source_target_pairs={{0,32},{32,64},{64,96},{96,0},{1,33},{33,65},{65,97},{97,1},{2,34}... | collective-permute-start | bytes 786440 | tf_op jit(solution)/shard_map/ppermute | solution.py:420
  9.1 10.0 %collective-permute-start.1 = (bf16[4,16,16,128]{3,2,1,0:T(8,128)(2,1)S(1)}, bf16[4,16,16,128]{3,2,1,0:T(8,128)(2,1)S(1)}, u32[]{:S(2)}, u32[]{:S(2)}) collective-permute-start(bf16[4,16,16,128]{3,2,1,0:T(8,128)(2,1)S(1)} %get-tuple-element.37), channel_id=1, source_target_pairs={{0,96},{32,0},{64,32},{96,64},{1,97},{33,1},{65,33},{97,65},{2,98}... | collective-permute-start | bytes 786440 | tf_op jit(solution)/shard_map/ppermute | solution.py:420
  13.7 11.1 %collective-permute-start.4 = (bf16[4,16,16,128]{3,2,1,0:T(8,128)(2,1)S(1)}, bf16[4,16,16,128]{3,2,1,0:T(8,128)(2,1)S(1)}, u32[]{:S(2)}, u32[]{:S(2)}) collective-permute-start(bf16[4,16,16,128]{3,2,1,0:T(8,128)(2,1)S(1)} %get-tuple-element.38), channel_id=1, source_target_pairs={{0,32},{32,64},{64,96},{96,0},{1,33},{33,65},{65,97},{97,1},{2,34}... | collective-permute-start | bytes 786440 | tf_op jit(solution)/shard_map/ppermute | solution.py:420
  14.1 10.7 %collective-permute-start.5 = (bf16[4,16,16,128]{3,2,1,0:T(8,128)(2,1)S(1)}, bf16[4,16,16,128]{3,2,1,0:T(8,128)(2,1)S(1)}, u32[]{:S(2)}, u32[]{:S(2)}) collective-permute-start(bf16[4,16,16,128]{3,2,1,0:T(8,128)(2,1)S(1)} %get-tuple-element.39), channel_id=1, source_target_pairs={{0,96},{32,0},{64,32},{96,64},{1,97},{33,1},{65,33},{97,65},{2,98}... | collective-permute-start | bytes 786440 | tf_op jit(solution)/shard_map/ppermute | solution.py:420
  17.2 39.2 %copy-start.1 = (bf16[512,512]{1,0:T(8,128)(2,1)}, bf16[512,512]{1,0:T(8,128)(2,1)S(1)}, u32[]{:S(2)}) copy-start(bf16[512,512]{1,0:T(8,128)(2,1)S(1)} %get-tuple-element.55.refs_0_) | copy-start | bytes 1572868
  26.9 29.5 %all-to-all-start = ((bf16[256,16,128]{2,1,0:T(8,128)(2,1)}), bf16[256,16,128]{2,1,0:T(8,128)(2,1)S(1)}, u32[]{:S(2)}, u32[]{:S(2)}) async-start(bf16[256,16,128]{2,1,0:T(8,128)(2,1)} %sum_and_gather.1), calls=%async_computation | async-start | bytes 2097152 | tf_op jit(solution)/shard_map/all_to_all | solution.py:449
  37.8 20.5 %copy-start.2 = (bf16[512,512]{1,0:T(8,128)(2,1)}, bf16[512,512]{1,0:T(8,128)(2,1)S(1)}, u32[]{:S(2)}) copy-start(bf16[512,512]{1,0:T(8,128)(2,1)S(1)} %get-tuple-element.56.refs_1_.refs_2_) | copy-start | bytes 1572868
  37.8 20.5 %copy-start.3 = (bf16[512,512]{1,0:T(8,128)(2,1)}, bf16[512,512]{1,0:T(8,128)(2,1)S(1)}, u32[]{:S(2)}) copy-start(bf16[512,512]{1,0:T(8,128)(2,1)S(1)} %get-tuple-element.57.refs_2_.refs_4_) | copy-start | bytes 1572868
  37.8 20.5 %copy-start.4 = (bf16[512,512]{1,0:T(8,128)(2,1)}, bf16[512,512]{1,0:T(8,128)(2,1)S(1)}, u32[]{:S(2)}) copy-start(bf16[512,512]{1,0:T(8,128)(2,1)S(1)} %get-tuple-element.58.refs_3_.refs_6_) | copy-start | bytes 1572868
  58.2 29.5 %all-to-all-start.1 = ((bf16[256,16,128]{2,1,0:T(8,128)(2,1)}), bf16[256,16,128]{2,1,0:T(8,128)(2,1)S(1)}, u32[]{:S(2)}, u32[]{:S(2)}) async-start(bf16[256,16,128]{2,1,0:T(8,128)(2,1)} %bitcast.13), calls=%async_computation.1 | async-start | bytes 2097152 | tf_op jit(solution)/shard_map/all_to_all | solution.py:457

commit v5 on v4

--- a/solution.py
+++ b/solution.py
@@ -87,24 +87,22 @@
     )(hbm(mine))
 
 
-def merge_kernel(hops, mine, low_in, high_in, low_out, high_out):
-    half, width = low_in.shape[0], low_in.shape[-1]
-    for k, (came, out) in enumerate(((low_in, low_out), (high_in, high_out))):
-        column = column_at(hops[k], width)
-        for b in range(half):
-            own = mine[k * half + b, :, :, column].astype(f32)
-            out[b] = (own + came[b].astype(f32)).astype(bf16)
-
-
-def merged(mine, hops, low_in, high_in):
-    return pl.pallas_call(
-        functools.partial(merge_kernel, hops),
-        out_shape=(pltpu.VMEM(low_in.shape, bf16),) * 2,
-        in_specs=[whole] * 3,
-        out_specs=(whole, whole),
+def merge_kernel(low, hop, mine, came, out):
+    column = column_at(hop, out.shape[-1])
+    for b in range(out.shape[0]):
+        own = mine[low + b, :, :, column].astype(f32)
+        out[b] = (own + came[b].astype(f32)).astype(bf16)
+
+
+def merged(mine, low, hop, came):
+    return pl.pallas_call(
+        functools.partial(merge_kernel, low, hop),
+        out_shape=pltpu.VMEM(came.shape, bf16),
+        in_specs=[whole] * 2,
+        out_specs=whole,
         compiler_params=params(4),
         name="merge_far_part",
-    )(vmem(mine), vmem(low_in), vmem(high_in))
+    )(vmem(mine), vmem(came))
 
 
 def gather_kernel(table, mine, ups, downs, ups_more, downs_more, out, held):
@@ -162,62 +160,81 @@
 
 def early_kernel(slots, count, *refs):
     items = len(slots)
-    ins, outs = refs[:items], refs[items : 3 * items]
-    roots, lows, in_sem, out_sem = refs[3 * items :]
-
-    def arrival(k):
-        return pltpu.make_async_copy(ins[k].at[slots[k]], roots.at[k], in_sem.at[k])
-
-    def departure(k):
-        return pltpu.make_async_copy(lows.at[k], outs[2 * k + 1], out_sem.at[k])
+    ins, outs = refs[: 2 * items], refs[2 * items : 5 * items]
+    roots, factors, lows, short, in_sem, out_sem = refs[5 * items :]
+
+    def arrivals(k):
+        return [
+            pltpu.make_async_copy(ins[2 * k + i].at[slots[k]], held.at[k], in_sem.at[k, i])
+            for i, held in enumerate((roots, factors))
+        ]
+
+    def departures(k):
+        return [
+            pltpu.make_async_copy(held.at[k], outs[3 * k + 1 + i], out_sem.at[k, i])
+            for i, held in enumerate((lows, short))
+        ]
+
+    for i in range(2):
+        for k in range(items):
+
+            @pl.when(slots[k] < count[0])
+            def _():
+                arrivals(k)[i].start()
 
     for k in range(items):
 
         @pl.when(slots[k] < count[0])
         def _():
-            arrival(k).start()
-
-    for k in range(items):
-
-        @pl.when(slots[k] < count[0])
-        def _():
-            arrival(k).wait()
+            (root_in, factor_in), going = arrivals(k), departures(k)
+            root_in.wait()
             x = halves(roots[k])
             square = halves(mul3(x, x))
             fourth = halves(mul3(square, square))
-            outs[2 * k][...], lows[k] = halves(mul3(x, fourth))
-            departure(k).start()
+            factor_in.wait()
+            short[k] = factors[k].astype(bf16)
+            going[1].start()
+            outs[3 * k][...], lows[k] = halves(mul3(x, fourth))
+            going[0].start()
 
     for k in range(items):
 
         @pl.when(slots[k] < count[0])
         def _():
-            departure(k).wait()
+            for copy in departures(k):
+                copy.wait()
 
 
 def early(count, *items):
     n = items[0][1].shape[1]
     many = len(items)
     made = pl.pallas_call(
-        functools.partial(early_kernel, [t for t, _ in items]),
-        out_shape=(pltpu.VMEM((n, n), bf16), stored(n, n, dtype=bf16)) * many,
-        in_specs=[scalars] + [in_place] * many,
-        out_specs=(whole, in_place) * many,
+        functools.partial(early_kernel, [t for t, _, _ in items]),
+        out_shape=(
+            pltpu.VMEM((n, n), bf16),
+            stored(n, n, dtype=bf16),
+            stored(n, n, dtype=bf16),
+        )
+        * many,
+        in_specs=[scalars] + [in_place] * (2 * many),
+        out_specs=(whole, in_place, in_place) * many,
         scratch_shapes=[
             pltpu.VMEM((many, n, n), f32),
+            pltpu.VMEM((many, n, n), f32),
             pltpu.VMEM((many, n, n), bf16),
-            pltpu.SemaphoreType.DMA((many,)),
-            pltpu.SemaphoreType.DMA((many,)),
+            pltpu.VMEM((many, n, n), bf16),
+            pltpu.SemaphoreType.DMA((many, 2)),
+            pltpu.SemaphoreType.DMA((many, 2)),
         ],
-        compiler_params=params(20),
+        compiler_params=params(24),
         cost_estimate=pl.CostEstimate(
             flops=many * 9 * 2 * n**3,
-            bytes_accessed=many * 8 * n * n,
+            bytes_accessed=many * 12 * n * n,
             transcendentals=0,
         ),
         name="early_products",
-    )(count, *[hbm(root) for _, root in items])
-    return [made[2 * k : 2 * k + 2] for k in range(many)]
+    )(count, *[hbm(x) for _, *pair in items for x in pair])
+    return [made[3 * k : 3 * k + 3] for k in range(many)]
 
 
 def assembled(pieces, t, block):
@@ -239,18 +256,23 @@
     return (0.25 * n) / jnp.sum(jnp.where(on, total, 0.0))
 
 
-def update_kernel(gain, slots, count, pieces, left, right, xl, xr, *refs):
-    fives, refs = refs[: 2 * slots], refs[2 * slots :]
-    out, blocks, singles, made, in_sem, out_sem = refs
+def update_kernel(gain, slots, count, pieces, xl, xr, *refs):
+    ready, refs = refs[: 4 * slots], refs[4 * slots :]
+    out, blocks, roots, factors, made, in_sem, out_sem = refs
     parts, shards, _, rows, width = made.shape
     n = parts * width
-    olds = (left, xl, right, xr)
+    roots_in = (xl, xr)
 
     def arrivals(t):
-        return [
-            pltpu.make_async_copy(old.at[t], singles.at[t, k], in_sem.at[t, k])
-            for k, old in enumerate(olds)
-        ]
+        copies = []
+        for k in range(2):
+            sources = (
+                (ready[4 * t + 2 * k + 1], factors.at[t, k]),
+                (roots_in[k].at[t], roots.at[t, k]),
+            )
+            for a, b in sources:
+                copies.append(pltpu.make_async_copy(a, b, in_sem.at[t, len(copies)]))
+        return copies
 
     def departure(h):
         span = pl.ds(h * parts // 2, parts // 2)
@@ -258,11 +280,11 @@
 
     def root(t, k, gram, copies):
         copies[2 * k].wait()
-        factor = singles[t, 2 * k] + (gain / decay_rate) * gram
+        factor = factors[t, k].astype(f32) + (gain / decay_rate) * gram
         scale = quarter_scale(factor)
-        product = mul(fives[2 * t + k][...], factor.astype(bf16))
+        product = mul(ready[4 * t + 2 * k][...], factor.astype(bf16))
         copies[2 * k + 1].wait()
-        return (1.25 * singles[t, 2 * k + 1] - scale * product).astype(bf16)
+        return (1.25 * roots[t, k] - scale * product).astype(bf16)
 
     def work(ts):
         copies = {t: arrivals(t) for t in ts}
@@ -303,25 +325,29 @@
     departure(1).wait()
 
 
-def update_pieces(gain, count, pieces, state, ready):
+def update_pieces(gain, count, pieces, xl, xr, ready):
     slots = pieces.shape[2]
-    n = state[0].shape[1]
-    fives = [vmem(high) for sides in ready for high, _ in sides]
+    n = xl.shape[1]
+    inputs = []
+    for sides in ready:
+        for high, _, factor in sides:
+            inputs += [vmem(high), hbm(factor)]
     return pl.pallas_call(
         functools.partial(update_kernel, gain, slots),
         out_shape=stored(*pieces.shape, dtype=bf16),
-        in_specs=[scalars, whole] + [in_place] * 4 + [whole] * len(fives),
+        in_specs=[scalars, whole] + [in_place] * 2 + [whole, in_place] * (2 * slots),
         out_specs=in_place,
         scratch_shapes=[
             pltpu.VMEM((slots, n, n), bf16),
-            pltpu.VMEM((slots, 4, n, n), f32),
+            pltpu.VMEM((slots, 2, n, n), f32),
+            pltpu.VMEM((slots, 2, n, n), bf16),
             pltpu.VMEM(pieces.shape, bf16),
             pltpu.SemaphoreType.DMA((slots, 4)),
             pltpu.SemaphoreType.DMA((2,)),
         ],
         compiler_params=params(36),
         name="update_pieces",
-    )(count, vmem(pieces), *[hbm(x) for x in state], *fives)
+    )(count, vmem(pieces), hbm(xl), hbm(xr), *inputs)
 
 
 def state_kernel(gain, slots, count, pieces, left, right, xl, xr, *refs):
@@ -382,7 +408,7 @@
 
 def new_state(gain, count, pieces, state, ready):
     slots, n, _ = state[0].shape
-    inputs = [hbm(x) for sides in ready for made in sides for x in made]
+    inputs = [hbm(x) for sides in ready for made in sides for x in made[:2]]
     return pl.pallas_call(
         functools.partial(state_kernel, gain, slots),
         out_shape=(stored(slots, n, n),) * 4,
@@ -438,22 +464,23 @@
     owner = lax.axis_index(("dp", "shard"))
     count = jnp.sum((owner_list == owner).astype(jnp.int32)).reshape(1)
 
-    far_low, far_high = merged(mine, (1, 3), far_low, far_high)
-    far_low, far_high = hop(far_low, 1), hop(far_high, -1)
-    (first,) = early(count, (0, left_root))
+    far_low = hop(merged(mine, 0, 1, far_low), 1)
+    far_high = hop(merged(mine, half, 3, far_high), -1)
+    (first,) = early(count, (0, left_root, left_factor))
     arrived = (near_high, near_low, far_low, far_high)
     arrived, first = lax.optimization_barrier((arrived, first))
 
     all_slots = replicas * shards * slots
     outgoing = gather_pieces(table, mine, arrived, all_slots)
     incoming = lax.all_to_all(outgoing, ("dp", "shard"), split_axis=0, concat_axis=0, tiled=True)
-    rest = [(t, side) for t in range(slots) for side in (left_root, right_root)][1:]
+    sides = ((left_root, left_factor), (right_root, right_factor))
+    rest = [(t, *side) for t in range(slots) for side in sides][1:]
     ready = [first, *early(count, *rest)]
     incoming, ready = lax.optimization_barrier((incoming, ready))
     ready = [ready[2 * t : 2 * t + 2] for t in range(slots)]
     pieces = incoming.reshape(replicas, shards, slots, rows, width)
     state = (left_factor, right_factor, left_root, right_root)
-    outbound = update_pieces(gain, count, pieces, state, ready)
+    outbound = update_pieces(gain, count, pieces, left_root, right_root, ready)
     returned = lax.all_to_all(
         outbound.reshape(all_slots, rows, width),
         ("dp", "shard"), split_axis=0, concat_axis=0, tiled=True,

time: 89.8 us -> 89.5 us (level)
  starting transfers between devices: 30.4 us -> 28.5 us
  waiting for transfers between devices: 39.5 us -> 41 us
    all_to_all x1, starting transfers between devices: 10.1 us -> 8.38 us  [body(): lax.all_to_all(outgoing, ('dp', 'shard'), split_axis=0, concat_axis=0, ti...]
    ppermute x6, waiting for transfers between devices: 8.39 us -> 9.87 us  [hop(): lax.ppermute(x, 'dp', [(i, (i + step) % replicas) for i in range(replicas)])]
where the time goes in v5:
time: 89.5 us; the launch traced here: 88.9 us
  waiting for transfers between devices  41 us (46%)
  starting transfers between devices  28.5 us (32%)
  Pallas kernels  15.6 us (17%)
  local copies, waits for them, and re-layouts  2.05 us (2%)
    all_to_all x1, waiting for transfers between devices, body(): lax.all_to_all(outgoing, ('dp', 'shard'), split_axis=0, concat_axis=0, ti...  18.6 us
    all_to_all x1, waiting for transfers between devices, body(): lax.all_to_all(outbound.reshape(all_slots, rows, width), ('dp', 'shard'),...  12.5 us
    ppermute x6, starting transfers between devices, hop(): lax.ppermute(x, 'dp', [(i, (i + step) % replicas) for i in range(replicas)])  10.7 us
    ppermute x6, waiting for transfers between devices, hop(): lax.ppermute(x, 'dp', [(i, (i + step) % replicas) for i in range(replicas)])  9.87 us
    all_to_all x1, starting transfers between devices, body(): lax.all_to_all(outbound.reshape(all_slots, rows, width), ('dp', 'shard'),...  9.42 us
    all_to_all x1, starting transfers between devices, body(): lax.all_to_all(outgoing, ('dp', 'shard'), split_axis=0, concat_axis=0, ti...  8.38 us
    pallas_call x1, Pallas kernels, new_state(): pl.pallas_call(functools.partial(state_kernel, gain, slots), out_shape=(s...  6.79 us
    pallas_call x1, Pallas kernels, gather_pieces(): pl.pallas_call(gather_kernel, out_shape=jax.ShapeDtypeStruct((slots, rows...  2.12 us
  transfers between devices with their start and end apart: 8, of which 5 were waited for; matrix products, arithmetic and copies ran while one was open for 1% of the time, Pallas kernels for 11%

profile of v5, /device:TPU:1, one launch (start us, length us, event | category | flops | bytes accessed | tf_op | source)
XLA Modules:
  0.0 88.9 jit_solution(17369999174852099708)
XLA Ops:
  0.6 0.0 copy-start
  0.6 0.0 copy-start.6
  0.7 0.0 copy-start.7
  0.7 0.0 copy-start.5
  0.7 2.0 %dynamic-slice_bitcast_fusion = (bf16[4,16,16,128]{3,2,1,0:T(8,128)(2,1)}, bf16[4,16,16,128]{3,2,1,0:T(8,128)(2,1)}) fusion(bf16[1,8,16,16,512]{4,3,2,1,0:T(8,128)(2,1)} %param.8, s32[]{:T(128)S(6)} %add.22, s32[]{:T(128)S(6)} %select_n.18), kind=kLoop, calls=%fused_computation | loop fusion | bytes 1048584 | tf_op jit(solution)/shard_map/slice | solution.py:451
  2.7 4.6 %collective-permute-start.4 = (bf16[4,16,16,128]{3,2,1,0:T(8,128)(2,1)}, bf16[4,16,16,128]{3,2,1,0:T(8,128)(2,1)S(1)}, u32[]{:S(2)}, u32[]{:S(2)}) collective-permute-start(bf16[4,16,16,128]{3,2,1,0:T(8,128)(2,1)} %get-tuple-element.81), channel_id=1, source_target_pairs={{0,96},{32,0},{64,32},{96,64},{1,97},{33,1},{65,33},{97,65},{2,98}... | collective-permute-start | bytes 786440 | tf_op jit(solution)/shard_map/ppermute | solution.py:446
  7.3 0.0 collective-permute-start.2
  7.3 1.8 %windows.1 = (bf16[4,16,16,128]{3,2,1,0:T(8,128)(2,1)}, bf16[4,16,16,128]{3,2,1,0:T(8,128)(2,1)S(1)}) custom-call(bf16[8,16,16,512]{3,2,1,0:T(8,128)(2,1)} %bitcast.8), custom_call_target="tpu_custom_call" | custom-call | tf_op jit(solution)/shard_map/windows/pallas_call | solution.py:79
  9.0 0.1 collective-permute-start
  9.1 2.7 %collective-permute-start.1 = (bf16[4,16,16,128]{3,2,1,0:T(8,128)(2,1)S(1)}, bf16[4,16,16,128]{3,2,1,0:T(8,128)(2,1)S(1)}, u32[]{:S(2)}, u32[]{:S(2)}) collective-permute-start(bf16[4,16,16,128]{3,2,1,0:T(8,128)(2,1)S(1)} %get-tuple-element.44), channel_id=1, source_target_pairs={{0,96},{32,0},{64,32},{96,64},{1,97},{33,1},{65,33},{97,65},{2,98}... | collective-permute-start | bytes 786440 | tf_op jit(solution)/shard_map/ppermute | solution.py:446
  11.9 0.0 copy-done.6
  11.9 0.0 copy-done.7
  11.9 0.0 copy-done.5
  11.9 0.2 convert_reduce_fusion
  12.1 0.6 fusion.1
  12.7 0.0 collective-permute-done.4.came
  12.7 0.0 copy-done
  12.7 0.1 merge_far_part.3
  12.8 3.3 %collective-permute-start.5 = (bf16[4,16,16,128]{3,2,1,0:T(8,128)(2,1)S(1)}, bf16[4,16,16,128]{3,2,1,0:T(8,128)(2,1)S(1)}, u32[]{:S(2)}, u32[]{:S(2)}) collective-permute-start(bf16[4,16,16,128]{3,2,1,0:T(8,128)(2,1)S(1)} %merge_far_part.3), channel_id=1, source_target_pairs={{0,96},{32,0},{64,32},{96,64},{1,97},{33,1},{65,33},{97,65},{2,98}... | collective-permute-start | bytes 786440 | tf_op jit(solution)/shard_map/ppermute | solution.py:446
  16.0 0.0 collective-permute-done.2.came
  16.0 0.1 merge_far_part.2
  16.1 0.1 collective-permute-start.3
  16.2 0.1 select_reduce_fusion.table
  16.3 0.6 early_products.2
  16.9 0.0 copy-start.1
  16.9 4.3 %collective-permute-done.ups = bf16[4,16,16,128]{3,2,1,0:T(8,128)(2,1)S(1)} collective-permute-done((bf16[4,16,16,128]{3,2,1,0:T(8,128)(2,1)}, bf16[4,16,16,128]{3,2,1,0:T(8,128)(2,1)S(1)}, u32[]{:S(2)}, u32[]{:S(2)}) %collective-permute-start) | collective-permute-done | bytes 262176 | tf_op jit(solution)/shard_map/ppermute | solution.py:446
  21.2 0.0 collective-permute-done.1.downs
  21.2 2.5 %collective-permute-done.5.downs_more = bf16[4,16,16,128]{3,2,1,0:T(8,128)(2,1)S(1)} collective-permute-done((bf16[4,16,16,128]{3,2,1,0:T(8,128)(2,1)S(1)}, bf16[4,16,16,128]{3,2,1,0:T(8,128)(2,1)S(1)}, u32[]{:S(2)}, u32[]{:S(2)}) %collective-permute-start.5) | collective-permute-done | bytes 262176 | tf_op jit(solution)/shard_map/ppermute | solution.py:446
  23.7 3.1 %collective-permute-done.3.ups_more = bf16[4,16,16,128]{3,2,1,0:T(8,128)(2,1)S(1)} collective-permute-done((bf16[4,16,16,128]{3,2,1,0:T(8,128)(2,1)S(1)}, bf16[4,16,16,128]{3,2,1,0:T(8,128)(2,1)S(1)}, u32[]{:S(2)}, u32[]{:S(2)}) %collective-permute-start.3) | collective-permute-done | bytes 262176 | tf_op jit(solution)/shard_map/ppermute | solution.py:446
  26.8 2.1 %sum_and_gather.1 = bf16[256,16,128]{2,1,0:T(8,128)(2,1)} custom-call(s32[128]{0:T(128)S(1)} %select_reduce_fusion.table, bf16[8,16,16,512]{3,2,1,0:T(8,128)(2,1)S(1)} %bitcast.11, bf16[4,16,16,128]{3,2,1,0:T(8,128)(2,1)S(1)} %collective-permute-done.ups, bf16[4,16,16,128]{3,2,1,0:T(8,128)(2,1)S(1)} %collective-permute-done.1.downs, ...), custom_call_target="tpu_custom_call" | custom-call | tf_op jit(solution)/shard_map/sum_and_gather/pallas_call | solution.py:126
  28.9 8.4 %all-to-all-start = ((bf16[256,16,128]{2,1,0:T(8,128)(2,1)}), bf16[256,16,128]{2,1,0:T(8,128)(2,1)S(1)}, u32[]{:S(2)}, u32[]{:S(2)}) async-start(bf16[256,16,128]{2,1,0:T(8,128)(2,1)} %sum_and_gather.1), calls=%async_computation | async-start | bytes 2097152 | tf_op jit(solution)/shard_map/all_to_all | solution.py:475
  37.3 0.7 early_products.3
  38.0 0.0 copy-start.2
  38.0 0.0 copy-start.3
  38.0 0.0 copy-start.4
  38.0 18.6 %all-to-all-done = bf16[256,16,128]{2,1,0:T(8,128)(2,1)S(1)} async-done(((bf16[256,16,128]{2,1,0:T(8,128)(2,1)}), bf16[256,16,128]{2,1,0:T(8,128)(2,1)S(1)}, u32[]{:S(2)}, u32[]{:S(2)}) %all-to-all-start) | async-done | bytes 1048608 | tf_op jit(solution)/shard_map/all_to_all | solution.py:475
  56.6 0.0 copy-done.1
  56.7 1.7 %update_pieces.1 = bf16[4,32,2,16,128]{4,3,2,1,0:T(8,128)(2,1)} custom-call(s32[1]{0:T(128)} %bitcast.count, bf16[4,32,2,16,128]{4,3,2,1,0:T(8,128)(2,1)S(1)} %bitcast.12, f32[2,512,512]{2,1,0:T(8,128)} %xl.3, f32[2,512,512]{2,1,0:T(8,128)} %xr.3, bf16[512,512]{1,0:T(8,128)(2,1)S(1)} %get-tuple-element.65.refs_0_, ...), custom_call_target="tpu_custom_call" | custom-call | tf_op jit(solution)/shard_map/update_pieces/pallas_call | solution.py:335
  58.4 0.0 copy-done.2
  58.4 0.0 copy-done.3
  58.4 0.0 copy-done.4
  58.4 9.4 %all-to-all-start.1 = ((bf16[256,16,128]{2,1,0:T(8,128)(2,1)}), bf16[256,16,128]{2,1,0:T(8,128)(2,1)S(1)}, u32[]{:S(2)}, u32[]{:S(2)}) async-start(bf16[256,16,128]{2,1,0:T(8,128)(2,1)} %bitcast.14), calls=%async_computation.1 | async-start | bytes 2097152 | tf_op jit(solution)/shard_map/all_to_all | solution.py:484
  67.9 6.8 %new_state.1 = (f32[2,512,512]{2,1,0:T(8,128)}, f32[2,512,512]{2,1,0:T(8,128)}, f32[2,512,512]{2,1,0:T(8,128)}, f32[2,512,512]{2,1,0:T(8,128)}) custom-call(s32[1]{0:T(128)} %bitcast.count, bf16[4,32,2,16,128]{4,3,2,1,0:T(8,128)(2,1)S(1)} %bitcast.13, f32[2,512,512]{2,1,0:T(8,128)} %left.1, f32[2,512,512]{2,1,0:T(8,128)} %right.1, f32[2,512,512]{2,1,0:T(8,128)} %xl.3, ...), custom_call_target="tpu_custom_call" | custom-call | flops 4294967296 | bytes 18874368 | tf_op jit(solution)/shard_map/new_state/pallas_call | solution.py:412
  74.7 12.5 %all-to-all-done.1.arrived = bf16[256,16,128]{2,1,0:T(8,128)(2,1)S(1)} async-done(((bf16[256,16,128]{2,1,0:T(8,128)(2,1)}), bf16[256,16,128]{2,1,0:T(8,128)(2,1)S(1)}, u32[]{:S(2)}, u32[]{:S(2)}) %all-to-all-start.1) | async-done | bytes 1048608 | tf_op jit(solution)/shard_map/all_to_all | solution.py:484
  87.2 1.7 %place_pieces.1 = bf16[8,16,16,128]{3,2,1,0:T(8,128)(2,1)} custom-call(s32[128]{0:T(128)S(1)} %select_reduce_fusion.table, bf16[256,16,128]{2,1,0:T(8,128)(2,1)S(1)} %all-to-all-done.1.arrived), custom_call_target="tpu_custom_call" | custom-call | tf_op jit(solution)/shard_map/place_pieces/pallas_call | solution.py:149
  (1 shorter events, 0.0 us)
Async XLA Ops:
  0.6 12.1 %copy-start = (bf16[1,8,16,16,512]{4,3,2,1,0:T(8,128)(2,1)S(1)}, bf16[1,8,16,16,512]{4,3,2,1,0:T(8,128)(2,1)}, u32[]{:S(2)}) copy-start(bf16[1,8,16,16,512]{4,3,2,1,0:T(8,128)(2,1)} %param.8) | copy-start | bytes 6291460
  0.6 11.2 %copy-start.6 = (s32[128]{0:T(128)S(1)}, s32[128]{0:T(128)}, u32[]{:S(2)}) copy-start(s32[128]{0:T(128)} %param.11) | copy-start | bytes 1540
  0.7 11.2 %copy-start.7 = (s32[128]{0:T(128)S(1)}, s32[128]{0:T(128)}, u32[]{:S(2)}) copy-start(s32[128]{0:T(128)} %param.10) | copy-start | bytes 1540
  0.7 11.2 %copy-start.5 = (s32[128]{0:T(128)S(1)}, s32[128]{0:T(128)}, u32[]{:S(2)}) copy-start(s32[128]{0:T(128)} %param.9) | copy-start | bytes 1540
  2.7 10.0 %collective-permute-start.4 = (bf16[4,16,16,128]{3,2,1,0:T(8,128)(2,1)}, bf16[4,16,16,128]{3,2,1,0:T(8,128)(2,1)S(1)}, u32[]{:S(2)}, u32[]{:S(2)}) collective-permute-start(bf16[4,16,16,128]{3,2,1,0:T(8,128)(2,1)} %get-tuple-element.81), channel_id=1, source_target_pairs={{0,96},{32,0},{64,32},{96,64},{1,97},{33,1},{65,33},{97,65},{2,98}... | collective-permute-start | bytes 786440 | tf_op jit(solution)/shard_map/ppermute | solution.py:446
  7.3 8.8 %collective-permute-start.2 = (bf16[4,16,16,128]{3,2,1,0:T(8,128)(2,1)}, bf16[4,16,16,128]{3,2,1,0:T(8,128)(2,1)S(1)}, u32[]{:S(2)}, u32[]{:S(2)}) collective-permute-start(bf16[4,16,16,128]{3,2,1,0:T(8,128)(2,1)} %get-tuple-element.82), channel_id=1, source_target_pairs={{0,32},{32,64},{64,96},{96,0},{1,33},{33,65},{65,97},{97,1},{2,34}... | collective-permute-start | bytes 786440 | tf_op jit(solution)/shard_map/ppermute | solution.py:446
  9.0 12.1 %collective-permute-start = (bf16[4,16,16,128]{3,2,1,0:T(8,128)(2,1)}, bf16[4,16,16,128]{3,2,1,0:T(8,128)(2,1)S(1)}, u32[]{:S(2)}, u32[]{:S(2)}) collective-permute-start(bf16[4,16,16,128]{3,2,1,0:T(8,128)(2,1)} %get-tuple-element.43), channel_id=1, source_target_pairs={{0,32},{32,64},{64,96},{96,0},{1,33},{33,65},{65,97},{97,1},{2,34}... | collective-permute-start | bytes 786440 | tf_op jit(solution)/shard_map/ppermute | solution.py:446
  9.1 12.0 %collective-permute-start.1 = (bf16[4,16,16,128]{3,2,1,0:T(8,128)(2,1)S(1)}, bf16[4,16,16,128]{3,2,1,0:T(8,128)(2,1)S(1)}, u32[]{:S(2)}, u32[]{:S(2)}) collective-permute-start(bf16[4,16,16,128]{3,2,1,0:T(8,128)(2,1)S(1)} %get-tuple-element.44), channel_id=1, source_target_pairs={{0,96},{32,0},{64,32},{96,64},{1,97},{33,1},{65,33},{97,65},{2,98}... | collective-permute-start | bytes 786440 | tf_op jit(solution)/shard_map/ppermute | solution.py:446
  12.8 10.9 %collective-permute-start.5 = (bf16[4,16,16,128]{3,2,1,0:T(8,128)(2,1)S(1)}, bf16[4,16,16,128]{3,2,1,0:T(8,128)(2,1)S(1)}, u32[]{:S(2)}, u32[]{:S(2)}) collective-permute-start(bf16[4,16,16,128]{3,2,1,0:T(8,128)(2,1)S(1)} %merge_far_part.3), channel_id=1, source_target_pairs={{0,96},{32,0},{64,32},{96,64},{1,97},{33,1},{65,33},{97,65},{2,98}... | collective-permute-start | bytes 786440 | tf_op jit(solution)/shard_map/ppermute | solution.py:446
  16.1 10.7 %collective-permute-start.3 = (bf16[4,16,16,128]{3,2,1,0:T(8,128)(2,1)S(1)}, bf16[4,16,16,128]{3,2,1,0:T(8,128)(2,1)S(1)}, u32[]{:S(2)}, u32[]{:S(2)}) collective-permute-start(bf16[4,16,16,128]{3,2,1,0:T(8,128)(2,1)S(1)} %merge_far_part.2), channel_id=1, source_target_pairs={{0,32},{32,64},{64,96},{96,0},{1,33},{33,65},{65,97},{97,1},{2,34}... | collective-permute-start | bytes 786440 | tf_op jit(solution)/shard_map/ppermute | solution.py:446
  16.9 39.7 %copy-start.1 = (bf16[512,512]{1,0:T(8,128)(2,1)}, bf16[512,512]{1,0:T(8,128)(2,1)S(1)}, u32[]{:S(2)}) copy-start(bf16[512,512]{1,0:T(8,128)(2,1)S(1)} %get-tuple-element.65.refs_0_) | copy-start | bytes 1572868
  28.9 27.7 %all-to-all-start = ((bf16[256,16,128]{2,1,0:T(8,128)(2,1)}), bf16[256,16,128]{2,1,0:T(8,128)(2,1)S(1)}, u32[]{:S(2)}, u32[]{:S(2)}) async-start(bf16[256,16,128]{2,1,0:T(8,128)(2,1)} %sum_and_gather.1), calls=%async_computation | async-start | bytes 2097152 | tf_op jit(solution)/shard_map/all_to_all | solution.py:475
  38.0 20.4 %copy-start.2 = (bf16[512,512]{1,0:T(8,128)(2,1)}, bf16[512,512]{1,0:T(8,128)(2,1)S(1)}, u32[]{:S(2)}) copy-start(bf16[512,512]{1,0:T(8,128)(2,1)S(1)} %get-tuple-element.67.refs_2_) | copy-start | bytes 1572868
  38.0 20.4 %copy-start.3 = (bf16[512,512]{1,0:T(8,128)(2,1)}, bf16[512,512]{1,0:T(8,128)(2,1)S(1)}, u32[]{:S(2)}) copy-start(bf16[512,512]{1,0:T(8,128)(2,1)S(1)} %get-tuple-element.69.refs_4_) | copy-start | bytes 1572868
  38.0 20.4 %copy-start.4 = (bf16[512,512]{1,0:T(8,128)(2,1)}, bf16[512,512]{1,0:T(8,128)(2,1)S(1)}, u32[]{:S(2)}) copy-start(bf16[512,512]{1,0:T(8,128)(2,1)S(1)} %get-tuple-element.71.refs_6_) | copy-start | bytes 1572868
  58.4 28.8 %all-to-all-start.1 = ((bf16[256,16,128]{2,1,0:T(8,128)(2,1)}), bf16[256,16,128]{2,1,0:T(8,128)(2,1)S(1)}, u32[]{:S(2)}, u32[]{:S(2)}) async-start(bf16[256,16,128]{2,1,0:T(8,128)(2,1)} %bitcast.14), calls=%async_computation.1 | async-start | bytes 2097152 | tf_op jit(solution)/shard_map/all_to_all | solution.py:484

commit v6 on v5

--- a/solution.py
+++ b/solution.py
@@ -451,7 +451,6 @@
     far_low, far_high = far[:half], far[half:]
     far_low, far_high = hop(far_low, 1), hop(far_high, -1)
     near_high, near_low = windows(mine, width, ((half, 1), (0, 3)))
-    near_high, near_low = hop(near_high, 1), hop(near_low, -1)
 
     entries = jnp.arange(owner_list.shape[0], dtype=jnp.int32)
     same = owner_list[None, :] == owner_list[:, None]
@@ -464,8 +463,11 @@
     owner = lax.axis_index(("dp", "shard"))
     count = jnp.sum((owner_list == owner).astype(jnp.int32)).reshape(1)
 
-    far_low = hop(merged(mine, 0, 1, far_low), 1)
-    far_high = hop(merged(mine, half, 3, far_high), -1)
+    far_low, far_high = merged(mine, 0, 1, far_low), merged(mine, half, 3, far_high)
+    far_low, near_high = lax.optimization_barrier((far_low, near_high))
+    far_high, near_low = lax.optimization_barrier((far_high, near_low))
+    far_low, far_high = hop(far_low, 1), hop(far_high, -1)
+    near_high, near_low = hop(near_high, 1), hop(near_low, -1)
     (first,) = early(count, (0, left_root, left_factor))
     arrived = (near_high, near_low, far_low, far_high)
     arrived, first = lax.optimization_barrier((arrived, first))

time: 89.5 us -> 93.7 us (1.047)
  Pallas kernels: 15.6 us -> 30.1 us
  waiting for transfers between devices: 41 us -> 33.4 us
  starting transfers between devices: 28.5 us -> 24.2 us
  other arithmetic: 0.89 us -> 2.34 us
    pallas_call x2, Pallas kernels: 1.3 us -> 11.6 us  [early(): pl.pallas_call(functools.partial(early_kernel, [t for t, _, _ in items]),...]
    all_to_all x1, waiting for transfers between devices: 18.6 us -> 13.5 us  [body(): lax.all_to_all(outgoing, ('dp', 'shard'), split_axis=0, concat_axis=0, ti...]
    all_to_all x1, starting transfers between devices: 9.42 us -> 5.75 us  [body(): lax.all_to_all(outbound.reshape(all_slots, rows, width), ('dp', 'shard'),...]
    pallas_call x1, Pallas kernels: 1.75 us -> 4.98 us  [update_pieces(): pl.pallas_call(functools.partial(update_kernel, gain, slots), out_shape=s...]
    ppermute x6, starting transfers between devices: 10.7 us -> 7.58 us  [hop(): lax.ppermute(x, 'dp', [(i, (i + step) % replicas) for i in range(replicas)])]
    all_to_all x1, starting transfers between devices: 8.38 us -> 10.9 us  [body(): lax.all_to_all(outgoing, ('dp', 'shard'), split_axis=0, concat_axis=0, ti...]
    pallas_call x1, Pallas kernels: 6.79 us -> 8.52 us  [new_state(): pl.pallas_call(functools.partial(state_kernel, gain, slots), out_shape=(s...]
    all_to_all x1, waiting for transfers between devices: 12.5 us -> 10.8 us  [body(): lax.all_to_all(outbound.reshape(all_slots, rows, width), ('dp', 'shard'),...]
  transfers between devices with their start and end apart: 8 -> 8, of which waited for: 5 -> 5; matrix products, arithmetic and copies ran while one was open for 1% -> 3% of each run, Pallas kernels for 11% -> 23%
where the time goes in v6:
time: 93.7 us; the launch traced here: 92.8 us
  waiting for transfers between devices  33.4 us (36%)
  Pallas kernels  30.1 us (32%)
  starting transfers between devices  24.2 us (26%)
  other arithmetic  2.34 us (2%)
  local copies, waits for them, and re-layouts  1.95 us (2%)
    all_to_all x1, waiting for transfers between devices, body(): lax.all_to_all(outgoing, ('dp', 'shard'), split_axis=0, concat_axis=0, ti...  13.5 us
    pallas_call x2, Pallas kernels, early(): pl.pallas_call(functools.partial(early_kernel, [t for t, _, _ in items]),...  11.6 us
    all_to_all x1, starting transfers between devices, body(): lax.all_to_all(outgoing, ('dp', 'shard'), split_axis=0, concat_axis=0, ti...  10.9 us
    all_to_all x1, waiting for transfers between devices, body(): lax.all_to_all(outbound.reshape(all_slots, rows, width), ('dp', 'shard'),...  10.8 us
    ppermute x6, waiting for transfers between devices, hop(): lax.ppermute(x, 'dp', [(i, (i + step) % replicas) for i in range(replicas)])  9.05 us
    pallas_call x1, Pallas kernels, new_state(): pl.pallas_call(functools.partial(state_kernel, gain, slots), out_shape=(s...  8.52 us
    ppermute x6, starting transfers between devices, hop(): lax.ppermute(x, 'dp', [(i, (i + step) % replicas) for i in range(replicas)])  7.58 us
    all_to_all x1, starting transfers between devices, body(): lax.all_to_all(outbound.reshape(all_slots, rows, width), ('dp', 'shard'),...  5.75 us
  transfers between devices with their start and end apart: 8, of which 5 were waited for; matrix products, arithmetic and copies ran while one was open for 3% of the time, Pallas kernels for 23%

profile of v6, /device:TPU:1, one launch (start us, length us, event | category | flops | bytes accessed | tf_op | source)
XLA Modules:
  0.0 92.8 jit_solution(9028237034611728776)
XLA Ops:
  0.6 0.0 copy-start
  0.6 0.0 copy-start.5
  0.7 1.9 %dynamic-slice_bitcast_fusion = (bf16[4,16,16,128]{3,2,1,0:T(8,128)(2,1)S(1)}, bf16[4,16,16,128]{3,2,1,0:T(8,128)(2,1)}) fusion(bf16[1,8,16,16,512]{4,3,2,1,0:T(8,128)(2,1)} %param.8, s32[]{:T(128)S(6)} %add.22, s32[]{:T(128)S(6)} %select_n.18), kind=kLoop, calls=%fused_computation | loop fusion | bytes 1048584 | tf_op jit(solution)/shard_map/slice | solution.py:451
  2.6 4.6 %collective-permute-start.2 = (bf16[4,16,16,128]{3,2,1,0:T(8,128)(2,1)S(1)}, bf16[4,16,16,128]{3,2,1,0:T(8,128)(2,1)S(1)}, u32[]{:S(2)}, u32[]{:S(2)}) collective-permute-start(bf16[4,16,16,128]{3,2,1,0:T(8,128)(2,1)S(1)} %get-tuple-element.89), channel_id=1, source_target_pairs={{0,96},{32,0},{64,32},{96,64},{1,97},{33,1},{65,33},{97,65},{2,98}... | collective-permute-start | bytes 786440 | tf_op jit(solution)/shard_map/ppermute | solution.py:446
  7.2 0.0 collective-permute-start
  7.2 0.7 fusion.2
  7.9 0.9 convert_reduce_fusion
  8.8 1.1 %windows.1 = (bf16[4,16,16,128]{3,2,1,0:T(8,128)(2,1)S(1)}, bf16[4,16,16,128]{3,2,1,0:T(8,128)(2,1)S(1)}) custom-call(bf16[8,16,16,512]{3,2,1,0:T(8,128)(2,1)} %bitcast.8), custom_call_target="tpu_custom_call" | custom-call | tf_op jit(solution)/shard_map/windows/pallas_call | solution.py:79
  9.8 0.0 copy-done.5
  9.9 0.7 fusion.1
  10.5 4.9 %collective-permute-done.came = bf16[4,16,16,128]{3,2,1,0:T(8,128)(2,1)S(1)} collective-permute-done((bf16[4,16,16,128]{3,2,1,0:T(8,128)(2,1)}, bf16[4,16,16,128]{3,2,1,0:T(8,128)(2,1)S(1)}, u32[]{:S(2)}, u32[]{:S(2)}) %collective-permute-start) | collective-permute-done | bytes 262176 | tf_op jit(solution)/shard_map/ppermute | solution.py:446
  15.5 0.0 copy-done
  15.5 0.1 merge_far_part.2
  15.5 0.0 collective-permute-done.2.came
  15.5 0.1 merge_far_part.3
  15.6 0.1 collective-permute-start.3
  15.7 0.1 collective-permute-start.5
  15.8 1.5 %collective-permute-start.1 = (bf16[4,16,16,128]{3,2,1,0:T(8,128)(2,1)S(1)}, bf16[4,16,16,128]{3,2,1,0:T(8,128)(2,1)S(1)}, u32[]{:S(2)}, u32[]{:S(2)}) collective-permute-start(bf16[4,16,16,128]{3,2,1,0:T(8,128)(2,1)S(1)} %get-tuple-element.48), channel_id=1, source_target_pairs={{0,32},{32,64},{64,96},{96,0},{1,33},{33,65},{65,97},{97,1},{2,34}... | collective-permute-start | bytes 786440 | tf_op jit(solution)/shard_map/ppermute | solution.py:446
  17.3 1.4 %collective-permute-start.4 = (bf16[4,16,16,128]{3,2,1,0:T(8,128)(2,1)S(1)}, bf16[4,16,16,128]{3,2,1,0:T(8,128)(2,1)S(1)}, u32[]{:S(2)}, u32[]{:S(2)}) collective-permute-start(bf16[4,16,16,128]{3,2,1,0:T(8,128)(2,1)S(1)} %merge_far_part.2), channel_id=1, source_target_pairs={{0,32},{32,64},{64,96},{96,0},{1,33},{33,65},{65,97},{97,1},{2,34}... | collective-permute-start | bytes 786440 | tf_op jit(solution)/shard_map/ppermute | solution.py:446
  18.6 0.1 select_reduce_fusion.table
  18.7 5.8 %early_products.2 = (bf16[512,512]{1,0:T(8,128)(2,1)S(1)}, bf16[512,512]{1,0:T(8,128)(2,1)}, bf16[512,512]{1,0:T(8,128)(2,1)}) custom-call(s32[1]{0:T(128)} %bitcast.count, f32[2,512,512]{2,1,0:T(8,128)} %xl.3, f32[2,512,512]{2,1,0:T(8,128)} %left.1), custom_call_target="tpu_custom_call" | custom-call | flops 2415919104 | bytes 3145728 | tf_op jit(solution)/shard_map/early_products/pallas_call | solution.py:211
  24.5 0.0 copy-start.1
  24.5 0.0 collective-permute-done.3.downs
  24.5 2.7 %collective-permute-done.5.downs_more = bf16[4,16,16,128]{3,2,1,0:T(8,128)(2,1)S(1)} collective-permute-done((bf16[4,16,16,128]{3,2,1,0:T(8,128)(2,1)S(1)}, bf16[4,16,16,128]{3,2,1,0:T(8,128)(2,1)S(1)}, u32[]{:S(2)}, u32[]{:S(2)}) %collective-permute-start.5) | collective-permute-done | bytes 262176 | tf_op jit(solution)/shard_map/ppermute | solution.py:446
  27.3 0.0 collective-permute-done.1.ups
  27.3 1.4 %collective-permute-done.4.ups_more = bf16[4,16,16,128]{3,2,1,0:T(8,128)(2,1)S(1)} collective-permute-done((bf16[4,16,16,128]{3,2,1,0:T(8,128)(2,1)S(1)}, bf16[4,16,16,128]{3,2,1,0:T(8,128)(2,1)S(1)}, u32[]{:S(2)}, u32[]{:S(2)}) %collective-permute-start.4) | collective-permute-done | bytes 262176 | tf_op jit(solution)/shard_map/ppermute | solution.py:446
  28.6 2.1 %sum_and_gather.1 = bf16[256,16,128]{2,1,0:T(8,128)(2,1)} custom-call(s32[128]{0:T(128)S(1)} %select_reduce_fusion.table, bf16[8,16,16,512]{3,2,1,0:T(8,128)(2,1)S(1)} %bitcast.11, bf16[4,16,16,128]{3,2,1,0:T(8,128)(2,1)S(1)} %collective-permute-done.1.ups, bf16[4,16,16,128]{3,2,1,0:T(8,128)(2,1)S(1)} %collective-permute-done.3.downs, ...), custom_call_target="tpu_custom_call" | custom-call | tf_op jit(solution)/shard_map/sum_and_gather/pallas_call | solution.py:126
  30.7 10.9 %all-to-all-start = ((bf16[256,16,128]{2,1,0:T(8,128)(2,1)}), bf16[256,16,128]{2,1,0:T(8,128)(2,1)S(1)}, u32[]{:S(2)}, u32[]{:S(2)}) async-start(bf16[256,16,128]{2,1,0:T(8,128)(2,1)} %sum_and_gather.1), calls=%async_computation | async-start | bytes 2097152 | tf_op jit(solution)/shard_map/all_to_all | solution.py:477
  41.7 5.8 %early_products.3 = (bf16[512,512]{1,0:T(8,128)(2,1)S(1)}, bf16[512,512]{1,0:T(8,128)(2,1)}, bf16[512,512]{1,0:T(8,128)(2,1)}, bf16[512,512]{1,0:T(8,128)(2,1)S(...) custom-call(s32[1]{0:T(128)} %bitcast.count, ...), custom_call_target="tpu_custom_call" | custom-call | flops 7247757312 | bytes 9437184 | tf_op jit(solution)/shard_map/early_products/pallas_call | solution.py:211
  47.5 0.0 copy-start.2
  47.5 0.0 copy-start.3
  47.5 0.0 copy-start.4
  47.5 13.5 %all-to-all-done = bf16[256,16,128]{2,1,0:T(8,128)(2,1)S(1)} async-done(((bf16[256,16,128]{2,1,0:T(8,128)(2,1)}), bf16[256,16,128]{2,1,0:T(8,128)(2,1)S(1)}, u32[]{:S(2)}, u32[]{:S(2)}) %all-to-all-start) | async-done | bytes 1048608 | tf_op jit(solution)/shard_map/all_to_all | solution.py:477
  61.0 0.0 copy-done.1
  61.0 5.0 %update_pieces.1 = bf16[4,32,2,16,128]{4,3,2,1,0:T(8,128)(2,1)} custom-call(s32[1]{0:T(128)} %bitcast.count, bf16[4,32,2,16,128]{4,3,2,1,0:T(8,128)(2,1)S(1)} %bitcast.12, f32[2,512,512]{2,1,0:T(8,128)} %xl.3, f32[2,512,512]{2,1,0:T(8,128)} %xr.3, bf16[512,512]{1,0:T(8,128)(2,1)S(1)} %get-tuple-element.73.refs_0_, ...), custom_call_target="tpu_custom_call" | custom-call | tf_op jit(solution)/shard_map/update_pieces/pallas_call | solution.py:335
  66.0 0.0 copy-done.2
  66.0 0.0 copy-done.3
  66.0 0.0 copy-done.4
  66.0 5.7 %all-to-all-start.1 = ((bf16[256,16,128]{2,1,0:T(8,128)(2,1)}), bf16[256,16,128]{2,1,0:T(8,128)(2,1)S(1)}, u32[]{:S(2)}, u32[]{:S(2)}) async-start(bf16[256,16,128]{2,1,0:T(8,128)(2,1)} %bitcast.14), calls=%async_computation.1 | async-start | bytes 2097152 | tf_op jit(solution)/shard_map/all_to_all | solution.py:486
  71.8 8.5 %new_state.1 = (f32[2,512,512]{2,1,0:T(8,128)}, f32[2,512,512]{2,1,0:T(8,128)}, f32[2,512,512]{2,1,0:T(8,128)}, f32[2,512,512]{2,1,0:T(8,128)}) custom-call(s32[1]{0:T(128)} %bitcast.count, bf16[4,32,2,16,128]{4,3,2,1,0:T(8,128)(2,1)S(1)} %bitcast.13, f32[2,512,512]{2,1,0:T(8,128)} %left.1, f32[2,512,512]{2,1,0:T(8,128)} %right.1, f32[2,512,512]{2,1,0:T(8,128)} %xl.3, ...), custom_call_target="tpu_custom_call" | custom-call | flops 4294967296 | bytes 18874368 | tf_op jit(solution)/shard_map/new_state/pallas_call | solution.py:412
  80.3 10.8 %all-to-all-done.1.arrived = bf16[256,16,128]{2,1,0:T(8,128)(2,1)S(1)} async-done(((bf16[256,16,128]{2,1,0:T(8,128)(2,1)}), bf16[256,16,128]{2,1,0:T(8,128)(2,1)S(1)}, u32[]{:S(2)}, u32[]{:S(2)}) %all-to-all-start.1) | async-done | bytes 1048608 | tf_op jit(solution)/shard_map/all_to_all | solution.py:486
  91.1 1.7 %place_pieces.1 = bf16[8,16,16,128]{3,2,1,0:T(8,128)(2,1)} custom-call(s32[128]{0:T(128)S(1)} %select_reduce_fusion.table, bf16[256,16,128]{2,1,0:T(8,128)(2,1)S(1)} %all-to-all-done.1.arrived), custom_call_target="tpu_custom_call" | custom-call | tf_op jit(solution)/shard_map/place_pieces/pallas_call | solution.py:149
Async XLA Ops:
  0.6 14.8 %copy-start = (bf16[1,8,16,16,512]{4,3,2,1,0:T(8,128)(2,1)S(1)}, bf16[1,8,16,16,512]{4,3,2,1,0:T(8,128)(2,1)}, u32[]{:S(2)}) copy-start(bf16[1,8,16,16,512]{4,3,2,1,0:T(8,128)(2,1)} %param.8) | copy-start | bytes 6291460
  0.6 9.2 %copy-start.5 = (s32[128]{0:T(128)S(1)}, s32[128]{0:T(128)}, u32[]{:S(2)}) copy-start(s32[128]{0:T(128)} %param.9) | copy-start | bytes 1540
  2.6 13.0 %collective-permute-start.2 = (bf16[4,16,16,128]{3,2,1,0:T(8,128)(2,1)S(1)}, bf16[4,16,16,128]{3,2,1,0:T(8,128)(2,1)S(1)}, u32[]{:S(2)}, u32[]{:S(2)}) collective-permute-start(bf16[4,16,16,128]{3,2,1,0:T(8,128)(2,1)S(1)} %get-tuple-element.89), channel_id=1, source_target_pairs={{0,96},{32,0},{64,32},{96,64},{1,97},{33,1},{65,33},{97,65},{2,98}... | collective-permute-start | bytes 786440 | tf_op jit(solution)/shard_map/ppermute | solution.py:446
  7.2 8.3 %collective-permute-start = (bf16[4,16,16,128]{3,2,1,0:T(8,128)(2,1)}, bf16[4,16,16,128]{3,2,1,0:T(8,128)(2,1)S(1)}, u32[]{:S(2)}, u32[]{:S(2)}) collective-permute-start(bf16[4,16,16,128]{3,2,1,0:T(8,128)(2,1)} %get-tuple-element.90), channel_id=1, source_target_pairs={{0,32},{32,64},{64,96},{96,0},{1,33},{33,65},{65,97},{97,1},{2,34}... | collective-permute-start | bytes 786440 | tf_op jit(solution)/shard_map/ppermute | solution.py:446
  15.6 8.9 %collective-permute-start.3 = (bf16[4,16,16,128]{3,2,1,0:T(8,128)(2,1)S(1)}, bf16[4,16,16,128]{3,2,1,0:T(8,128)(2,1)S(1)}, u32[]{:S(2)}, u32[]{:S(2)}) collective-permute-start(bf16[4,16,16,128]{3,2,1,0:T(8,128)(2,1)S(1)} %get-tuple-element.50), channel_id=1, source_target_pairs={{0,96},{32,0},{64,32},{96,64},{1,97},{33,1},{65,33},{97,65},{2,98}... | collective-permute-start | bytes 786440 | tf_op jit(solution)/shard_map/ppermute | solution.py:446
  15.7 11.5 %collective-permute-start.5 = (bf16[4,16,16,128]{3,2,1,0:T(8,128)(2,1)S(1)}, bf16[4,16,16,128]{3,2,1,0:T(8,128)(2,1)S(1)}, u32[]{:S(2)}, u32[]{:S(2)}) collective-permute-start(bf16[4,16,16,128]{3,2,1,0:T(8,128)(2,1)S(1)} %merge_far_part.3), channel_id=1, source_target_pairs={{0,96},{32,0},{64,32},{96,64},{1,97},{33,1},{65,33},{97,65},{2,98}... | collective-permute-start | bytes 786440 | tf_op jit(solution)/shard_map/ppermute | solution.py:446
  15.8 11.5 %collective-permute-start.1 = (bf16[4,16,16,128]{3,2,1,0:T(8,128)(2,1)S(1)}, bf16[4,16,16,128]{3,2,1,0:T(8,128)(2,1)S(1)}, u32[]{:S(2)}, u32[]{:S(2)}) collective-permute-start(bf16[4,16,16,128]{3,2,1,0:T(8,128)(2,1)S(1)} %get-tuple-element.48), channel_id=1, source_target_pairs={{0,32},{32,64},{64,96},{96,0},{1,33},{33,65},{65,97},{97,1},{2,34}... | collective-permute-start | bytes 786440 | tf_op jit(solution)/shard_map/ppermute | solution.py:446
  17.3 11.4 %collective-permute-start.4 = (bf16[4,16,16,128]{3,2,1,0:T(8,128)(2,1)S(1)}, bf16[4,16,16,128]{3,2,1,0:T(8,128)(2,1)S(1)}, u32[]{:S(2)}, u32[]{:S(2)}) collective-permute-start(bf16[4,16,16,128]{3,2,1,0:T(8,128)(2,1)S(1)} %merge_far_part.2), channel_id=1, source_target_pairs={{0,32},{32,64},{64,96},{96,0},{1,33},{33,65},{65,97},{97,1},{2,34}... | collective-permute-start | bytes 786440 | tf_op jit(solution)/shard_map/ppermute | solution.py:446
  24.5 36.5 %copy-start.1 = (bf16[512,512]{1,0:T(8,128)(2,1)}, bf16[512,512]{1,0:T(8,128)(2,1)S(1)}, u32[]{:S(2)}) copy-start(bf16[512,512]{1,0:T(8,128)(2,1)S(1)} %get-tuple-element.73.refs_0_) | copy-start | bytes 1572868
  30.7 30.3 %all-to-all-start = ((bf16[256,16,128]{2,1,0:T(8,128)(2,1)}), bf16[256,16,128]{2,1,0:T(8,128)(2,1)S(1)}, u32[]{:S(2)}, u32[]{:S(2)}) async-start(bf16[256,16,128]{2,1,0:T(8,128)(2,1)} %sum_and_gather.1), calls=%async_computation | async-start | bytes 2097152 | tf_op jit(solution)/shard_map/all_to_all | solution.py:477
  47.5 18.5 %copy-start.2 = (bf16[512,512]{1,0:T(8,128)(2,1)}, bf16[512,512]{1,0:T(8,128)(2,1)S(1)}, u32[]{:S(2)}) copy-start(bf16[512,512]{1,0:T(8,128)(2,1)S(1)} %get-tuple-element.75.refs_2_) | copy-start | bytes 1572868
  47.5 18.5 %copy-start.3 = (bf16[512,512]{1,0:T(8,128)(2,1)}, bf16[512,512]{1,0:T(8,128)(2,1)S(1)}, u32[]{:S(2)}) copy-start(bf16[512,512]{1,0:T(8,128)(2,1)S(1)} %get-tuple-element.77.refs_4_) | copy-start | bytes 1572868
  47.5 18.5 %copy-start.4 = (bf16[512,512]{1,0:T(8,128)(2,1)}, bf16[512,512]{1,0:T(8,128)(2,1)S(1)}, u32[]{:S(2)}) copy-start(bf16[512,512]{1,0:T(8,128)(2,1)S(1)} %get-tuple-element.79.refs_6_) | copy-start | bytes 1572868
  66.0 25.1 %all-to-all-start.1 = ((bf16[256,16,128]{2,1,0:T(8,128)(2,1)}), bf16[256,16,128]{2,1,0:T(8,128)(2,1)S(1)}, u32[]{:S(2)}, u32[]{:S(2)}) async-start(bf16[256,16,128]{2,1,0:T(8,128)(2,1)} %bitcast.14), calls=%async_computation.1 | async-start | bytes 2097152 | tf_op jit(solution)/shard_map/all_to_all | solution.py:486

commit v7 on v5

--- a/solution.py
+++ b/solution.py
@@ -87,33 +87,29 @@
     )(hbm(mine))
 
 
-def merge_kernel(low, hop, mine, came, out):
-    column = column_at(hop, out.shape[-1])
+def merge_kernel(own, came, out):
     for b in range(out.shape[0]):
-        own = mine[low + b, :, :, column].astype(f32)
-        out[b] = (own + came[b].astype(f32)).astype(bf16)
-
-
-def merged(mine, low, hop, came):
-    return pl.pallas_call(
-        functools.partial(merge_kernel, low, hop),
+        out[b] = (own[b].astype(f32) + came[b].astype(f32)).astype(bf16)
+
+
+def merged(own, came):
+    return pl.pallas_call(
+        merge_kernel,
         out_shape=pltpu.VMEM(came.shape, bf16),
         in_specs=[whole] * 2,
         out_specs=whole,
         compiler_params=params(4),
         name="merge_far_part",
-    )(vmem(mine), vmem(came))
-
-
-def gather_kernel(table, mine, ups, downs, ups_more, downs_more, out, held):
-    row_blocks, rows, cols, _ = mine.shape
-    width = ups.shape[-1]
-    half = row_blocks // 2
-    column = column_at(0, width)
+    )(vmem(own), vmem(came))
+
+
+def gather_kernel(table, *refs):
+    parts, (out, held) = refs[:6], refs[6:]
+    half, rows, cols, width = parts[0].shape
     out[...] = jnp.zeros_like(out)
-    for b in range(row_blocks):
-        near, far = (downs, ups_more) if b < half else (ups, downs_more)
-        total = mine[b, :, :, column].astype(f32) + near[b % half].astype(f32)
+    for b in range(2 * half):
+        own, near, far = parts[b // half * 3 : b // half * 3 + 3]
+        total = own[b % half].astype(f32) + near[b % half].astype(f32)
         total = total + far[b % half].astype(f32)
         held[b] = total.reshape(rows * cols, width)
         for c in range(cols):
@@ -121,17 +117,17 @@
             out[table[b * cols + c]] = piece.astype(out.dtype)
 
 
-def gather_pieces(table, mine, arrived, slots):
-    half, rows, cols, width = arrived[0].shape
+def gather_pieces(table, parts, slots):
+    half, rows, cols, width = parts[0].shape
     return pl.pallas_call(
         gather_kernel,
         out_shape=jax.ShapeDtypeStruct((slots, rows, width), bf16),
-        in_specs=[scalars] + [whole] * 5,
+        in_specs=[scalars] + [whole] * len(parts),
         out_specs=whole,
         scratch_shapes=[pltpu.VMEM((2 * half, rows * cols, width), f32)],
         compiler_params=params(6),
         name="sum_and_gather",
-    )(table, vmem(mine), *[vmem(a) for a in arrived])
+    )(table, *[vmem(x) for x in parts])
 
 
 def place_kernel(per_step, rows, cols, table, arrived, out, held):
@@ -450,7 +446,9 @@
     far = lax.dynamic_slice_in_dim(mine, far, width, axis=3)
     far_low, far_high = far[:half], far[half:]
     far_low, far_high = hop(far_low, 1), hop(far_high, -1)
-    near_high, near_low = windows(mine, width, ((half, 1), (0, 3)))
+    near_high, near_low, own_low, own_high, last_low, last_high = windows(
+        mine, width, ((half, 1), (0, 3), (0, 1), (half, 3), (0, 0), (half, 0))
+    )
     near_high, near_low = hop(near_high, 1), hop(near_low, -1)
 
     entries = jnp.arange(owner_list.shape[0], dtype=jnp.int32)
@@ -464,14 +462,14 @@
     owner = lax.axis_index(("dp", "shard"))
     count = jnp.sum((owner_list == owner).astype(jnp.int32)).reshape(1)
 
-    far_low = hop(merged(mine, 0, 1, far_low), 1)
-    far_high = hop(merged(mine, half, 3, far_high), -1)
+    far_low = hop(merged(own_low, far_low), 1)
+    far_high = hop(merged(own_high, far_high), -1)
     (first,) = early(count, (0, left_root, left_factor))
-    arrived = (near_high, near_low, far_low, far_high)
+    arrived = (last_low, near_low, far_low, last_high, near_high, far_high)
     arrived, first = lax.optimization_barrier((arrived, first))
 
     all_slots = replicas * shards * slots
-    outgoing = gather_pieces(table, mine, arrived, all_slots)
+    outgoing = gather_pieces(table, arrived, all_slots)
     incoming = lax.all_to_all(outgoing, ("dp", "shard"), split_axis=0, concat_axis=0, tiled=True)
     sides = ((left_root, left_factor), (right_root, right_factor))
     rest = [(t, *side) for t in range(slots) for side in sides][1:]

time: 89.5 us -> 89 us (level)
  Pallas kernels: 15.6 us -> 30.5 us
  waiting for transfers between devices: 41 us -> 29.8 us
  starting transfers between devices: 28.5 us -> 25.3 us
  local copies, waits for them, and re-layouts: 2.05 us -> 1.11 us
    pallas_call x2, Pallas kernels: 1.3 us -> 11.6 us  [early(): pl.pallas_call(functools.partial(early_kernel, [t for t, _, _ in items]),...]
    all_to_all x1, waiting for transfers between devices: 18.6 us -> 13.5 us  [body(): lax.all_to_all(outgoing, ('dp', 'shard'), split_axis=0, concat_axis=0, ti...]
    ppermute x6, waiting for transfers between devices: 9.87 us -> 5.5 us  [hop(): lax.ppermute(x, 'dp', [(i, (i + step) % replicas) for i in range(replicas)])]
    all_to_all x1, starting transfers between devices: 9.42 us -> 6.14 us  [body(): lax.all_to_all(outbound.reshape(all_slots, rows, width), ('dp', 'shard'),...]
    pallas_call x1, Pallas kernels: 1.75 us -> 4.99 us  [update_pieces(): pl.pallas_call(functools.partial(update_kernel, gain, slots), out_shape=s...]
    all_to_all x1, waiting for transfers between devices: 12.5 us -> 10.8 us  [body(): lax.all_to_all(outbound.reshape(all_slots, rows, width), ('dp', 'shard'),...]
    pallas_call x1, Pallas kernels: 6.79 us -> 8.53 us  [new_state(): pl.pallas_call(functools.partial(state_kernel, gain, slots), out_shape=(s...]
    slice x1, local copies, waits for them, and re-layouts: 2.01 us -> 1.08 us  [body(): far_low, far_high = (far[:half], far[half:])]
  transfers between devices with their start and end apart: 8 -> 8, of which waited for: 5 -> 4; matrix products, arithmetic and copies ran while one was open for 1% -> 1% of each run, Pallas kernels for 11% -> 25%
where the time goes in v7:
time: 89 us; the launch traced here: 88.4 us
  Pallas kernels  30.5 us (34%)
  waiting for transfers between devices  29.8 us (33%)
  starting transfers between devices  25.3 us (28%)
  local copies, waits for them, and re-layouts  1.11 us (1%)
  other arithmetic  0.94 us (1%)
    all_to_all x1, waiting for transfers between devices, body(): lax.all_to_all(outgoing, ('dp', 'shard'), split_axis=0, concat_axis=0, ti...  13.5 us
    pallas_call x2, Pallas kernels, early(): pl.pallas_call(functools.partial(early_kernel, [t for t, _, _ in items]),...  11.6 us
    all_to_all x1, waiting for transfers between devices, body(): lax.all_to_all(outbound.reshape(all_slots, rows, width), ('dp', 'shard'),...  10.8 us
    ppermute x6, starting transfers between devices, hop(): lax.ppermute(x, 'dp', [(i, (i + step) % replicas) for i in range(replicas)])  10.2 us
    all_to_all x1, starting transfers between devices, body(): lax.all_to_all(outgoing, ('dp', 'shard'), split_axis=0, concat_axis=0, ti...  8.93 us
    pallas_call x1, Pallas kernels, new_state(): pl.pallas_call(functools.partial(state_kernel, gain, slots), out_shape=(s...  8.53 us
    all_to_all x1, starting transfers between devices, body(): lax.all_to_all(outbound.reshape(all_slots, rows, width), ('dp', 'shard'),...  6.14 us
    ppermute x6, waiting for transfers between devices, hop(): lax.ppermute(x, 'dp', [(i, (i + step) % replicas) for i in range(replicas)])  5.5 us
  transfers between devices with their start and end apart: 8, of which 4 were waited for; matrix products, arithmetic and copies ran while one was open for 1% of the time, Pallas kernels for 25%

profile of v7, /device:TPU:1, one launch (start us, length us, event | category | flops | bytes accessed | tf_op | source)
XLA Modules:
  0.0 88.4 jit_solution(8824614836071593444)
XLA Ops:
  0.6 0.0 copy-start.5
  0.6 0.0 copy-start.6
  0.7 0.0 copy-start.4
  0.7 1.1 %dynamic-slice_bitcast_fusion = (bf16[4,16,16,128]{3,2,1,0:T(8,128)(2,1)S(1)}, bf16[4,16,16,128]{3,2,1,0:T(8,128)(2,1)S(1)}) fusion(bf16[1,8,16,16,512]{4,3,2,1,0:T(8,128)(2,1)} %param.8, s32[]{:T(128)S(6)} %add.22, s32[]{:T(128)S(6)} %select_n.18), kind=kLoop, calls=%fused_computation | loop fusion | bytes 1048584 | tf_op jit(solution)/shard_map/slice | solution.py:447
  1.8 4.7 %collective-permute-start.4 = (bf16[4,16,16,128]{3,2,1,0:T(8,128)(2,1)S(1)}, bf16[4,16,16,128]{3,2,1,0:T(8,128)(2,1)S(1)}, u32[]{:S(2)}, u32[]{:S(2)}) collective-permute-start(bf16[4,16,16,128]{3,2,1,0:T(8,128)(2,1)S(1)} %get-tuple-element.93), channel_id=1, source_target_pairs={{0,96},{32,0},{64,32},{96,64},{1,97},{33,1},{65,33},{97,65},{2,98}... | collective-permute-start | bytes 786440 | tf_op jit(solution)/shard_map/ppermute | solution.py:442
  6.4 0.0 collective-permute-start.1
  6.4 1.4 %windows.1 = (bf16[4,16,16,128]{3,2,1,0:T(8,128)(2,1)S(1)}, bf16[4,16,16,128]{3,2,1,0:T(8,128)(2,1)S(1)}, bf16[4,16,16,128]{3,2,1,0:T(8,128)(2,1)S(1)}, bf16[4,1...) custom-call(bf16[8,16,16,512]{3,2,1,0:T(8,128)(2,1)} %bitcast.11), custom_call_target="tpu_custom_call" | custom-call | tf_op jit(solution)/shard_map/windows/pallas_call | solution.py:79
  7.9 2.7 %collective-permute-start = (bf16[4,16,16,128]{3,2,1,0:T(8,128)(2,1)S(1)}, bf16[4,16,16,128]{3,2,1,0:T(8,128)(2,1)S(1)}, u32[]{:S(2)}, u32[]{:S(2)}) collective-permute-start(bf16[4,16,16,128]{3,2,1,0:T(8,128)(2,1)S(1)} %get-tuple-element.50), channel_id=1, source_target_pairs={{0,96},{32,0},{64,32},{96,64},{1,97},{33,1},{65,33},{97,65},{2,98}... | collective-permute-start | bytes 786440 | tf_op jit(solution)/shard_map/ppermute | solution.py:442
  10.6 0.0 collective-permute-start.3
  10.6 0.0 copy-done.5
  10.6 0.0 copy-done.6
  10.6 0.0 copy-done.4
  10.6 0.2 convert_reduce_fusion
  10.8 0.7 fusion.1
  11.5 3.0 %collective-permute-done.1.came = bf16[4,16,16,128]{3,2,1,0:T(8,128)(2,1)S(1)} collective-permute-done((bf16[4,16,16,128]{3,2,1,0:T(8,128)(2,1)S(1)}, bf16[4,16,16,128]{3,2,1,0:T(8,128)(2,1)S(1)}, u32[]{:S(2)}, u32[]{:S(2)}) %collective-permute-start.1) | collective-permute-done | bytes 262176 | tf_op jit(solution)/shard_map/ppermute | solution.py:442
  14.5 0.1 merge_far_part.2
  14.5 0.1 collective-permute-start.2
  14.6 0.0 collective-permute-done.4.came
  14.6 0.1 merge_far_part.3
  14.7 2.7 %collective-permute-start.5 = (bf16[4,16,16,128]{3,2,1,0:T(8,128)(2,1)S(1)}, bf16[4,16,16,128]{3,2,1,0:T(8,128)(2,1)S(1)}, u32[]{:S(2)}, u32[]{:S(2)}) collective-permute-start(bf16[4,16,16,128]{3,2,1,0:T(8,128)(2,1)S(1)} %merge_far_part.3), channel_id=1, source_target_pairs={{0,96},{32,0},{64,32},{96,64},{1,97},{33,1},{65,33},{97,65},{2,98}... | collective-permute-start | bytes 786440 | tf_op jit(solution)/shard_map/ppermute | solution.py:442
  17.4 0.1 select_reduce_fusion.table
  17.5 5.8 %early_products.2 = (bf16[512,512]{1,0:T(8,128)(2,1)S(1)}, bf16[512,512]{1,0:T(8,128)(2,1)}, bf16[512,512]{1,0:T(8,128)(2,1)}) custom-call(s32[1]{0:T(128)} %bitcast.count, f32[2,512,512]{2,1,0:T(8,128)} %xl.3, f32[2,512,512]{2,1,0:T(8,128)} %left.1), custom_call_target="tpu_custom_call" | custom-call | flops 2415919104 | bytes 3145728 | tf_op jit(solution)/shard_map/early_products/pallas_call | solution.py:207
  23.3 0.0 copy-start
  23.3 0.0 collective-permute-done.refs_1_
  23.3 0.0 collective-permute-done.3.refs_4_
  23.3 2.5 %collective-permute-done.2.refs_2_ = bf16[4,16,16,128]{3,2,1,0:T(8,128)(2,1)S(1)} collective-permute-done((bf16[4,16,16,128]{3,2,1,0:T(8,128)(2,1)S(1)}, bf16[4,16,16,128]{3,2,1,0:T(8,128)(2,1)S(1)}, u32[]{:S(2)}, u32[]{:S(2)}) %collective-permute-start.2) | collective-permute-done | bytes 262176 | tf_op jit(solution)/shard_map/ppermute | solution.py:442
  25.8 0.0 collective-permute-done.5.refs_5_
  25.8 2.1 %sum_and_gather.1 = bf16[256,16,128]{2,1,0:T(8,128)(2,1)} custom-call(s32[128]{0:T(128)S(1)} %select_reduce_fusion.table, bf16[4,16,16,128]{3,2,1,0:T(8,128)(2,1)S(1)} %get-tuple-element.58.refs_0_, bf16[4,16,16,128]{3,2,1,0:T(8,128)(2,1)S(1)} %collective-permute-done.refs_1_, bf16[4,16,16,128]{3,2,1,0:T(8,128)(2,1)S(1)} %collective-permute-done.2.refs_2_, ...), custom_call_target="tpu_custom_call" | custom-call | tf_op jit(solution)/shard_map/sum_and_gather/pallas_call | solution.py:122
  27.9 8.9 %all-to-all-start = ((bf16[256,16,128]{2,1,0:T(8,128)(2,1)}), bf16[256,16,128]{2,1,0:T(8,128)(2,1)S(1)}, u32[]{:S(2)}, u32[]{:S(2)}) async-start(bf16[256,16,128]{2,1,0:T(8,128)(2,1)} %sum_and_gather.1), calls=%async_computation | async-start | bytes 2097152 | tf_op jit(solution)/shard_map/all_to_all | solution.py:473
  36.9 5.8 %early_products.3 = (bf16[512,512]{1,0:T(8,128)(2,1)S(1)}, bf16[512,512]{1,0:T(8,128)(2,1)}, bf16[512,512]{1,0:T(8,128)(2,1)}, bf16[512,512]{1,0:T(8,128)(2,1)S(...) custom-call(s32[1]{0:T(128)} %bitcast.count, ...), custom_call_target="tpu_custom_call" | custom-call | flops 7247757312 | bytes 9437184 | tf_op jit(solution)/shard_map/early_products/pallas_call | solution.py:207
  42.7 0.0 copy-start.1
  42.7 0.0 copy-start.2
  42.7 0.0 copy-start.3
  42.7 13.5 %all-to-all-done = bf16[256,16,128]{2,1,0:T(8,128)(2,1)S(1)} async-done(((bf16[256,16,128]{2,1,0:T(8,128)(2,1)}), bf16[256,16,128]{2,1,0:T(8,128)(2,1)S(1)}, u32[]{:S(2)}, u32[]{:S(2)}) %all-to-all-start) | async-done | bytes 1048608 | tf_op jit(solution)/shard_map/all_to_all | solution.py:473
  56.2 0.0 copy-done
  56.2 5.0 %update_pieces.1 = bf16[4,32,2,16,128]{4,3,2,1,0:T(8,128)(2,1)} custom-call(s32[1]{0:T(128)} %bitcast.count, bf16[4,32,2,16,128]{4,3,2,1,0:T(8,128)(2,1)S(1)} %bitcast.8, f32[2,512,512]{2,1,0:T(8,128)} %xl.3, f32[2,512,512]{2,1,0:T(8,128)} %xr.3, bf16[512,512]{1,0:T(8,128)(2,1)S(1)} %get-tuple-element.77.refs_0_, ...), custom_call_target="tpu_custom_call" | custom-call | tf_op jit(solution)/shard_map/update_pieces/pallas_call | solution.py:331
  61.2 0.0 copy-done.1
  61.2 0.0 copy-done.2
  61.2 0.0 copy-done.3
  61.2 6.1 %all-to-all-start.1 = ((bf16[256,16,128]{2,1,0:T(8,128)(2,1)}), bf16[256,16,128]{2,1,0:T(8,128)(2,1)S(1)}, u32[]{:S(2)}, u32[]{:S(2)}) async-start(bf16[256,16,128]{2,1,0:T(8,128)(2,1)} %bitcast.10), calls=%async_computation.1 | async-start | bytes 2097152 | tf_op jit(solution)/shard_map/all_to_all | solution.py:482
  67.4 8.5 %new_state.1 = (f32[2,512,512]{2,1,0:T(8,128)}, f32[2,512,512]{2,1,0:T(8,128)}, f32[2,512,512]{2,1,0:T(8,128)}, f32[2,512,512]{2,1,0:T(8,128)}) custom-call(s32[1]{0:T(128)} %bitcast.count, bf16[4,32,2,16,128]{4,3,2,1,0:T(8,128)(2,1)S(1)} %bitcast.9, f32[2,512,512]{2,1,0:T(8,128)} %left.1, f32[2,512,512]{2,1,0:T(8,128)} %right.1, f32[2,512,512]{2,1,0:T(8,128)} %xl.3, ...), custom_call_target="tpu_custom_call" | custom-call | flops 4294967296 | bytes 18874368 | tf_op jit(solution)/shard_map/new_state/pallas_call | solution.py:408
  75.9 10.8 %all-to-all-done.1.arrived = bf16[256,16,128]{2,1,0:T(8,128)(2,1)S(1)} async-done(((bf16[256,16,128]{2,1,0:T(8,128)(2,1)}), bf16[256,16,128]{2,1,0:T(8,128)(2,1)S(1)}, u32[]{:S(2)}, u32[]{:S(2)}) %all-to-all-start.1) | async-done | bytes 1048608 | tf_op jit(solution)/shard_map/all_to_all | solution.py:482
  86.7 1.7 %place_pieces.1 = bf16[8,16,16,128]{3,2,1,0:T(8,128)(2,1)} custom-call(s32[128]{0:T(128)S(1)} %select_reduce_fusion.table, bf16[256,16,128]{2,1,0:T(8,128)(2,1)S(1)} %all-to-all-done.1.arrived), custom_call_target="tpu_custom_call" | custom-call | tf_op jit(solution)/shard_map/place_pieces/pallas_call | solution.py:145
  (1 shorter events, 0.0 us)
Async XLA Ops:
  0.6 10.0 %copy-start.5 = (s32[128]{0:T(128)S(1)}, s32[128]{0:T(128)}, u32[]{:S(2)}) copy-start(s32[128]{0:T(128)} %param.11) | copy-start | bytes 1540
  0.6 10.0 %copy-start.6 = (s32[128]{0:T(128)S(1)}, s32[128]{0:T(128)}, u32[]{:S(2)}) copy-start(s32[128]{0:T(128)} %param.10) | copy-start | bytes 1540
  0.7 10.0 %copy-start.4 = (s32[128]{0:T(128)S(1)}, s32[128]{0:T(128)}, u32[]{:S(2)}) copy-start(s32[128]{0:T(128)} %param.9) | copy-start | bytes 1540
  1.8 12.9 %collective-permute-start.4 = (bf16[4,16,16,128]{3,2,1,0:T(8,128)(2,1)S(1)}, bf16[4,16,16,128]{3,2,1,0:T(8,128)(2,1)S(1)}, u32[]{:S(2)}, u32[]{:S(2)}) collective-permute-start(bf16[4,16,16,128]{3,2,1,0:T(8,128)(2,1)S(1)} %get-tuple-element.93), channel_id=1, source_target_pairs={{0,96},{32,0},{64,32},{96,64},{1,97},{33,1},{65,33},{97,65},{2,98}... | collective-permute-start | bytes 786440 | tf_op jit(solution)/shard_map/ppermute | solution.py:442
  6.4 8.1 %collective-permute-start.1 = (bf16[4,16,16,128]{3,2,1,0:T(8,128)(2,1)S(1)}, bf16[4,16,16,128]{3,2,1,0:T(8,128)(2,1)S(1)}, u32[]{:S(2)}, u32[]{:S(2)}) collective-permute-start(bf16[4,16,16,128]{3,2,1,0:T(8,128)(2,1)S(1)} %get-tuple-element.94), channel_id=1, source_target_pairs={{0,32},{32,64},{64,96},{96,0},{1,33},{33,65},{65,97},{97,1},{2,34}... | collective-permute-start | bytes 786440 | tf_op jit(solution)/shard_map/ppermute | solution.py:442
  7.9 15.4 %collective-permute-start = (bf16[4,16,16,128]{3,2,1,0:T(8,128)(2,1)S(1)}, bf16[4,16,16,128]{3,2,1,0:T(8,128)(2,1)S(1)}, u32[]{:S(2)}, u32[]{:S(2)}) collective-permute-start(bf16[4,16,16,128]{3,2,1,0:T(8,128)(2,1)S(1)} %get-tuple-element.50), channel_id=1, source_target_pairs={{0,96},{32,0},{64,32},{96,64},{1,97},{33,1},{65,33},{97,65},{2,98}... | collective-permute-start | bytes 786440 | tf_op jit(solution)/shard_map/ppermute | solution.py:442
  10.6 12.7 %collective-permute-start.3 = (bf16[4,16,16,128]{3,2,1,0:T(8,128)(2,1)S(1)}, bf16[4,16,16,128]{3,2,1,0:T(8,128)(2,1)S(1)}, u32[]{:S(2)}, u32[]{:S(2)}) collective-permute-start(bf16[4,16,16,128]{3,2,1,0:T(8,128)(2,1)S(1)} %get-tuple-element.53), channel_id=1, source_target_pairs={{0,32},{32,64},{64,96},{96,0},{1,33},{33,65},{65,97},{97,1},{2,34}... | collective-permute-start | bytes 786440 | tf_op jit(solution)/shard_map/ppermute | solution.py:442
  14.5 11.3 %collective-permute-start.2 = (bf16[4,16,16,128]{3,2,1,0:T(8,128)(2,1)S(1)}, bf16[4,16,16,128]{3,2,1,0:T(8,128)(2,1)S(1)}, u32[]{:S(2)}, u32[]{:S(2)}) collective-permute-start(bf16[4,16,16,128]{3,2,1,0:T(8,128)(2,1)S(1)} %merge_far_part.2), channel_id=1, source_target_pairs={{0,32},{32,64},{64,96},{96,0},{1,33},{33,65},{65,97},{97,1},{2,34}... | collective-permute-start | bytes 786440 | tf_op jit(solution)/shard_map/ppermute | solution.py:442
  14.7 11.1 %collective-permute-start.5 = (bf16[4,16,16,128]{3,2,1,0:T(8,128)(2,1)S(1)}, bf16[4,16,16,128]{3,2,1,0:T(8,128)(2,1)S(1)}, u32[]{:S(2)}, u32[]{:S(2)}) collective-permute-start(bf16[4,16,16,128]{3,2,1,0:T(8,128)(2,1)S(1)} %merge_far_part.3), channel_id=1, source_target_pairs={{0,96},{32,0},{64,32},{96,64},{1,97},{33,1},{65,33},{97,65},{2,98}... | collective-permute-start | bytes 786440 | tf_op jit(solution)/shard_map/ppermute | solution.py:442
  23.3 32.9 %copy-start = (bf16[512,512]{1,0:T(8,128)(2,1)}, bf16[512,512]{1,0:T(8,128)(2,1)S(1)}, u32[]{:S(2)}) copy-start(bf16[512,512]{1,0:T(8,128)(2,1)S(1)} %get-tuple-element.77.refs_0_) | copy-start | bytes 1572868
  27.9 28.3 %all-to-all-start = ((bf16[256,16,128]{2,1,0:T(8,128)(2,1)}), bf16[256,16,128]{2,1,0:T(8,128)(2,1)S(1)}, u32[]{:S(2)}, u32[]{:S(2)}) async-start(bf16[256,16,128]{2,1,0:T(8,128)(2,1)} %sum_and_gather.1), calls=%async_computation | async-start | bytes 2097152 | tf_op jit(solution)/shard_map/all_to_all | solution.py:473
  42.7 18.5 %copy-start.1 = (bf16[512,512]{1,0:T(8,128)(2,1)}, bf16[512,512]{1,0:T(8,128)(2,1)S(1)}, u32[]{:S(2)}) copy-start(bf16[512,512]{1,0:T(8,128)(2,1)S(1)} %get-tuple-element.79.refs_2_) | copy-start | bytes 1572868
  42.7 18.5 %copy-start.2 = (bf16[512,512]{1,0:T(8,128)(2,1)}, bf16[512,512]{1,0:T(8,128)(2,1)S(1)}, u32[]{:S(2)}) copy-start(bf16[512,512]{1,0:T(8,128)(2,1)S(1)} %get-tuple-element.81.refs_4_) | copy-start | bytes 1572868
  42.7 18.5 %copy-start.3 = (bf16[512,512]{1,0:T(8,128)(2,1)}, bf16[512,512]{1,0:T(8,128)(2,1)S(1)}, u32[]{:S(2)}) copy-start(bf16[512,512]{1,0:T(8,128)(2,1)S(1)} %get-tuple-element.83.refs_6_) | copy-start | bytes 1572868
  61.2 25.5 %all-to-all-start.1 = ((bf16[256,16,128]{2,1,0:T(8,128)(2,1)}), bf16[256,16,128]{2,1,0:T(8,128)(2,1)S(1)}, u32[]{:S(2)}, u32[]{:S(2)}) async-start(bf16[256,16,128]{2,1,0:T(8,128)(2,1)} %bitcast.10), calls=%async_computation.1 | async-start | bytes 2097152 | tf_op jit(solution)/shard_map/all_to_all | solution.py:482

commit v8 on v7

--- a/solution.py
+++ b/solution.py
@@ -55,18 +55,22 @@
 in_place = pl.BlockSpec(memory_space=pl.ANY)
 
 
+def direction(index):
+    return 1 - 2 * lax.rem(index, 2)
+
+
 def column_at(hop, width):
     replicas = lax.axis_size("dp")
-    z = lax.rem(lax.axis_index("dp").astype(jnp.int32) + hop, replicas)
+    way = direction(lax.axis_index("shard").astype(jnp.int32))
+    z = lax.rem(lax.axis_index("dp").astype(jnp.int32) + way * hop + replicas, replicas)
     return pl.ds(pl.multiple_of(z * width, width), width)
 
 
-def window_kernel(parts, mine, *refs):
+def window_kernel(hops, mine, *refs):
     outs, sem = refs[:-1], refs[-1]
     copies = []
-    for k, ((low, hop), out) in enumerate(zip(parts, outs)):
-        half, width = out.shape[0], out.shape[-1]
-        source = mine.at[low : low + half, :, :, column_at(hop, width)]
+    for k, (hop, out) in enumerate(zip(hops, outs)):
+        source = mine.at[:, :, :, column_at(hop, out.shape[-1])]
         copies.append(pltpu.make_async_copy(source, out, sem.at[k]))
     for copy in copies:
         copy.start()
@@ -74,14 +78,14 @@
         copy.wait()
 
 
-def windows(mine, width, parts):
+def windows(mine, width, hops):
     row_blocks, rows, cols, _ = mine.shape
     return pl.pallas_call(
-        functools.partial(window_kernel, parts),
-        out_shape=(pltpu.VMEM((row_blocks // 2, rows, cols, width), bf16),) * len(parts),
+        functools.partial(window_kernel, hops),
+        out_shape=(pltpu.VMEM((row_blocks, rows, cols, width), bf16),) * len(hops),
         in_specs=[in_place],
-        out_specs=(whole,) * len(parts),
-        scratch_shapes=[pltpu.SemaphoreType.DMA((len(parts),))],
+        out_specs=(whole,) * len(hops),
+        scratch_shapes=[pltpu.SemaphoreType.DMA((len(hops),))],
         compiler_params=params(4),
         name="windows",
     )(hbm(mine))
@@ -103,14 +107,11 @@
     )(vmem(own), vmem(came))
 
 
-def gather_kernel(table, *refs):
-    parts, (out, held) = refs[:6], refs[6:]
-    half, rows, cols, width = parts[0].shape
+def gather_kernel(table, own, near, far, out, held):
+    row_blocks, rows, cols, width = own.shape
     out[...] = jnp.zeros_like(out)
-    for b in range(2 * half):
-        own, near, far = parts[b // half * 3 : b // half * 3 + 3]
-        total = own[b % half].astype(f32) + near[b % half].astype(f32)
-        total = total + far[b % half].astype(f32)
+    for b in range(row_blocks):
+        total = own[b].astype(f32) + near[b].astype(f32) + far[b].astype(f32)
         held[b] = total.reshape(rows * cols, width)
         for c in range(cols):
             piece = held[b, pl.ds(c, rows, stride=cols), :]
@@ -118,13 +119,13 @@
 
 
 def gather_pieces(table, parts, slots):
-    half, rows, cols, width = parts[0].shape
+    row_blocks, rows, cols, width = parts[0].shape
     return pl.pallas_call(
         gather_kernel,
         out_shape=jax.ShapeDtypeStruct((slots, rows, width), bf16),
         in_specs=[scalars] + [whole] * len(parts),
         out_specs=whole,
-        scratch_shapes=[pltpu.VMEM((2 * half, rows * cols, width), f32)],
+        scratch_shapes=[pltpu.VMEM((row_blocks, rows * cols, width), f32)],
         compiler_params=params(6),
         name="sum_and_gather",
     )(table, *[vmem(x) for x in parts])
@@ -438,18 +439,19 @@
     gain = (1.0 - decay_rate) / n
     mine = gradients[0]
 
-    def hop(x, step):
-        return lax.ppermute(x, "dp", [(i, (i + step) % replicas) for i in range(replicas)])
-
-    half = row_blocks // 2
-    far = lax.rem(lax.axis_index("dp") + 2, replicas) * width
-    far = lax.dynamic_slice_in_dim(mine, far, width, axis=3)
-    far_low, far_high = far[:half], far[half:]
-    far_low, far_high = hop(far_low, 1), hop(far_high, -1)
-    near_high, near_low, own_low, own_high, last_low, last_high = windows(
-        mine, width, ((half, 1), (0, 3), (0, 1), (half, 3), (0, 0), (half, 0))
-    )
-    near_high, near_low = hop(near_high, 1), hop(near_low, -1)
+    def hop(x, way):
+        pairs = []
+        for z in range(replicas):
+            for shard in range(shards):
+                to = (z + way * direction_of[shard % 2]) % replicas
+                pairs.append((z * shards + shard, to * shards + shard))
+        return lax.ppermute(x, ("dp", "shard"), pairs)
+
+    direction_of = (1, -1)
+    column = lax.rem(lax.axis_index("dp") + replicas // 2, replicas) * width
+    far = hop(lax.dynamic_slice_in_dim(mine, column, width, axis=3), 1)
+    near, ahead, own = windows(mine, width, (-1, 1, 0))
+    near = hop(near, -1)
 
     entries = jnp.arange(owner_list.shape[0], dtype=jnp.int32)
     same = owner_list[None, :] == owner_list[:, None]
@@ -462,11 +464,9 @@
     owner = lax.axis_index(("dp", "shard"))
     count = jnp.sum((owner_list == owner).astype(jnp.int32)).reshape(1)
 
-    far_low = hop(merged(own_low, far_low), 1)
-    far_high = hop(merged(own_high, far_high), -1)
+    far = hop(merged(ahead, far), 1)
     (first,) = early(count, (0, left_root, left_factor))
-    arrived = (last_low, near_low, far_low, last_high, near_high, far_high)
-    arrived, first = lax.optimization_barrier((arrived, first))
+    arrived, first = lax.optimization_barrier(((own, near, far), first))
 
     all_slots = replicas * shards * slots
     outgoing = gather_pieces(table, arrived, all_slots)

time: 89 us -> 91.8 us (1.031)
  Pallas kernels: 30.5 us -> 15.7 us
  waiting for transfers between devices: 29.8 us -> 42.9 us
  starting transfers between devices: 25.3 us -> 30 us
    pallas_call x2, Pallas kernels: 11.6 us -> 1.55 us  [early(): pl.pallas_call(functools.partial(early_kernel, [t for t, _, _ in items]),...]
    ppermute x6 -> x3, waiting for transfers between devices: 5.5 us -> 11.8 us  [hop(): return lax.ppermute(x, ('dp', 'shard'), pairs)]
    all_to_all x1, waiting for transfers between devices: 13.5 us -> 18.5 us  [body(): lax.all_to_all(outgoing, ('dp', 'shard'), split_axis=0, concat_axis=0, ti...]
    all_to_all x1, starting transfers between devices: 6.14 us -> 9.82 us  [body(): lax.all_to_all(outbound.reshape(all_slots, rows, width), ('dp', 'shard'),...]
    pallas_call x1, Pallas kernels: 4.99 us -> 1.87 us  [update_pieces(): pl.pallas_call(functools.partial(update_kernel, gain, slots), out_shape=s...]
    all_to_all x1, starting transfers between devices: 8.93 us -> 11.9 us  [body(): lax.all_to_all(outgoing, ('dp', 'shard'), split_axis=0, concat_axis=0, ti...]
    ppermute x6 -> x3, starting transfers between devices: 10.2 us -> 8.21 us  [hop(): return lax.ppermute(x, ('dp', 'shard'), pairs)]
    all_to_all x1, waiting for transfers between devices: 10.8 us -> 12.6 us  [body(): lax.all_to_all(outbound.reshape(all_slots, rows, width), ('dp', 'shard'),...]
  transfers between devices with their start and end apart: 8 -> 5, of which waited for: 4 -> 4; matrix products, arithmetic and copies ran while one was open for 1% -> 1% of each run, Pallas kernels for 25% -> 11%
where the time goes in v8:
time: 91.8 us; the launch traced here: 91.5 us
  waiting for transfers between devices  42.9 us (47%)
  starting transfers between devices  30 us (33%)
  Pallas kernels  15.7 us (17%)
  local copies, waits for them, and re-layouts  1.11 us (1%)
  other arithmetic  0.98 us (1%)
    all_to_all x1, waiting for transfers between devices, body(): lax.all_to_all(outgoing, ('dp', 'shard'), split_axis=0, concat_axis=0, ti...  18.5 us
    all_to_all x1, waiting for transfers between devices, body(): lax.all_to_all(outbound.reshape(all_slots, rows, width), ('dp', 'shard'),...  12.6 us
    all_to_all x1, starting transfers between devices, body(): lax.all_to_all(outgoing, ('dp', 'shard'), split_axis=0, concat_axis=0, ti...  11.9 us
    ppermute x3, waiting for transfers between devices, hop(): return lax.ppermute(x, ('dp', 'shard'), pairs)  11.8 us
    all_to_all x1, starting transfers between devices, body(): lax.all_to_all(outbound.reshape(all_slots, rows, width), ('dp', 'shard'),...  9.82 us
    ppermute x3, starting transfers between devices, hop(): return lax.ppermute(x, ('dp', 'shard'), pairs)  8.21 us
    pallas_call x1, Pallas kernels, new_state(): pl.pallas_call(functools.partial(state_kernel, gain, slots), out_shape=(s...  6.92 us
    pallas_call x1, Pallas kernels, gather_pieces(): pl.pallas_call(gather_kernel, out_shape=jax.ShapeDtypeStruct((slots, rows...  2.1 us
  transfers between devices with their start and end apart: 5, of which 4 were waited for; matrix products, arithmetic and copies ran while one was open for 1% of the time, Pallas kernels for 11%

profile of v8, /device:TPU:1, one launch (start us, length us, event | category | flops | bytes accessed | tf_op | source)
XLA Modules:
  0.0 91.5 jit_solution(14494664007118023504)
XLA Ops:
  0.6 0.0 copy-start.4
  0.6 0.0 copy-start.5
  0.7 0.0 copy-start.6
  0.7 1.1 %dynamic-slice_bitcast_fusion = bf16[8,16,16,128]{3,2,1,0:T(8,128)(2,1)S(1)} fusion(bf16[1,8,16,16,512]{4,3,2,1,0:T(8,128)(2,1)} %param.8, s32[]{:T(128)S(6)} %select_n.18), kind=kLoop, calls=%fused_computation | loop fusion | bytes 1048580 | tf_op jit(solution)/shard_map/dynamic_slice | solution.py:452
  1.8 4.7 %collective-permute-start.1 = (bf16[8,16,16,128]{3,2,1,0:T(8,128)(2,1)S(1)}, bf16[8,16,16,128]{3,2,1,0:T(8,128)(2,1)S(1)}, u32[]{:S(2)}, u32[]{:S(2)}) collective-permute-start(bf16[8,16,16,128]{3,2,1,0:T(8,128)(2,1)S(1)} %dynamic-slice_bitcast_fusion), channel_id=1, source_target_pairs={{0,32},{1,97},{2,34},{3,99},{4,36},{5,101},{6,38},{7,103},{8,40},{... | collective-permute-start | bytes 1572872 | tf_op jit(solution)/shard_map/ppermute | solution.py:448
  6.4 1.4 %windows.1 = (bf16[8,16,16,128]{3,2,1,0:T(8,128)(2,1)S(1)}, bf16[8,16,16,128]{3,2,1,0:T(8,128)(2,1)S(1)}, bf16[8,16,16,128]{3,2,1,0:T(8,128)(2,1)S(1)}) custom-call(bf16[8,16,16,512]{3,2,1,0:T(8,128)(2,1)} %bitcast.9), custom_call_target="tpu_custom_call" | custom-call | tf_op jit(solution)/shard_map/windows/pallas_call | solution.py:83
  7.8 0.1 collective-permute-start
  7.9 0.0 copy-done.4
  7.9 0.2 convert_reduce_fusion
  8.1 0.0 copy-done.5
  8.1 0.0 copy-done.6
  8.2 7.3 %collective-permute-done.1.came = bf16[8,16,16,128]{3,2,1,0:T(8,128)(2,1)S(1)} collective-permute-done((bf16[8,16,16,128]{3,2,1,0:T(8,128)(2,1)S(1)}, bf16[8,16,16,128]{3,2,1,0:T(8,128)(2,1)S(1)}, u32[]{:S(2)}, u32[]{:S(2)}) %collective-permute-start.1) | collective-permute-done | bytes 524320 | tf_op jit(solution)/shard_map/ppermute | solution.py:448
  15.4 0.1 merge_far_part.1
  15.6 3.5 %collective-permute-start.2 = (bf16[8,16,16,128]{3,2,1,0:T(8,128)(2,1)S(1)}, bf16[8,16,16,128]{3,2,1,0:T(8,128)(2,1)S(1)}, u32[]{:S(2)}, u32[]{:S(2)}) collective-permute-start(bf16[8,16,16,128]{3,2,1,0:T(8,128)(2,1)S(1)} %merge_far_part.1), channel_id=1, source_target_pairs={{0,32},{1,97},{2,34},{3,99},{4,36},{5,101},{6,38},{7,103},{8,40},{... | collective-permute-start | bytes 1572872 | tf_op jit(solution)/shard_map/ppermute | solution.py:448
  19.0 0.7 fusion.1
  19.7 0.1 select_reduce_fusion.table
  19.8 0.7 early_products.2
  20.6 0.0 copy-start
  20.6 0.0 collective-permute-done.near
  20.6 4.6 %collective-permute-done.2.far = bf16[8,16,16,128]{3,2,1,0:T(8,128)(2,1)S(1)} collective-permute-done((bf16[8,16,16,128]{3,2,1,0:T(8,128)(2,1)S(1)}, bf16[8,16,16,128]{3,2,1,0:T(8,128)(2,1)S(1)}, u32[]{:S(2)}, u32[]{:S(2)}) %collective-permute-start.2) | collective-permute-done | bytes 524320 | tf_op jit(solution)/shard_map/ppermute | solution.py:448
  25.2 2.1 %sum_and_gather.1 = bf16[256,16,128]{2,1,0:T(8,128)(2,1)} custom-call(s32[128]{0:T(128)S(1)} %select_reduce_fusion.table, bf16[8,16,16,128]{3,2,1,0:T(8,128)(2,1)S(1)} %get-tuple-element.49.own, bf16[8,16,16,128]{3,2,1,0:T(8,128)(2,1)S(1)} %collective-permute-done.near, bf16[8,16,16,128]{3,2,1,0:T(8,128)(2,1)S(1)} %collective-permute-done.2.far), custom_call_target="tpu_custom_call" | custom-call | tf_op jit(solution)/shard_map/sum_and_gather/pallas_call | solution.py:123
  27.3 11.9 %all-to-all-start = ((bf16[256,16,128]{2,1,0:T(8,128)(2,1)}), bf16[256,16,128]{2,1,0:T(8,128)(2,1)S(1)}, u32[]{:S(2)}, u32[]{:S(2)}) async-start(bf16[256,16,128]{2,1,0:T(8,128)(2,1)} %sum_and_gather.1), calls=%async_computation | async-start | bytes 2097152 | tf_op jit(solution)/shard_map/all_to_all | solution.py:473
  39.2 0.8 early_products.3
  40.0 0.0 copy-start.1
  40.0 0.0 copy-start.2
  40.1 0.0 copy-start.3
  40.1 18.5 %all-to-all-done = bf16[256,16,128]{2,1,0:T(8,128)(2,1)S(1)} async-done(((bf16[256,16,128]{2,1,0:T(8,128)(2,1)}), bf16[256,16,128]{2,1,0:T(8,128)(2,1)S(1)}, u32[]{:S(2)}, u32[]{:S(2)}) %all-to-all-start) | async-done | bytes 1048608 | tf_op jit(solution)/shard_map/all_to_all | solution.py:473
  58.6 0.0 copy-done
  58.6 1.9 %update_pieces.1 = bf16[4,32,2,16,128]{4,3,2,1,0:T(8,128)(2,1)} custom-call(s32[1]{0:T(128)} %bitcast.count, bf16[4,32,2,16,128]{4,3,2,1,0:T(8,128)(2,1)S(1)} %bitcast.6, f32[2,512,512]{2,1,0:T(8,128)} %xl.3, f32[2,512,512]{2,1,0:T(8,128)} %xr.3, bf16[512,512]{1,0:T(8,128)(2,1)S(1)} %get-tuple-element.65.refs_0_, ...), custom_call_target="tpu_custom_call" | custom-call | tf_op jit(solution)/shard_map/update_pieces/pallas_call | solution.py:332
  60.4 0.0 copy-done.1
  60.4 0.0 copy-done.2
  60.5 0.0 copy-done.3
  60.5 9.8 %all-to-all-start.1 = ((bf16[256,16,128]{2,1,0:T(8,128)(2,1)}), bf16[256,16,128]{2,1,0:T(8,128)(2,1)S(1)}, u32[]{:S(2)}, u32[]{:S(2)}) async-start(bf16[256,16,128]{2,1,0:T(8,128)(2,1)} %bitcast.8), calls=%async_computation.1 | async-start | bytes 2097152 | tf_op jit(solution)/shard_map/all_to_all | solution.py:482
  70.3 6.9 %new_state.1 = (f32[2,512,512]{2,1,0:T(8,128)}, f32[2,512,512]{2,1,0:T(8,128)}, f32[2,512,512]{2,1,0:T(8,128)}, f32[2,512,512]{2,1,0:T(8,128)}) custom-call(s32[1]{0:T(128)} %bitcast.count, bf16[4,32,2,16,128]{4,3,2,1,0:T(8,128)(2,1)S(1)} %bitcast.7, f32[2,512,512]{2,1,0:T(8,128)} %left.1, f32[2,512,512]{2,1,0:T(8,128)} %right.1, f32[2,512,512]{2,1,0:T(8,128)} %xl.3, ...), custom_call_target="tpu_custom_call" | custom-call | flops 4294967296 | bytes 18874368 | tf_op jit(solution)/shard_map/new_state/pallas_call | solution.py:409
  77.2 12.6 %all-to-all-done.1.arrived = bf16[256,16,128]{2,1,0:T(8,128)(2,1)S(1)} async-done(((bf16[256,16,128]{2,1,0:T(8,128)(2,1)}), bf16[256,16,128]{2,1,0:T(8,128)(2,1)S(1)}, u32[]{:S(2)}, u32[]{:S(2)}) %all-to-all-start.1) | async-done | bytes 1048608 | tf_op jit(solution)/shard_map/all_to_all | solution.py:482
  89.8 1.7 %place_pieces.1 = bf16[8,16,16,128]{3,2,1,0:T(8,128)(2,1)} custom-call(s32[128]{0:T(128)S(1)} %select_reduce_fusion.table, bf16[256,16,128]{2,1,0:T(8,128)(2,1)S(1)} %all-to-all-done.1.arrived), custom_call_target="tpu_custom_call" | custom-call | tf_op jit(solution)/shard_map/place_pieces/pallas_call | solution.py:146
  (1 shorter events, 0.0 us)
Async XLA Ops:
  0.6 7.3 %copy-start.4 = (s32[128]{0:T(128)S(1)}, s32[128]{0:T(128)}, u32[]{:S(2)}) copy-start(s32[128]{0:T(128)} %param.9) | copy-start | bytes 1540
  0.6 7.5 %copy-start.5 = (s32[128]{0:T(128)S(1)}, s32[128]{0:T(128)}, u32[]{:S(2)}) copy-start(s32[128]{0:T(128)} %param.11) | copy-start | bytes 1540
  0.7 7.5 %copy-start.6 = (s32[128]{0:T(128)S(1)}, s32[128]{0:T(128)}, u32[]{:S(2)}) copy-start(s32[128]{0:T(128)} %param.10) | copy-start | bytes 1540
  1.8 13.7 %collective-permute-start.1 = (bf16[8,16,16,128]{3,2,1,0:T(8,128)(2,1)S(1)}, bf16[8,16,16,128]{3,2,1,0:T(8,128)(2,1)S(1)}, u32[]{:S(2)}, u32[]{:S(2)}) collective-permute-start(bf16[8,16,16,128]{3,2,1,0:T(8,128)(2,1)S(1)} %dynamic-slice_bitcast_fusion), channel_id=1, source_target_pairs={{0,32},{1,97},{2,34},{3,99},{4,36},{5,101},{6,38},{7,103},{8,40},{... | collective-permute-start | bytes 1572872 | tf_op jit(solution)/shard_map/ppermute | solution.py:448
  7.8 12.8 %collective-permute-start = (bf16[8,16,16,128]{3,2,1,0:T(8,128)(2,1)S(1)}, bf16[8,16,16,128]{3,2,1,0:T(8,128)(2,1)S(1)}, u32[]{:S(2)}, u32[]{:S(2)}) collective-permute-start(bf16[8,16,16,128]{3,2,1,0:T(8,128)(2,1)S(1)} %get-tuple-element.44), channel_id=1, source_target_pairs={{0,96},{1,33},{2,98},{3,35},{4,100},{5,37},{6,102},{7,39},{8,104},... | collective-permute-start | bytes 1572872 | tf_op jit(solution)/shard_map/ppermute | solution.py:448
  15.6 9.6 %collective-permute-start.2 = (bf16[8,16,16,128]{3,2,1,0:T(8,128)(2,1)S(1)}, bf16[8,16,16,128]{3,2,1,0:T(8,128)(2,1)S(1)}, u32[]{:S(2)}, u32[]{:S(2)}) collective-permute-start(bf16[8,16,16,128]{3,2,1,0:T(8,128)(2,1)S(1)} %merge_far_part.1), channel_id=1, source_target_pairs={{0,32},{1,97},{2,34},{3,99},{4,36},{5,101},{6,38},{7,103},{8,40},{... | collective-permute-start | bytes 1572872 | tf_op jit(solution)/shard_map/ppermute | solution.py:448
  20.6 38.0 %copy-start = (bf16[512,512]{1,0:T(8,128)(2,1)}, bf16[512,512]{1,0:T(8,128)(2,1)S(1)}, u32[]{:S(2)}) copy-start(bf16[512,512]{1,0:T(8,128)(2,1)S(1)} %get-tuple-element.65.refs_0_) | copy-start | bytes 1572868
  27.3 31.3 %all-to-all-start = ((bf16[256,16,128]{2,1,0:T(8,128)(2,1)}), bf16[256,16,128]{2,1,0:T(8,128)(2,1)S(1)}, u32[]{:S(2)}, u32[]{:S(2)}) async-start(bf16[256,16,128]{2,1,0:T(8,128)(2,1)} %sum_and_gather.1), calls=%async_computation | async-start | bytes 2097152 | tf_op jit(solution)/shard_map/all_to_all | solution.py:473
  40.0 20.4 %copy-start.1 = (bf16[512,512]{1,0:T(8,128)(2,1)}, bf16[512,512]{1,0:T(8,128)(2,1)S(1)}, u32[]{:S(2)}) copy-start(bf16[512,512]{1,0:T(8,128)(2,1)S(1)} %get-tuple-element.67.refs_2_) | copy-start | bytes 1572868
  40.0 20.4 %copy-start.2 = (bf16[512,512]{1,0:T(8,128)(2,1)}, bf16[512,512]{1,0:T(8,128)(2,1)S(1)}, u32[]{:S(2)}) copy-start(bf16[512,512]{1,0:T(8,128)(2,1)S(1)} %get-tuple-element.69.refs_4_) | copy-start | bytes 1572868
  40.1 20.4 %copy-start.3 = (bf16[512,512]{1,0:T(8,128)(2,1)}, bf16[512,512]{1,0:T(8,128)(2,1)S(1)}, u32[]{:S(2)}) copy-start(bf16[512,512]{1,0:T(8,128)(2,1)S(1)} %get-tuple-element.71.refs_6_) | copy-start | bytes 1572868
  60.5 29.3 %all-to-all-start.1 = ((bf16[256,16,128]{2,1,0:T(8,128)(2,1)}), bf16[256,16,128]{2,1,0:T(8,128)(2,1)S(1)}, u32[]{:S(2)}, u32[]{:S(2)}) async-start(bf16[256,16,128]{2,1,0:T(8,128)(2,1)} %bitcast.8), calls=%async_computation.1 | async-start | bytes 2097152 | tf_op jit(solution)/shard_map/all_to_all | solution.py:482

commit v9 on v7

--- a/solution.py
+++ b/solution.py
@@ -104,7 +104,9 @@
 
 
 def gather_kernel(table, *refs):
-    parts, (out, held) = refs[:6], refs[6:]
+    parts, (out, held, slots, sem) = refs[:6], refs[6:]
+    copy = pltpu.make_async_copy(table, slots, sem)
+    copy.start()
     half, rows, cols, width = parts[0].shape
     out[...] = jnp.zeros_like(out)
     for b in range(2 * half):
@@ -112,9 +114,11 @@
         total = own[b % half].astype(f32) + near[b % half].astype(f32)
         total = total + far[b % half].astype(f32)
         held[b] = total.reshape(rows * cols, width)
+    copy.wait()
+    for b in range(2 * half):
         for c in range(cols):
             piece = held[b, pl.ds(c, rows, stride=cols), :]
-            out[table[b * cols + c]] = piece.astype(out.dtype)
+            out[slots[b * cols + c]] = piece.astype(out.dtype)
 
 
 def gather_pieces(table, parts, slots):
@@ -122,12 +126,16 @@
     return pl.pallas_call(
         gather_kernel,
         out_shape=jax.ShapeDtypeStruct((slots, rows, width), bf16),
-        in_specs=[scalars] + [whole] * len(parts),
+        in_specs=[whole] + [whole] * len(parts),
         out_specs=whole,
-        scratch_shapes=[pltpu.VMEM((2 * half, rows * cols, width), f32)],
+        scratch_shapes=[
+            pltpu.VMEM((2 * half, rows * cols, width), f32),
+            pltpu.SMEM(table.shape, jnp.int32),
+            pltpu.SemaphoreType.DMA(()),
+        ],
         compiler_params=params(6),
         name="sum_and_gather",
-    )(table, *[vmem(x) for x in parts])
+    )(vmem(table), *[vmem(x) for x in parts])
 
 
 def place_kernel(per_step, rows, cols, table, arrived, out, held):

time: 89 us -> 88.9 us (level)
  no operation moved by 1% of the time
where the time goes in v9:
time: 88.9 us; the launch traced here: 88.3 us
  Pallas kernels  30.2 us (34%)
  waiting for transfers between devices  29.8 us (34%)
  starting transfers between devices  25.4 us (29%)
  local copies, waits for them, and re-layouts  1.11 us (1%)
  other arithmetic  0.94 us (1%)
    all_to_all x1, waiting for transfers between devices, body(): lax.all_to_all(outgoing, ('dp', 'shard'), split_axis=0, concat_axis=0, ti...  13.5 us
    pallas_call x2, Pallas kernels, early(): pl.pallas_call(functools.partial(early_kernel, [t for t, _, _ in items]),...  11.6 us
    all_to_all x1, waiting for transfers between devices, body(): lax.all_to_all(outbound.reshape(all_slots, rows, width), ('dp', 'shard'),...  10.8 us
    ppermute x6, starting transfers between devices, hop(): lax.ppermute(x, 'dp', [(i, (i + step) % replicas) for i in range(replicas)])  10.2 us
    all_to_all x1, starting transfers between devices, body(): lax.all_to_all(outgoing, ('dp', 'shard'), split_axis=0, concat_axis=0, ti...  8.93 us
    pallas_call x1, Pallas kernels, new_state(): pl.pallas_call(functools.partial(state_kernel, gain, slots), out_shape=(s...  8.53 us
    all_to_all x1, starting transfers between devices, body(): lax.all_to_all(outbound.reshape(all_slots, rows, width), ('dp', 'shard'),...  6.3 us
    ppermute x6, waiting for transfers between devices, hop(): lax.ppermute(x, 'dp', [(i, (i + step) % replicas) for i in range(replicas)])  5.5 us
  transfers between devices with their start and end apart: 8, of which 4 were waited for; matrix products, arithmetic and copies ran while one was open for 1% of the time, Pallas kernels for 25%

profile of v9, /device:TPU:1, one launch (start us, length us, event | category | flops | bytes accessed | tf_op | source)
XLA Modules:
  0.0 88.3 jit_solution(11461407028469573487)
XLA Ops:
  0.6 0.0 copy-start.5
  0.6 0.0 copy-start.6
  0.7 0.0 copy-start.4
  0.7 1.1 %dynamic-slice_bitcast_fusion = (bf16[4,16,16,128]{3,2,1,0:T(8,128)(2,1)S(1)}, bf16[4,16,16,128]{3,2,1,0:T(8,128)(2,1)S(1)}) fusion(bf16[1,8,16,16,512]{4,3,2,1,0:T(8,128)(2,1)} %param.8, s32[]{:T(128)S(6)} %add.22, s32[]{:T(128)S(6)} %select_n.18), kind=kLoop, calls=%fused_computation | loop fusion | bytes 1048584 | tf_op jit(solution)/shard_map/slice | solution.py:455
  1.8 4.7 %collective-permute-start.4 = (bf16[4,16,16,128]{3,2,1,0:T(8,128)(2,1)S(1)}, bf16[4,16,16,128]{3,2,1,0:T(8,128)(2,1)S(1)}, u32[]{:S(2)}, u32[]{:S(2)}) collective-permute-start(bf16[4,16,16,128]{3,2,1,0:T(8,128)(2,1)S(1)} %get-tuple-element.93), channel_id=1, source_target_pairs={{0,96},{32,0},{64,32},{96,64},{1,97},{33,1},{65,33},{97,65},{2,98}... | collective-permute-start | bytes 786440 | tf_op jit(solution)/shard_map/ppermute | solution.py:450
  6.4 0.0 collective-permute-start.1
  6.4 1.4 %windows.1 = (bf16[4,16,16,128]{3,2,1,0:T(8,128)(2,1)S(1)}, bf16[4,16,16,128]{3,2,1,0:T(8,128)(2,1)S(1)}, bf16[4,16,16,128]{3,2,1,0:T(8,128)(2,1)S(1)}, bf16[4,1...) custom-call(bf16[8,16,16,512]{3,2,1,0:T(8,128)(2,1)} %bitcast.11), custom_call_target="tpu_custom_call" | custom-call | tf_op jit(solution)/shard_map/windows/pallas_call | solution.py:79
  7.9 2.7 %collective-permute-start = (bf16[4,16,16,128]{3,2,1,0:T(8,128)(2,1)S(1)}, bf16[4,16,16,128]{3,2,1,0:T(8,128)(2,1)S(1)}, u32[]{:S(2)}, u32[]{:S(2)}) collective-permute-start(bf16[4,16,16,128]{3,2,1,0:T(8,128)(2,1)S(1)} %get-tuple-element.50), channel_id=1, source_target_pairs={{0,96},{32,0},{64,32},{96,64},{1,97},{33,1},{65,33},{97,65},{2,98}... | collective-permute-start | bytes 786440 | tf_op jit(solution)/shard_map/ppermute | solution.py:450
  10.6 0.0 collective-permute-start.3
  10.6 0.0 copy-done.5
  10.6 0.0 copy-done.6
  10.6 0.0 copy-done.4
  10.6 0.2 convert_reduce_fusion
  10.8 0.7 fusion.1
  11.5 3.0 %collective-permute-done.1.came = bf16[4,16,16,128]{3,2,1,0:T(8,128)(2,1)S(1)} collective-permute-done((bf16[4,16,16,128]{3,2,1,0:T(8,128)(2,1)S(1)}, bf16[4,16,16,128]{3,2,1,0:T(8,128)(2,1)S(1)}, u32[]{:S(2)}, u32[]{:S(2)}) %collective-permute-start.1) | collective-permute-done | bytes 262176 | tf_op jit(solution)/shard_map/ppermute | solution.py:450
  14.5 0.1 merge_far_part.2
  14.5 0.1 collective-permute-start.2
  14.6 0.0 collective-permute-done.4.came
  14.6 0.1 merge_far_part.3
  14.7 2.7 %collective-permute-start.5 = (bf16[4,16,16,128]{3,2,1,0:T(8,128)(2,1)S(1)}, bf16[4,16,16,128]{3,2,1,0:T(8,128)(2,1)S(1)}, u32[]{:S(2)}, u32[]{:S(2)}) collective-permute-start(bf16[4,16,16,128]{3,2,1,0:T(8,128)(2,1)S(1)} %merge_far_part.3), channel_id=1, source_target_pairs={{0,96},{32,0},{64,32},{96,64},{1,97},{33,1},{65,33},{97,65},{2,98}... | collective-permute-start | bytes 786440 | tf_op jit(solution)/shard_map/ppermute | solution.py:450
  17.4 0.1 select_reduce_fusion.table
  17.5 5.8 %early_products.2 = (bf16[512,512]{1,0:T(8,128)(2,1)S(1)}, bf16[512,512]{1,0:T(8,128)(2,1)}, bf16[512,512]{1,0:T(8,128)(2,1)}) custom-call(s32[1]{0:T(128)} %bitcast.count, f32[2,512,512]{2,1,0:T(8,128)} %xl.3, f32[2,512,512]{2,1,0:T(8,128)} %left.1), custom_call_target="tpu_custom_call" | custom-call | flops 2415919104 | bytes 3145728 | tf_op jit(solution)/shard_map/early_products/pallas_call | solution.py:215
  23.3 0.0 copy-start
  23.3 0.0 collective-permute-done.refs_1_
  23.3 0.0 collective-permute-done.3.refs_4_
  23.3 2.5 %collective-permute-done.2.refs_2_ = bf16[4,16,16,128]{3,2,1,0:T(8,128)(2,1)S(1)} collective-permute-done((bf16[4,16,16,128]{3,2,1,0:T(8,128)(2,1)S(1)}, bf16[4,16,16,128]{3,2,1,0:T(8,128)(2,1)S(1)}, u32[]{:S(2)}, u32[]{:S(2)}) %collective-permute-start.2) | collective-permute-done | bytes 262176 | tf_op jit(solution)/shard_map/ppermute | solution.py:450
  25.8 0.0 collective-permute-done.5.refs_5_
  25.8 1.8 %sum_and_gather.1 = bf16[256,16,128]{2,1,0:T(8,128)(2,1)} custom-call(s32[128]{0:T(128)S(1)} %select_reduce_fusion.table, bf16[4,16,16,128]{3,2,1,0:T(8,128)(2,1)S(1)} %get-tuple-element.58.refs_0_, bf16[4,16,16,128]{3,2,1,0:T(8,128)(2,1)S(1)} %collective-permute-done.refs_1_, bf16[4,16,16,128]{3,2,1,0:T(8,128)(2,1)S(1)} %collective-permute-done.2.refs_2_, ...), custom_call_target="tpu_custom_call" | custom-call | tf_op jit(solution)/shard_map/sum_and_gather/pallas_call | solution.py:126
  27.7 8.9 %all-to-all-start = ((bf16[256,16,128]{2,1,0:T(8,128)(2,1)}), bf16[256,16,128]{2,1,0:T(8,128)(2,1)S(1)}, u32[]{:S(2)}, u32[]{:S(2)}) async-start(bf16[256,16,128]{2,1,0:T(8,128)(2,1)} %sum_and_gather.1), calls=%async_computation | async-start | bytes 2097152 | tf_op jit(solution)/shard_map/all_to_all | solution.py:481
  36.6 5.8 %early_products.3 = (bf16[512,512]{1,0:T(8,128)(2,1)S(1)}, bf16[512,512]{1,0:T(8,128)(2,1)}, bf16[512,512]{1,0:T(8,128)(2,1)}, bf16[512,512]{1,0:T(8,128)(2,1)S(...) custom-call(s32[1]{0:T(128)} %bitcast.count, ...), custom_call_target="tpu_custom_call" | custom-call | flops 7247757312 | bytes 9437184 | tf_op jit(solution)/shard_map/early_products/pallas_call | solution.py:215
  42.4 0.0 copy-start.1
  42.5 0.0 copy-start.2
  42.5 0.0 copy-start.3
  42.5 13.5 %all-to-all-done = bf16[256,16,128]{2,1,0:T(8,128)(2,1)S(1)} async-done(((bf16[256,16,128]{2,1,0:T(8,128)(2,1)}), bf16[256,16,128]{2,1,0:T(8,128)(2,1)S(1)}, u32[]{:S(2)}, u32[]{:S(2)}) %all-to-all-start) | async-done | bytes 1048608 | tf_op jit(solution)/shard_map/all_to_all | solution.py:481
  56.0 0.0 copy-done
  56.0 5.0 %update_pieces.1 = bf16[4,32,2,16,128]{4,3,2,1,0:T(8,128)(2,1)} custom-call(s32[1]{0:T(128)} %bitcast.count, bf16[4,32,2,16,128]{4,3,2,1,0:T(8,128)(2,1)S(1)} %bitcast.8, f32[2,512,512]{2,1,0:T(8,128)} %xl.3, f32[2,512,512]{2,1,0:T(8,128)} %xr.3, bf16[512,512]{1,0:T(8,128)(2,1)S(1)} %get-tuple-element.77.refs_0_, ...), custom_call_target="tpu_custom_call" | custom-call | tf_op jit(solution)/shard_map/update_pieces/pallas_call | solution.py:339
  61.0 0.0 copy-done.1
  61.0 0.0 copy-done.2
  61.0 0.0 copy-done.3
  61.0 6.3 %all-to-all-start.1 = ((bf16[256,16,128]{2,1,0:T(8,128)(2,1)}), bf16[256,16,128]{2,1,0:T(8,128)(2,1)S(1)}, u32[]{:S(2)}, u32[]{:S(2)}) async-start(bf16[256,16,128]{2,1,0:T(8,128)(2,1)} %bitcast.10), calls=%async_computation.1 | async-start | bytes 2097152 | tf_op jit(solution)/shard_map/all_to_all | solution.py:490
  67.3 8.5 %new_state.1 = (f32[2,512,512]{2,1,0:T(8,128)}, f32[2,512,512]{2,1,0:T(8,128)}, f32[2,512,512]{2,1,0:T(8,128)}, f32[2,512,512]{2,1,0:T(8,128)}) custom-call(s32[1]{0:T(128)} %bitcast.count, bf16[4,32,2,16,128]{4,3,2,1,0:T(8,128)(2,1)S(1)} %bitcast.9, f32[2,512,512]{2,1,0:T(8,128)} %left.1, f32[2,512,512]{2,1,0:T(8,128)} %right.1, f32[2,512,512]{2,1,0:T(8,128)} %xl.3, ...), custom_call_target="tpu_custom_call" | custom-call | flops 4294967296 | bytes 18874368 | tf_op jit(solution)/shard_map/new_state/pallas_call | solution.py:416
  75.8 10.8 %all-to-all-done.1.arrived = bf16[256,16,128]{2,1,0:T(8,128)(2,1)S(1)} async-done(((bf16[256,16,128]{2,1,0:T(8,128)(2,1)}), bf16[256,16,128]{2,1,0:T(8,128)(2,1)S(1)}, u32[]{:S(2)}, u32[]{:S(2)}) %all-to-all-start.1) | async-done | bytes 1048608 | tf_op jit(solution)/shard_map/all_to_all | solution.py:490
  86.6 1.7 %place_pieces.1 = bf16[8,16,16,128]{3,2,1,0:T(8,128)(2,1)} custom-call(s32[128]{0:T(128)S(1)} %select_reduce_fusion.table, bf16[256,16,128]{2,1,0:T(8,128)(2,1)S(1)} %all-to-all-done.1.arrived), custom_call_target="tpu_custom_call" | custom-call | tf_op jit(solution)/shard_map/place_pieces/pallas_call | solution.py:153
  (1 shorter events, 0.0 us)
Async XLA Ops:
  0.6 10.0 %copy-start.5 = (s32[128]{0:T(128)S(1)}, s32[128]{0:T(128)}, u32[]{:S(2)}) copy-start(s32[128]{0:T(128)} %param.11) | copy-start | bytes 1540
  0.6 10.0 %copy-start.6 = (s32[128]{0:T(128)S(1)}, s32[128]{0:T(128)}, u32[]{:S(2)}) copy-start(s32[128]{0:T(128)} %param.10) | copy-start | bytes 1540
  0.7 10.0 %copy-start.4 = (s32[128]{0:T(128)S(1)}, s32[128]{0:T(128)}, u32[]{:S(2)}) copy-start(s32[128]{0:T(128)} %param.9) | copy-start | bytes 1540
  1.8 12.9 %collective-permute-start.4 = (bf16[4,16,16,128]{3,2,1,0:T(8,128)(2,1)S(1)}, bf16[4,16,16,128]{3,2,1,0:T(8,128)(2,1)S(1)}, u32[]{:S(2)}, u32[]{:S(2)}) collective-permute-start(bf16[4,16,16,128]{3,2,1,0:T(8,128)(2,1)S(1)} %get-tuple-element.93), channel_id=1, source_target_pairs={{0,96},{32,0},{64,32},{96,64},{1,97},{33,1},{65,33},{97,65},{2,98}... | collective-permute-start | bytes 786440 | tf_op jit(solution)/shard_map/ppermute | solution.py:450
  6.4 8.1 %collective-permute-start.1 = (bf16[4,16,16,128]{3,2,1,0:T(8,128)(2,1)S(1)}, bf16[4,16,16,128]{3,2,1,0:T(8,128)(2,1)S(1)}, u32[]{:S(2)}, u32[]{:S(2)}) collective-permute-start(bf16[4,16,16,128]{3,2,1,0:T(8,128)(2,1)S(1)} %get-tuple-element.94), channel_id=1, source_target_pairs={{0,32},{32,64},{64,96},{96,0},{1,33},{33,65},{65,97},{97,1},{2,34}... | collective-permute-start | bytes 786440 | tf_op jit(solution)/shard_map/ppermute | solution.py:450
  7.9 15.4 %collective-permute-start = (bf16[4,16,16,128]{3,2,1,0:T(8,128)(2,1)S(1)}, bf16[4,16,16,128]{3,2,1,0:T(8,128)(2,1)S(1)}, u32[]{:S(2)}, u32[]{:S(2)}) collective-permute-start(bf16[4,16,16,128]{3,2,1,0:T(8,128)(2,1)S(1)} %get-tuple-element.50), channel_id=1, source_target_pairs={{0,96},{32,0},{64,32},{96,64},{1,97},{33,1},{65,33},{97,65},{2,98}... | collective-permute-start | bytes 786440 | tf_op jit(solution)/shard_map/ppermute | solution.py:450
  10.6 12.7 %collective-permute-start.3 = (bf16[4,16,16,128]{3,2,1,0:T(8,128)(2,1)S(1)}, bf16[4,16,16,128]{3,2,1,0:T(8,128)(2,1)S(1)}, u32[]{:S(2)}, u32[]{:S(2)}) collective-permute-start(bf16[4,16,16,128]{3,2,1,0:T(8,128)(2,1)S(1)} %get-tuple-element.53), channel_id=1, source_target_pairs={{0,32},{32,64},{64,96},{96,0},{1,33},{33,65},{65,97},{97,1},{2,34}... | collective-permute-start | bytes 786440 | tf_op jit(solution)/shard_map/ppermute | solution.py:450
  14.5 11.3 %collective-permute-start.2 = (bf16[4,16,16,128]{3,2,1,0:T(8,128)(2,1)S(1)}, bf16[4,16,16,128]{3,2,1,0:T(8,128)(2,1)S(1)}, u32[]{:S(2)}, u32[]{:S(2)}) collective-permute-start(bf16[4,16,16,128]{3,2,1,0:T(8,128)(2,1)S(1)} %merge_far_part.2), channel_id=1, source_target_pairs={{0,32},{32,64},{64,96},{96,0},{1,33},{33,65},{65,97},{97,1},{2,34}... | collective-permute-start | bytes 786440 | tf_op jit(solution)/shard_map/ppermute | solution.py:450
  14.7 11.1 %collective-permute-start.5 = (bf16[4,16,16,128]{3,2,1,0:T(8,128)(2,1)S(1)}, bf16[4,16,16,128]{3,2,1,0:T(8,128)(2,1)S(1)}, u32[]{:S(2)}, u32[]{:S(2)}) collective-permute-start(bf16[4,16,16,128]{3,2,1,0:T(8,128)(2,1)S(1)} %merge_far_part.3), channel_id=1, source_target_pairs={{0,96},{32,0},{64,32},{96,64},{1,97},{33,1},{65,33},{97,65},{2,98}... | collective-permute-start | bytes 786440 | tf_op jit(solution)/shard_map/ppermute | solution.py:450
  23.3 32.7 %copy-start = (bf16[512,512]{1,0:T(8,128)(2,1)}, bf16[512,512]{1,0:T(8,128)(2,1)S(1)}, u32[]{:S(2)}) copy-start(bf16[512,512]{1,0:T(8,128)(2,1)S(1)} %get-tuple-element.77.refs_0_) | copy-start | bytes 1572868
  27.7 28.3 %all-to-all-start = ((bf16[256,16,128]{2,1,0:T(8,128)(2,1)}), bf16[256,16,128]{2,1,0:T(8,128)(2,1)S(1)}, u32[]{:S(2)}, u32[]{:S(2)}) async-start(bf16[256,16,128]{2,1,0:T(8,128)(2,1)} %sum_and_gather.1), calls=%async_computation | async-start | bytes 2097152 | tf_op jit(solution)/shard_map/all_to_all | solution.py:481
  42.4 18.5 %copy-start.1 = (bf16[512,512]{1,0:T(8,128)(2,1)}, bf16[512,512]{1,0:T(8,128)(2,1)S(1)}, u32[]{:S(2)}) copy-start(bf16[512,512]{1,0:T(8,128)(2,1)S(1)} %get-tuple-element.79.refs_2_) | copy-start | bytes 1572868
  42.5 18.5 %copy-start.2 = (bf16[512,512]{1,0:T(8,128)(2,1)}, bf16[512,512]{1,0:T(8,128)(2,1)S(1)}, u32[]{:S(2)}) copy-start(bf16[512,512]{1,0:T(8,128)(2,1)S(1)} %get-tuple-element.81.refs_4_) | copy-start | bytes 1572868
  42.5 18.5 %copy-start.3 = (bf16[512,512]{1,0:T(8,128)(2,1)}, bf16[512,512]{1,0:T(8,128)(2,1)S(1)}, u32[]{:S(2)}) copy-start(bf16[512,512]{1,0:T(8,128)(2,1)S(1)} %get-tuple-element.83.refs_6_) | copy-start | bytes 1572868
  61.0 25.7 %all-to-all-start.1 = ((bf16[256,16,128]{2,1,0:T(8,128)(2,1)}), bf16[256,16,128]{2,1,0:T(8,128)(2,1)S(1)}, u32[]{:S(2)}, u32[]{:S(2)}) async-start(bf16[256,16,128]{2,1,0:T(8,128)(2,1)} %bitcast.10), calls=%async_computation.1 | async-start | bytes 2097152 | tf_op jit(solution)/shard_map/all_to_all | solution.py:490
